TPU v7x, 128 devices: a whole 4x4x4 slice. The times are simulated.
128 devices in a mesh: tm: 8 (over x, y_hi), space: 16 (over z, y_lo, core).
Axes of the slice: x: 4, y: 4 (y_hi: 2, y_lo: 2; y = y_hi * 2 + y_lo), z: 4, core: 2. Of those that a mesh axis runs over, the one named last changes fastest.
Arguments:
- potential: float32 [64, 64, 128, 128], P('tm', 'space'), may hold values from -6 to 6
- multiplier: float32 [4, 64, 64, 128, 128], P(None, 'tm', 'space'), may hold values from -12 to 12
- start_density: float32 [64, 128, 128], P('space'), may hold values from 0.1 to 1
- final_density: float32 [64, 128, 128], P('space'), may hold values from 0.1 to 1
Outputs:
- next_potential: float32 [64, 64, 128, 128], P('tm', 'space')
- next_multiplier: float32 [4, 64, 64, 128, 128], P(None, 'tm', 'space')
All inputs are finite; a program needn't handle non-finite values.
Results may differ from a plain program's by a relative error of at most 0.0003.
Values sent between devices are 32-bit elements; how exact they have to be, the bound alone decides.
A program may use at most 128 MiB of HBM per device.

v0:
```python
import functools

import jax
import jax.numpy as jnp
from jax import lax
from jax.sharding import PartitionSpec as P
from jax.experimental import pallas as pl
from jax.experimental.pallas import tpu as pltpu

NEWTON = 10


RATE = 4.0
PROX = 0.01


def from_behind(block, axis, distance):
    devices = range(lax.axis_size(axis))
    route = [(i - distance, i) for i in devices if i - distance in devices]
    return lax.ppermute(block, axis, route)


def cosine_table(length):
    freq = jnp.arange(length, dtype=jnp.float32)[:, None]
    place = jnp.arange(length, dtype=jnp.float32)[None, :]
    weight = jnp.where(freq == 0.0, jnp.sqrt(jnp.float32(0.5)), jnp.float32(1.0))
    return (
        jnp.sqrt(jnp.float32(2.0) / length)
        * weight
        * jnp.cos(jnp.pi * freq * (place + 0.5) / length)
    )


def eigen_at(length, freq):
    return 4.0 * jnp.square(jnp.sin(jnp.pi * freq / (2.0 * length)))


def adjoint(face, axis):
    size = face.shape[axis]
    inner = lax.slice_in_dim(face, 0, size - 1, axis=axis)
    edge = jnp.zeros_like(lax.slice_in_dim(face, 0, 1, axis=axis))
    return jnp.concatenate([edge, inner], axis=axis) - jnp.concatenate([inner, edge], axis=axis)


def local_diff(field, axis):
    size = field.shape[axis]
    upper = lax.slice_in_dim(field, 1, size, axis=axis)
    lower = lax.slice_in_dim(field, 0, size - 1, axis=axis)
    edge = jnp.zeros_like(lax.slice_in_dim(field, 0, 1, axis=axis))
    return jnp.concatenate([upper - lower, edge], axis=axis)


def project(target):
    lead = target[0]
    side = target[1:]
    wsq = jnp.sum(side * side, axis=0)
    excess = lead + 0.5 * wsq
    stretch = jnp.maximum(1.0, lead + 1.0)
    shifted = lead + 1.0
    half_again = 1.5 * wsq
    for step in range(NEWTON):
        square = stretch * stretch
        cube = square * stretch
        stretch = jnp.maximum(1.0, stretch * (shifted * square + half_again) / (cube + wsq))
    inside = excess <= 0.0
    new_lead = jnp.where(inside, lead, lead - (stretch - 1.0))
    shrink = 1.0 / stretch
    new_side = jnp.where(inside[None], side, side * shrink[None])
    return jnp.concatenate([new_lead[None], new_side], axis=0)


def cell_kernel(n_tm, n_sp, idx_ref, pc, pn, at, ax, m, sd, fd, nm_out, pay_out, ft_out, fx_out, ft_carry):
    t = pl.program_id(0)
    steps_t = pl.num_programs(0)
    rows_x, width_y, width_z = pc.shape[1], pc.shape[2], pc.shape[3]
    t_glob = idx_ref[0] * steps_t + t
    last_t = t_glob == n_tm * steps_t - 1
    last_x_dev = idx_ref[1] == n_sp - 1
    row = lax.broadcasted_iota(jnp.int32, (width_y, width_z), 0)
    col = lax.broadcasted_iota(jnp.int32, (width_y, width_z), 1)
    first_row = row == 0
    last_row = row == width_y - 1
    last_col = col == width_z - 1
    first_col = col == 0
    fx_prev = None
    for x in range(rows_x):
        p = pc[0, x]
        nxt = jnp.where(t == steps_t - 1, at[0, x], pn[0, x])
        grad_t = jnp.where(last_t, 0.0, nxt - p)
        if x < rows_x - 1:
            grad_x = pc[0, x + 1] - p
        else:
            grad_x = jnp.where(last_x_dev, 0.0, ax[0, 0] - p)
        grad_y = jnp.where(last_row, 0.0, pltpu.roll(p, width_y - 1, 0) - p)
        grad_z = jnp.where(last_col, 0.0, pltpu.roll(p, width_z - 1, 1) - p)
        grads = (grad_t, grad_x, grad_y, grad_z)
        mults = tuple(m[c, 0, x] for c in range(4))
        target = tuple(g + mu * (1.0 / RATE) for g, mu in zip(grads, mults))
        lead = target[0]
        wsq = target[1] * target[1] + target[2] * target[2] + target[3] * target[3]
        excess = lead + 0.5 * wsq
        shifted = lead + 1.0
        half_again = 1.5 * wsq
        stretch = jnp.maximum(1.0, shifted)
        for step in range(NEWTON):
            square = stretch * stretch
            cube = square * stretch
            stretch = jnp.maximum(1.0, stretch * (shifted * square + half_again) / (cube + wsq))
        inside = excess <= 0.0
        shrink = 1.0 / stretch
        proj = (jnp.where(inside, lead, lead - (stretch - 1.0)),) + tuple(
            jnp.where(inside, target[c], target[c] * shrink) for c in (1, 2, 3)
        )
        flux = []
        for c in range(4):
            nm = mults[c] + RATE * (grads[c] - proj[c])
            nm_out[c, 0, x] = nm
            flux.append(nm - RATE * proj[c])
        flow_y = jnp.where(first_row, 0.0, pltpu.roll(flux[2], 1, 0)) - jnp.where(last_row, 0.0, flux[2])
        flow_z = jnp.where(first_col, 0.0, pltpu.roll(flux[3], 1, 1)) - jnp.where(last_col, 0.0, flux[3])
        rest = PROX * p - (flow_y + flow_z)
        rest = rest + jnp.where(t_glob == 0, sd[x], 0.0) - jnp.where(last_t, fd[x], 0.0)
        ft_prev = jnp.where(t == 0, 0.0, ft_carry[x])
        div_t = ft_prev - jnp.where(last_t, 0.0, flux[0])
        ft_carry[x] = flux[0]
        ft_out[0, x] = flux[0]
        if x < rows_x - 1:
            fx_cur = flux[1]
        else:
            fx_cur = jnp.where(last_x_dev, 0.0, flux[1])
            fx_out[0, 0] = flux[1]
        div_x = -fx_cur if fx_prev is None else fx_prev - fx_cur
        fx_prev = flux[1]
        pay_out[0, x] = rest - div_t - div_x


def cells(potential, ahead_t, ahead_x, multiplier, start_density, final_density, n_tm, n_sp):
    steps_t, rows_x, width_y, width_z = potential.shape
    idx = jnp.stack([lax.axis_index("tm"), lax.axis_index("space")]).astype(jnp.int32)
    slab = (1, rows_x, width_y, width_z)
    f32 = jnp.float32
    grid_spec = pltpu.PrefetchScalarGridSpec(
        num_scalar_prefetch=1,
        grid=(steps_t,),
        in_specs=[
            pl.BlockSpec(slab, lambda t, s: (t, 0, 0, 0)),
            pl.BlockSpec(slab, lambda t, s: (jnp.minimum(t + 1, steps_t - 1), 0, 0, 0)),
            pl.BlockSpec(slab, lambda t, s: (0, 0, 0, 0)),
            pl.BlockSpec((1, 1, width_y, width_z), lambda t, s: (t, 0, 0, 0)),
            pl.BlockSpec((4, 1, rows_x, width_y, width_z), lambda t, s: (0, t, 0, 0, 0)),
            pl.BlockSpec((rows_x, width_y, width_z), lambda t, s: (0, 0, 0)),
            pl.BlockSpec((rows_x, width_y, width_z), lambda t, s: (0, 0, 0)),
        ],
        out_specs=[
            pl.BlockSpec((4, 1, rows_x, width_y, width_z), lambda t, s: (0, t, 0, 0, 0)),
            pl.BlockSpec(slab, lambda t, s: (t, 0, 0, 0)),
            pl.BlockSpec(slab, lambda t, s: (0, 0, 0, 0)),
            pl.BlockSpec((1, 1, width_y, width_z), lambda t, s: (t, 0, 0, 0)),
        ],
        scratch_shapes=[pltpu.VMEM((rows_x, width_y, width_z), f32)],
    )
    cells_n = potential.size
    return pl.pallas_call(
        functools.partial(cell_kernel, n_tm, n_sp),
        grid_spec=grid_spec,
        out_shape=[
            jax.ShapeDtypeStruct(multiplier.shape, f32),
            jax.ShapeDtypeStruct(potential.shape, f32),
            jax.ShapeDtypeStruct(slab, f32),
            jax.ShapeDtypeStruct((steps_t, 1, width_y, width_z), f32),
        ],
        compiler_params=pltpu.CompilerParams(dimension_semantics=("arbitrary",)),
        cost_estimate=pl.CostEstimate(
            flops=cells_n * 200, transcendentals=cells_n * 11, bytes_accessed=cells_n * 4 * 12
        ),
    )(idx, potential, potential, ahead_t, ahead_x, multiplier, start_density, final_density)


def body(potential, multiplier, start_density, final_density):
    high = lax.Precision.HIGHEST
    steps_t, rows_x, width_y, width_z = potential.shape
    n_tm = lax.axis_size("tm")
    n_sp = lax.axis_size("space")
    total_t = steps_t * n_tm
    total_x = rows_x * n_sp
    block_y = width_y // (n_tm * n_sp)
    time_at = lax.axis_index("tm") * steps_t + jnp.arange(steps_t)
    row_at = lax.axis_index("space") * rows_x + jnp.arange(rows_x)
    ahead_t = from_behind(potential[:1], "tm", -1)
    ahead_x = from_behind(potential[:, :1], "space", -1)
    next_multiplier, partial, flux_t_last, flux_x_last = cells(
        potential, ahead_t, ahead_x, multiplier, start_density, final_density, n_tm, n_sp
    )
    behind_t = from_behind(flux_t_last, "tm", 1)
    behind_x = from_behind(flux_x_last, "space", 1)
    cos_y = cosine_table(width_y)
    cos_z = cosine_table(width_z)
    payload = jnp.einsum("txyi,ki->txyk", partial, cos_z, precision=high)
    payload = jnp.einsum("txiz,ki->txkz", payload, cos_y, precision=high)
    edge_t = jnp.einsum("txyi,ki->txyk", behind_t, cos_z, precision=high)
    edge_t = jnp.einsum("txiz,ki->txkz", edge_t, cos_y, precision=high)
    edge_x = jnp.einsum("txyi,ki->txyk", behind_x, cos_z, precision=high)
    edge_x = jnp.einsum("txiz,ki->txkz", edge_x, cos_y, precision=high)
    payload = payload.at[:, :1].add(-edge_x)
    payload = payload.at[:1].add(-edge_t)
    both = ("tm", "space")
    middle = lax.all_to_all(payload, both, split_axis=2, concat_axis=0, tiled=True)
    middle = middle.reshape(n_tm, n_sp, steps_t, rows_x, block_y, width_z)
    cos_t = cosine_table(total_t).reshape(total_t, n_tm, steps_t)
    cos_x = cosine_table(total_x).reshape(total_x, n_sp, rows_x)
    hat = jnp.einsum("kat,abtxyz->kbxyz", cos_t, middle, precision=high)
    hat = jnp.einsum("jbx,kbxyz->kjyz", cos_x, hat, precision=high)
    freq_y = (
        (lax.axis_index("tm") * n_sp + lax.axis_index("space")) * block_y + jnp.arange(block_y)
    ).astype(jnp.float32)
    eig_t = eigen_at(total_t, jnp.arange(total_t, dtype=jnp.float32))
    eig_x = eigen_at(total_x, jnp.arange(total_x, dtype=jnp.float32))
    eig_y = eigen_at(width_y, freq_y)
    eig_z = eigen_at(width_z, jnp.arange(width_z, dtype=jnp.float32))
    denom = eig_t[:, None, None, None] + eig_x[None, :, None, None]
    denom = denom + eig_y[None, None, :, None] + eig_z[None, None, None, :]
    hat = hat / (RATE * denom + PROX)
    hat = jnp.einsum("atk,kjyz->atjyz", cos_t.reshape(n_tm, steps_t, total_t), hat, precision=high)
    solved = jnp.einsum("bxj,atjyz->abtxyz", cos_x.reshape(n_sp, rows_x, total_x), hat, precision=high)
    solved = solved.reshape(n_tm * n_sp * steps_t, rows_x, block_y, width_z)
    local = lax.all_to_all(solved, both, split_axis=0, concat_axis=2, tiled=True)
    local = jnp.einsum("ik,txkz->txiz", cos_y, local, precision=high)
    next_potential = jnp.einsum("ik,txyk->txyi", cos_z, local, precision=high)
    return (next_potential, next_multiplier)


def solution(mesh):
    in_specs = (
        P("tm", "space", None, None),
        P(None, "tm", "space", None, None),
        P("space", None, None),
        P("space", None, None),
    )
    out_specs = (P("tm", "space", None, None), P(None, "tm", "space", None, None))
    return jax.shard_map(body, mesh=mesh, in_specs=in_specs, out_specs=out_specs, check_vma=False)
```

profile of v0, /device:TPU:1, one launch (start us, length us, event | category | flops | bytes accessed | tf_op | source)
XLA Modules:
  0.0 160.8 jit_solution(17252735364477245399)
XLA Ops:
  0.6 1.1 slice.65
  1.7 3.3 %collective-permute-start.1 = (f32[8,1,128,128]{3,2,1,0:T(8,128)S(1)}, f32[8,1,128,128]{3,2,1,0:T(8,128)S(1)}, u32[]{:S(2)}, u32[]{:S(2)}) collective-permute-start(f32[8,1,128,128]{3,2,1,0:T(8,128)S(1)} %slice.65), channel_id=1, source_target_pairs={{1,0},{2,1},{3,2},{4,3},{5,4},{6,5},{7,6},{8,7},{9,8},{10,9},{11,1... | collective-permute-start | bytes 1572872 | tf_op jit(solution)/shard_map/ppermute | solution.py:20
  5.1 1.0 slice.64
  6.0 1.3 collective-permute-start
  7.3 0.6 pad_add_fusion.idx_ref
  7.9 9.5 %collective-permute-done.at = f32[1,4,128,128]{3,2,1,0:T(8,128)S(1)} collective-permute-done((f32[1,4,128,128]{3,2,1,0:T(8,128)S(1)}, f32[1,4,128,128]{3,2,1,0:T(8,128)S(1)}, u32[]{:S(2)}, u32[]{:S(2)}) %collective-permute-start) | collective-permute-done | bytes 262176 | tf_op jit(solution)/shard_map/ppermute | solution.py:20
  17.4 0.0 copy-start.1
  17.4 0.0 collective-permute-done.1.ax
  17.4 0.7 copy-done.1
  18.1 0.0 copy-start
  18.1 0.8 copy-done
  18.9 17.3 %shard_map.59 = (f32[4,8,4,128,128]{4,3,2,1,0:T(8,128)}, f32[8,4,128,128]{3,2,1,0:T(8,128)}, f32[1,4,128,128]{3,2,1,0:T(8,128)}, f32[8,1,128,128]{3,2,1,0:T(8,128)}) custom-call(s32[2]{0:T(128)} %pad_add_fusion.idx_ref, f32[8,4,128,128]{3,2,1,0:T(8,128)} %pn.1, f32[8,4,128,128]{3,2,1,0:T(8,128)} %pn.1, f32[1,4,128,128]{3,2,1,0:T(8,128)} %copy-done.1, ...), custom_call_target="tpu_custom_call" | custom-call | flops 104857600 | bytes 25165824 | tf_op jit(solution)/shard_map/pallas_call | solution.py:163
  36.2 6.1 %collective-permute-start.2 = (f32[8,1,128,128]{3,2,1,0:T(8,128)}, f32[8,1,128,128]{3,2,1,0:T(8,128)S(1)}, u32[]{:S(2)}, u32[]{:S(2)}) collective-permute-start(f32[8,1,128,128]{3,2,1,0:T(8,128)} %get-tuple-element.31), channel_id=1, source_target_pairs={{0,1},{1,2},{2,3},{3,4},{4,5},{5,6},{6,7},{7,8},{8,9},{9,10},{10,1... | collective-permute-start | bytes 1572872 | tf_op jit(solution)/shard_map/ppermute | solution.py:20
  42.3 3.3 %collective-permute-start.3 = (f32[1,4,128,128]{3,2,1,0:T(8,128)}, f32[1,4,128,128]{3,2,1,0:T(8,128)S(1)}, u32[]{:S(2)}, u32[]{:S(2)}) collective-permute-start(f32[1,4,128,128]{3,2,1,0:T(8,128)} %get-tuple-element.32), channel_id=1, source_target_pairs={{0,16},{16,32},{32,48},{48,64},{64,80},{80,96},{96,112},{1,17},{17... | collective-permute-start | bytes 786440 | tf_op jit(solution)/shard_map/ppermute | solution.py:20
  45.6 3.7 %fusion.39 = f32[8,4,128,128]{3,2,1,0:T(8,128)S(1)} fusion(f32[8,4,128,128]{3,2,1,0:T(8,128)} %get-tuple-element.30, f32[128]{0:T(128)S(1)} %get-tuple-element.35, f32[128]{0:T(128)S(1)} %iota_multiply_fusion, f32[128]{0:T(128)S(1)} %get-tuple-element.34), kind=kOutput, calls=%fused_computation.37 | convolution fusion | flops 805355520 | bytes 4195840 | tf_op jit(solution)/shard_map/txyi,ki->txyk/dot_general | solution.py:198
  49.3 2.2 %fusion.37 = f32[128,8,4,128]{3,0,2,1:T(8,128)S(1)} fusion(f32[8,4,128,128]{3,2,1,0:T(8,128)S(1)} %fusion.39, f32[128]{0:T(128)S(1)} %get-tuple-element.35, f32[128]{0:T(128)S(1)} %iota_multiply_fusion, f32[128]{0:T(128)S(1)} %get-tuple-element.34), kind=kOutput, calls=%fused_computation.35 | convolution fusion | flops 805355520 | bytes 4195840 | tf_op jit(solution)/shard_map/txiz,ki->txkz/dot_general | solution.py:199
  51.5 0.2 copy.51
  51.7 2.6 %collective-permute-done.3 = f32[1,4,128,128]{3,2,1,0:T(8,128)S(1)} collective-permute-done((f32[1,4,128,128]{3,2,1,0:T(8,128)}, f32[1,4,128,128]{3,2,1,0:T(8,128)S(1)}, u32[]{:S(2)}, u32[]{:S(2)}) %collective-permute-start.3) | collective-permute-done | bytes 262176 | tf_op jit(solution)/shard_map/ppermute | solution.py:20
  54.3 0.7 fusion.29
  55.0 0.0 collective-permute-done.2
  55.0 0.9 fusion.27
  55.9 0.9 fusion.23
  56.7 0.7 fusion.26
  57.4 2.7 %copy.14 = f32[8,4,128,128]{3,1,0,2:T(4,128)} copy(f32[8,4,128,128]{3,2,1,0:T(8,128)S(1)} %fusion.26) | data formatting | bytes 4194304 | tf_op jit(solution)/shard_map/scatter-add | solution.py:205
  60.1 12.4 %all-to-all-start = ((f32[8,4,128,128]{3,1,0,2:T(4,128)}), f32[8,4,128,128]{3,1,0,2:T(4,128)S(1)}, u32[]{:S(2)}, u32[]{:S(2)}) async-start(f32[8,4,128,128]{3,1,0,2:T(4,128)} %copy.14), calls=%async_computation | async-start | bytes 4194304 | tf_op jit(solution)/shard_map/all_to_all | solution.py:207
  72.8 0.1 add_add_fusion
  72.9 29.5 %all-to-all-done = f32[8,4,128,128]{3,1,0,2:T(4,128)S(1)} async-done(((f32[8,4,128,128]{3,1,0,2:T(4,128)}), f32[8,4,128,128]{3,1,0,2:T(4,128)S(1)}, u32[]{:S(2)}, u32[]{:S(2)}) %all-to-all-start) | async-done | bytes 2097184 | tf_op jit(solution)/shard_map/all_to_all | solution.py:207
  102.4 0.2 copy.15
  102.6 2.1 %convolution_bitcast_fusion = f32[64,16,4,128]{3,0,2,1:T(8,128)S(1)} fusion(f32[8,16,8,4,128]{4,2,3,1,0:T(8,128)S(1)} %bitcast.116, f32[8,8]{1,0:T(8,128)S(1)} %fusion.109, f32[64]{0:T(128)S(1)} %get-tuple-element.37, f32[64]{0:T(128)S(1)} %get-tuple-element.36), kind=kOutput, calls=%fused_computation.15 | convolution fusion | flops 402665472 | bytes 4195072 | tf_op jit(solution)/shard_map/kat,abtxyz->kbxyz/dot_general | solution.py:211
  104.7 3.6 %fusion.2 = f32[64,64,128]{2,1,0:T(8,128)S(1)} fusion(f32[64,16,4,128]{3,0,2,1:T(8,128)S(1)} %convolution_bitcast_fusion, f32[128]{0:T(128)S(1)} %multiply_multiply_fusion, f32[64,64]{1,0:T(8,128)S(1)} %add_add_fusion, f32[16,4]{0,1:T(4,128)S(1)} %fusion.114, f32[64]{0:T(128)S(1)} %get-tuple-element.37, f32[64]{0:T(128)S(1)} %get-tuple-element.36), kind=kOutput, calls=%fused_computation.3 | convolution fusion | flops 404762624 | bytes 4211968 | tf_op jit(solution)/shard_map/jbx,kbxyz->kjyz/dot_general | solution.py:212
  108.3 3.2 %fusion.12 = f32[8,8,64,128,1]{3,1,2,0,4:T(8,128)S(1)} fusion(f32[64,64,128]{2,1,0:T(8,128)S(1)} %fusion.2, f32[64]{0:T(128)S(1)} %iota_add_fusion.1, f32[8,8]{1,0:T(8,128)S(1)} %get-tuple-element.39, f32[8,8]{1,0:T(8,128)S(1)} %get-tuple-element.38), kind=kOutput, calls=%fused_computation.13 | convolution fusion | flops 402665472 | bytes 4195072 | tf_op jit(solution)/shard_map/atk,kjyz->atjyz/dot_general | solution.py:223
  111.5 2.3 %fusion.15 = f32[8,16,8,4,1,128]{5,1,3,2,0,4:T(8,128)S(1)} fusion(f32[8,8,64,128,1]{3,1,2,0,4:T(8,128)S(1)} %fusion.12, f32[64]{0:T(128)S(1)} %iota_add_fusion.1, f32[16,4]{0,1:T(4,128)S(1)} %get-tuple-element.41, f32[16,4]{0,1:T(4,128)S(1)} %get-tuple-element.40), kind=kOutput, calls=%fused_computation.14 | convolution fusion | flops 402665472 | bytes 4195072 | tf_op jit(solution)/shard_map/bxj,atjyz->abtxyz/dot_general | solution.py:224
  113.8 1.4 copy.20
  115.3 1.4 copy.21
  116.6 34.9 %all_to_all.33 = f32[1024,4,1,128]{3,1,2,0:T(4,128)} all-to-all(f32[1024,4,1,128]{3,1,2,0:T(4,128)S(1)} %copy.21), channel_id=1, replica_groups=mesh['tm'=8,'space'=16] {'tm','space'}, dimensions={0} | all-to-all | bytes 4194304 | tf_op jit(solution)/shard_map/all_to_all | solution.py:226
  151.6 2.0 %copy.23 = f32[128,8,4,1,128]{0,4,2,1,3:T(8,128)S(1)} copy(f32[128,8,4,1,128]{4,2,1,0,3:T(4,128)} %bitcast.118) | data formatting | bytes 4194304 | tf_op jit(solution)/shard_map/all_to_all | solution.py:226
  153.6 2.1 %fusion = f32[8,4,128,128]{3,2,1,0:T(8,128)S(1)} fusion(f32[128,8,4,1,128]{0,4,2,1,3:T(8,128)S(1)} %copy.23, f32[128]{0:T(128)S(1)} %get-tuple-element.35, f32[128]{0:T(128)S(1)} %iota_multiply_fusion, f32[128]{0:T(128)S(1)} %get-tuple-element.34), kind=kOutput, calls=%fused_computation | convolution fusion | flops 805355520 | bytes 4195840 | tf_op jit(solution)/shard_map/ik,txkz->txiz/dot_general | solution.py:227
  155.7 5.0 %fusion.3 = f32[8,4,128,128]{3,2,1,0:T(8,128)} fusion(f32[8,4,128,128]{3,2,1,0:T(8,128)S(1)} %fusion, f32[128]{0:T(128)S(1)} %get-tuple-element.35, f32[128]{0:T(128)S(1)} %iota_multiply_fusion, f32[128]{0:T(128)S(1)} %get-tuple-element.34), kind=kOutput, calls=%fused_computation.4 | convolution fusion | flops 805355520 | bytes 4195840 | tf_op jit(solution)/shard_map/ik,txyk->txyi/dot_general | solution.py:228
  (10 shorter events, 0.2 us)
Async XLA Ops:
  1.7 15.7 %collective-permute-start.1 = (f32[8,1,128,128]{3,2,1,0:T(8,128)S(1)}, f32[8,1,128,128]{3,2,1,0:T(8,128)S(1)}, u32[]{:S(2)}, u32[]{:S(2)}) collective-permute-start(f32[8,1,128,128]{3,2,1,0:T(8,128)S(1)} %slice.65), channel_id=1, source_target_pairs={{1,0},{2,1},{3,2},{4,3},{5,4},{6,5},{7,6},{8,7},{9,8},{10,9},{11,1... | collective-permute-start | bytes 1572872 | tf_op jit(solution)/shard_map/ppermute | solution.py:20
  6.0 11.4 %collective-permute-start = (f32[1,4,128,128]{3,2,1,0:T(8,128)S(1)}, f32[1,4,128,128]{3,2,1,0:T(8,128)S(1)}, u32[]{:S(2)}, u32[]{:S(2)}) collective-permute-start(f32[1,4,128,128]{3,2,1,0:T(8,128)S(1)} %slice.64), channel_id=1, source_target_pairs={{16,0},{32,16},{48,32},{64,48},{80,64},{96,80},{112,96},{17,1},{33... | collective-permute-start | bytes 786440 | tf_op jit(solution)/shard_map/ppermute | solution.py:20
  17.4 0.7 copy-start.1
  18.1 0.8 copy-start
  36.2 18.8 %collective-permute-start.2 = (f32[8,1,128,128]{3,2,1,0:T(8,128)}, f32[8,1,128,128]{3,2,1,0:T(8,128)S(1)}, u32[]{:S(2)}, u32[]{:S(2)}) collective-permute-start(f32[8,1,128,128]{3,2,1,0:T(8,128)} %get-tuple-element.31), channel_id=1, source_target_pairs={{0,1},{1,2},{2,3},{3,4},{4,5},{5,6},{6,7},{7,8},{8,9},{9,10},{10,1... | collective-permute-start | bytes 1572872 | tf_op jit(solution)/shard_map/ppermute | solution.py:20
  42.3 12.0 %collective-permute-start.3 = (f32[1,4,128,128]{3,2,1,0:T(8,128)}, f32[1,4,128,128]{3,2,1,0:T(8,128)S(1)}, u32[]{:S(2)}, u32[]{:S(2)}) collective-permute-start(f32[1,4,128,128]{3,2,1,0:T(8,128)} %get-tuple-element.32), channel_id=1, source_target_pairs={{0,16},{16,32},{32,48},{48,64},{64,80},{80,96},{96,112},{1,17},{17... | collective-permute-start | bytes 786440 | tf_op jit(solution)/shard_map/ppermute | solution.py:20
  60.1 42.3 %all-to-all-start = ((f32[8,4,128,128]{3,1,0,2:T(4,128)}), f32[8,4,128,128]{3,1,0,2:T(4,128)S(1)}, u32[]{:S(2)}, u32[]{:S(2)}) async-start(f32[8,4,128,128]{3,1,0,2:T(4,128)} %copy.14), calls=%async_computation | async-start | bytes 4194304 | tf_op jit(solution)/shard_map/all_to_all | solution.py:207
where the time goes:
time: 161 us
  waiting for transfers between devices  41.5 us (26%)
  blocking collectives  34.9 us (22%)
  matrix products  27.4 us (17%)
  starting transfers between devices  26.4 us (16%)
  Pallas kernels  17.3 us (11%)
  local copies, waits for them, and re-layouts  11.4 us (7%)
    all_to_all x1, blocking collectives, body(): lax.all_to_all(solved, both, split_axis=0, concat_axis=2, tiled=True)  34.9 us
    all_to_all x1, waiting for transfers between devices, body(): lax.all_to_all(payload, both, split_axis=2, concat_axis=0, tiled=True)  29.5 us
    pallas_call x1, Pallas kernels, cells(): pl.pallas_call(functools.partial(cell_kernel, n_tm, n_sp), grid_spec=grid...  17.3 us
    ppermute x4, starting transfers between devices, from_behind(): return lax.ppermute(block, axis, route)  14 us
    all_to_all x1, starting transfers between devices, body(): lax.all_to_all(payload, both, split_axis=2, concat_axis=0, tiled=True)  12.4 us
    ppermute x4, waiting for transfers between devices, from_behind(): return lax.ppermute(block, axis, route)  12 us
    dot_general x1, matrix products, body(): next_potential = jnp.einsum('ik,txyk->txyi', cos_z, local, precision=high)  5.03 us
    dot_general x1, matrix products, body(): payload = jnp.einsum('txyi,ki->txyk', partial, cos_z, precision=high)  3.73 us
  transfers between devices with their start and end apart: 5, of which 3 were waited for; matrix products, arithmetic and copies ran while one was open for 5% of the time, Pallas kernels for 0%

commit v1 on v0

--- a/solution.py
+++ b/solution.py
@@ -176,6 +176,58 @@
     )(idx, potential, potential, ahead_t, ahead_x, multiplier, start_density, final_density)
 
 
+def exchange_kernel(n_sp, src_ref, out_ref, send_sem, recv_sem, own_sem):
+    n_dev = src_ref.shape[0]
+    me = lax.axis_index("tm") * n_sp + lax.axis_index("space")
+
+    def peer_copy(peer, source):
+        return pltpu.make_async_remote_copy(
+            src_ref.at[peer],
+            out_ref.at[source],
+            send_sem.at[peer],
+            recv_sem.at[source],
+            device_id=(peer // n_sp, peer % n_sp),
+            device_id_type=pl.DeviceIdType.MESH,
+        )
+
+    def start(k, carry):
+        peer = lax.rem(me + k, n_dev)
+        peer_copy(peer, me).start()
+        return carry
+
+    lax.fori_loop(1, n_dev, start, 0)
+    own = pltpu.make_async_copy(src_ref.at[me], out_ref.at[me], own_sem)
+    own.start()
+
+    def finish(k, carry):
+        peer = lax.rem(me + k, n_dev)
+        peer_copy(peer, me).wait_send()
+        source = lax.rem(me + n_dev - k, n_dev)
+        peer_copy(me, source).wait_recv()
+        return carry
+
+    lax.fori_loop(1, n_dev, finish, 0)
+    own.wait()
+
+
+def exchange(blocks, n_sp):
+    n_dev = blocks.shape[0]
+    any_space = pl.BlockSpec(memory_space=pl.ANY)
+    return pl.pallas_call(
+        functools.partial(exchange_kernel, n_sp),
+        out_shape=jax.ShapeDtypeStruct(blocks.shape, blocks.dtype),
+        in_specs=[any_space],
+        out_specs=any_space,
+        scratch_shapes=[
+            pltpu.SemaphoreType.DMA((n_dev,)),
+            pltpu.SemaphoreType.DMA((n_dev,)),
+            pltpu.SemaphoreType.DMA(()),
+        ],
+        compiler_params=pltpu.CompilerParams(has_side_effects=True),
+        cost_estimate=pl.CostEstimate(flops=0, transcendentals=0, bytes_accessed=2 * blocks.size * 4),
+    )(blocks)
+
+
 def body(potential, multiplier, start_density, final_density):
     high = lax.Precision.HIGHEST
     steps_t, rows_x, width_y, width_z = potential.shape
@@ -203,9 +255,11 @@
     edge_x = jnp.einsum("txiz,ki->txkz", edge_x, cos_y, precision=high)
     payload = payload.at[:, :1].add(-edge_x)
     payload = payload.at[:1].add(-edge_t)
-    both = ("tm", "space")
-    middle = lax.all_to_all(payload, both, split_axis=2, concat_axis=0, tiled=True)
-    middle = middle.reshape(n_tm, n_sp, steps_t, rows_x, block_y, width_z)
+    n_dev = n_tm * n_sp
+    blocks = payload.reshape(steps_t, rows_x, n_dev, block_y, width_z).transpose(2, 3, 0, 1, 4)
+    blocks = blocks.reshape(n_dev, block_y * steps_t * rows_x, width_z)
+    middle = exchange(blocks, n_sp)
+    middle = middle.reshape(n_tm, n_sp, block_y, steps_t, rows_x, width_z).transpose(0, 1, 3, 4, 2, 5)
     cos_t = cosine_table(total_t).reshape(total_t, n_tm, steps_t)
     cos_x = cosine_table(total_x).reshape(total_x, n_sp, rows_x)
     hat = jnp.einsum("kat,abtxyz->kbxyz", cos_t, middle, precision=high)
@@ -222,9 +276,10 @@
     hat = hat / (RATE * denom + PROX)
     hat = jnp.einsum("atk,kjyz->atjyz", cos_t.reshape(n_tm, steps_t, total_t), hat, precision=high)
     solved = jnp.einsum("bxj,atjyz->abtxyz", cos_x.reshape(n_sp, rows_x, total_x), hat, precision=high)
-    solved = solved.reshape(n_tm * n_sp * steps_t, rows_x, block_y, width_z)
-    local = lax.all_to_all(solved, both, split_axis=0, concat_axis=2, tiled=True)
-    local = jnp.einsum("ik,txkz->txiz", cos_y, local, precision=high)
+    solved = solved.transpose(0, 1, 4, 2, 3, 5).reshape(n_dev, block_y * steps_t * rows_x, width_z)
+    local = exchange(solved, n_sp)
+    local = local.reshape(n_dev * block_y, steps_t, rows_x, width_z)
+    local = jnp.einsum("ik,ktxz->txiz", cos_y, local, precision=high)
     next_potential = jnp.einsum("ik,txyk->txyi", cos_z, local, precision=high)
     return (next_potential, next_multiplier)
 

time: 161 us -> 187 us (1.16); the launches traced: 161 us -> 183 us
  Pallas kernels: 17.3 us -> 117 us
  blocking collectives: 34.9 us -> 0 us
  waiting for transfers between devices: 41.5 us -> 11.7 us
  starting transfers between devices: 26.4 us -> 14 us
  matrix products: 27.4 us -> 30 us
  local copies, waits for them, and re-layouts: 11.4 us -> 9 us
    pallas_call x0 -> x2, Pallas kernels: none -> 99.6 us  [exchange(): pl.pallas_call(functools.partial(exchange_kernel, n_sp), out_shape=jax.Sh...]
    all_to_all x1 -> x0, blocking collectives: 34.9 us -> none  [body(): lax.all_to_all(solved, both, split_axis=0, concat_axis=2, tiled=True)]
    all_to_all x1 -> x0, waiting for transfers between devices: 29.5 us -> none  [body(): lax.all_to_all(payload, both, split_axis=2, concat_axis=0, tiled=True)]
    all_to_all x1 -> x0, starting transfers between devices: 12.4 us -> none  [body(): lax.all_to_all(payload, both, split_axis=2, concat_axis=0, tiled=True)]
    transpose x1 -> x2, local copies, waits for them, and re-layouts: 1.44 us -> 5.02 us  [the longest x1 2.67 us: body(): payload.reshape(steps_t, rows_x, n_dev, block_y, width_z)]
    dot_general x1, matrix products: 2.14 us -> 4.88 us  [body(): local = jnp.einsum('ik,ktxz->txiz', cos_y, local, precision=high)]
    scatter-add x1 -> x0, local copies, waits for them, and re-layouts: 2.67 us -> none  [body(): payload = payload.at[:1].add(-edge_t)]
    all_to_all x2 -> x0, local copies, waits for them, and re-layouts: 2.18 us -> none  [the longest x1 2.01 us: body(): lax.all_to_all(solved, both, split_axis=0, concat_axis=2, tiled=True)]
  transfers between devices with their start and end apart: 5 -> 4, of which waited for: 3 -> 2; matrix products, arithmetic and copies ran while one was open for 5% -> 5% of each run, Pallas kernels for 0% -> 0%
where the time goes in v1:
time: 187 us; the launch traced here: 183 us
  Pallas kernels  117 us (63%)
  matrix products  30 us (16%)
  starting transfers between devices  14 us (7%)
  waiting for transfers between devices  11.7 us (6%)
  local copies, waits for them, and re-layouts  9 us (5%)
    pallas_call x2, Pallas kernels, exchange(): pl.pallas_call(functools.partial(exchange_kernel, n_sp), out_shape=jax.Sh...  99.6 us
    pallas_call x1, Pallas kernels, cells(): pl.pallas_call(functools.partial(cell_kernel, n_tm, n_sp), grid_spec=grid...  17.3 us
    ppermute x4, starting transfers between devices, from_behind(): return lax.ppermute(block, axis, route)  14 us
    ppermute x4, waiting for transfers between devices, from_behind(): return lax.ppermute(block, axis, route)  11.7 us
    dot_general x1, matrix products, body(): local = jnp.einsum('ik,ktxz->txiz', cos_y, local, precision=high)  4.88 us
  transfers between devices with their start and end apart: 4, of which 2 were waited for; matrix products, arithmetic and copies ran while one was open for 5% of the time, Pallas kernels for 0%

profile of v1, /device:TPU:1, one launch (start us, length us, event | category | flops | bytes accessed | tf_op | source)
XLA Modules:
  0.0 183.4 jit_solution(413345872223608497)
XLA Ops:
  0.6 1.1 slice.65
  1.7 3.3 %collective-permute-start.1 = (f32[8,1,128,128]{3,2,1,0:T(8,128)S(1)}, f32[8,1,128,128]{3,2,1,0:T(8,128)S(1)}, u32[]{:S(2)}, u32[]{:S(2)}) collective-permute-start(f32[8,1,128,128]{3,2,1,0:T(8,128)S(1)} %slice.65), channel_id=1, source_target_pairs={{1,0},{2,1},{3,2},{4,3},{5,4},{6,5},{7,6},{8,7},{9,8},{10,9},{11,1... | collective-permute-start | bytes 1572872 | tf_op jit(solution)/shard_map/ppermute | solution.py:20
  5.1 1.0 slice.64
  6.0 1.3 collective-permute-start
  7.5 0.6 pad_add_fusion.idx_ref
  8.2 0.1 add_add_fusion
  8.3 9.1 %collective-permute-done.at = f32[1,4,128,128]{3,2,1,0:T(8,128)S(1)} collective-permute-done((f32[1,4,128,128]{3,2,1,0:T(8,128)S(1)}, f32[1,4,128,128]{3,2,1,0:T(8,128)S(1)}, u32[]{:S(2)}, u32[]{:S(2)}) %collective-permute-start) | collective-permute-done | bytes 262176 | tf_op jit(solution)/shard_map/ppermute | solution.py:20
  17.4 0.0 copy-start.1
  17.4 0.0 collective-permute-done.1.ax
  17.4 0.7 copy-done.1
  18.1 0.0 copy-start
  18.1 0.8 copy-done
  18.9 17.3 %shard_map.59 = (f32[4,8,4,128,128]{4,3,2,1,0:T(8,128)}, f32[8,4,128,128]{3,2,1,0:T(8,128)}, f32[1,4,128,128]{3,2,1,0:T(8,128)}, f32[8,1,128,128]{3,2,1,0:T(8,128)}) custom-call(s32[2]{0:T(128)} %pad_add_fusion.idx_ref, f32[8,4,128,128]{3,2,1,0:T(8,128)} %pn.1, f32[8,4,128,128]{3,2,1,0:T(8,128)} %pn.1, f32[1,4,128,128]{3,2,1,0:T(8,128)} %copy-done.1, ...), custom_call_target="tpu_custom_call" | custom-call | flops 104857600 | bytes 25165824 | tf_op jit(solution)/shard_map/pallas_call | solution.py:163
  36.2 6.1 %collective-permute-start.2 = (f32[8,1,128,128]{3,2,1,0:T(8,128)}, f32[8,1,128,128]{3,2,1,0:T(8,128)S(1)}, u32[]{:S(2)}, u32[]{:S(2)}) collective-permute-start(f32[8,1,128,128]{3,2,1,0:T(8,128)} %get-tuple-element.31), channel_id=1, source_target_pairs={{0,1},{1,2},{2,3},{3,4},{4,5},{5,6},{6,7},{7,8},{8,9},{9,10},{10,1... | collective-permute-start | bytes 1572872 | tf_op jit(solution)/shard_map/ppermute | solution.py:20
  42.3 3.3 %collective-permute-start.3 = (f32[1,4,128,128]{3,2,1,0:T(8,128)}, f32[1,4,128,128]{3,2,1,0:T(8,128)S(1)}, u32[]{:S(2)}, u32[]{:S(2)}) collective-permute-start(f32[1,4,128,128]{3,2,1,0:T(8,128)} %get-tuple-element.32), channel_id=1, source_target_pairs={{0,16},{16,32},{32,48},{48,64},{64,80},{80,96},{96,112},{1,17},{17... | collective-permute-start | bytes 786440 | tf_op jit(solution)/shard_map/ppermute | solution.py:20
  45.6 3.7 %fusion.42 = f32[8,4,128,128]{3,2,1,0:T(8,128)S(1)} fusion(f32[8,4,128,128]{3,2,1,0:T(8,128)} %get-tuple-element.30, f32[128]{0:T(128)S(1)} %get-tuple-element.35, f32[128]{0:T(128)S(1)} %iota_multiply_fusion, f32[128]{0:T(128)S(1)} %get-tuple-element.34), kind=kOutput, calls=%fused_computation.39 | convolution fusion | flops 805355520 | bytes 4195840 | tf_op jit(solution)/shard_map/txyi,ki->txyk/dot_general | solution.py:250
  49.3 2.2 %fusion.40 = f32[128,8,4,128]{3,0,2,1:T(8,128)S(1)} fusion(f32[8,4,128,128]{3,2,1,0:T(8,128)S(1)} %fusion.42, f32[128]{0:T(128)S(1)} %get-tuple-element.35, f32[128]{0:T(128)S(1)} %iota_multiply_fusion, f32[128]{0:T(128)S(1)} %get-tuple-element.34), kind=kOutput, calls=%fused_computation.37 | convolution fusion | flops 805355520 | bytes 4195840 | tf_op jit(solution)/shard_map/txiz,ki->txkz/dot_general | solution.py:251
  51.5 0.2 copy.43
  51.7 2.6 %collective-permute-done.3 = f32[1,4,128,128]{3,2,1,0:T(8,128)S(1)} collective-permute-done((f32[1,4,128,128]{3,2,1,0:T(8,128)}, f32[1,4,128,128]{3,2,1,0:T(8,128)S(1)}, u32[]{:S(2)}, u32[]{:S(2)}) %collective-permute-start.3) | collective-permute-done | bytes 262176 | tf_op jit(solution)/shard_map/ppermute | solution.py:20
  54.3 0.7 fusion.32
  55.0 0.0 collective-permute-done.2
  55.0 0.9 fusion.30
  55.8 0.9 fusion.25
  56.7 0.2 copy.44
  56.9 0.6 fusion.29
  57.6 2.7 %copy.10 = f32[128,1,8,4,128]{4,3,2,0,1:T(4,128)} copy(f32[128,1,8,4,128]{4,0,3,2,1:T(8,128)S(1)} %bitcast.114) | data formatting | bytes 4194304 | tf_op jit(solution)/shard_map/transpose | solution.py:259
  60.3 49.8 %shard_map.60 = f32[128,32,128]{2,1,0:T(8,128)} custom-call(f32[128,32,128]{2,1,0:T(8,128)} %bitcast.115), custom_call_target="tpu_custom_call" | custom-call | bytes 4194304 | tf_op jit(solution)/shard_map/pallas_call | solution.py:216
  110.1 3.7 %fusion.12 = f32[64,16,4,128,1]{3,0,4,2,1:T(8,128)S(1)} fusion(f32[8,16,8,4,128]{4,3,2,1,0:T(4,128)} %bitcast.113, f32[8,8]{1,0:T(8,128)S(1)} %fusion.112, f32[64]{0:T(128)S(1)} %get-tuple-element.37, f32[64]{0:T(128)S(1)} %get-tuple-element.36), kind=kOutput, calls=%fused_computation.13 | convolution fusion | flops 402665472 | bytes 4195072 | tf_op jit(solution)/shard_map/kat,abtxyz->kbxyz/dot_general | solution.py:265
  113.8 3.6 %fusion = f32[64,64,128,1]{2,1,0,3:T(8,128)S(1)} fusion(f32[64,16,4,128,1]{3,0,4,2,1:T(8,128)S(1)} %fusion.12, f32[128]{0:T(128)S(1)} %multiply_multiply_fusion, f32[64,64]{1,0:T(8,128)S(1)} %add_add_fusion, f32[16,4]{0,1:T(4,128)S(1)} %fusion.117, f32[64]{0:T(128)S(1)} %get-tuple-element.37, f32[64]{0:T(128)S(1)} %get-tuple-element.36), kind=kOutput, calls=%fused_computation.1 | convolution fusion | flops 404762624 | bytes 4211968 | tf_op jit(solution)/shard_map/jbx,kbxyz->kjyz/dot_general | solution.py:266
  117.4 3.2 %fusion.14 = f32[8,8,64,128,1]{3,1,2,0,4:T(8,128)S(1)} fusion(f32[64,64,128,1]{2,1,0,3:T(8,128)S(1)} %fusion, f32[64]{0:T(128)S(1)} %iota_add_fusion.1, f32[8,8]{1,0:T(8,128)S(1)} %get-tuple-element.39, f32[8,8]{1,0:T(8,128)S(1)} %get-tuple-element.38), kind=kOutput, calls=%fused_computation.15 | convolution fusion | flops 402665472 | bytes 4195072 | tf_op jit(solution)/shard_map/atk,kjyz->atjyz/dot_general | solution.py:277
  120.6 2.3 %fusion.17 = f32[8,16,1,8,4,128]{5,1,4,3,0,2:T(8,128)S(1)} fusion(f32[8,8,64,128,1]{3,1,2,0,4:T(8,128)S(1)} %fusion.14, f32[64]{0:T(128)S(1)} %iota_add_fusion.1, f32[16,4]{0,1:T(4,128)S(1)} %get-tuple-element.41, f32[16,4]{0,1:T(4,128)S(1)} %get-tuple-element.40), kind=kOutput, calls=%fused_computation.16 | convolution fusion | flops 402665472 | bytes 4195072 | tf_op jit(solution)/shard_map/bxj,atjyz->abtxyz/dot_general | solution.py:278
  122.9 2.4 %copy.11 = f32[8,16,1,8,4,128]{5,4,3,1,0,2:T(4,128)} copy(f32[8,16,1,8,4,128]{5,1,4,3,0,2:T(8,128)S(1)} %fusion.17) | data formatting | bytes 4194304 | tf_op jit(solution)/shard_map/transpose;bxj,atjyz->abtxyz/transpose | solution.py:279
  125.3 49.8 %shard_map.61 = f32[128,32,128]{2,1,0:T(8,128)} custom-call(f32[128,32,128]{2,1,0:T(8,128)} %bitcast.116), custom_call_target="tpu_custom_call" | custom-call | bytes 4194304 | tf_op jit(solution)/shard_map/pallas_call | solution.py:216
  175.1 4.9 %fusion.7 = f32[8,4,128,128]{2,3,1,0:T(8,128)S(1)} fusion(f32[128,8,4,128]{3,2,1,0:T(4,128)} %bitcast.112, f32[128]{0:T(128)S(1)} %get-tuple-element.35, f32[128]{0:T(128)S(1)} %iota_multiply_fusion, f32[128]{0:T(128)S(1)} %get-tuple-element.34), kind=kOutput, calls=%fused_computation.8 | convolution fusion | flops 805355520 | bytes 4195840 | tf_op jit(solution)/shard_map/ik,ktxz->txiz/dot_general | solution.py:282
  180.0 3.4 %fusion.1 = f32[8,4,128,128]{3,2,1,0:T(8,128)} fusion(f32[8,4,128,128]{2,3,1,0:T(8,128)S(1)} %fusion.7, f32[128]{0:T(128)S(1)} %get-tuple-element.35, f32[128]{0:T(128)S(1)} %iota_multiply_fusion, f32[128]{0:T(128)S(1)} %get-tuple-element.34), kind=kOutput, calls=%fused_computation.2 | convolution fusion | flops 805355520 | bytes 4195840 | tf_op jit(solution)/shard_map/ik,txyk->txyi/dot_general | solution.py:283
  (10 shorter events, 0.2 us)
Async XLA Ops:
  1.7 15.7 %collective-permute-start.1 = (f32[8,1,128,128]{3,2,1,0:T(8,128)S(1)}, f32[8,1,128,128]{3,2,1,0:T(8,128)S(1)}, u32[]{:S(2)}, u32[]{:S(2)}) collective-permute-start(f32[8,1,128,128]{3,2,1,0:T(8,128)S(1)} %slice.65), channel_id=1, source_target_pairs={{1,0},{2,1},{3,2},{4,3},{5,4},{6,5},{7,6},{8,7},{9,8},{10,9},{11,1... | collective-permute-start | bytes 1572872 | tf_op jit(solution)/shard_map/ppermute | solution.py:20
  6.0 11.4 %collective-permute-start = (f32[1,4,128,128]{3,2,1,0:T(8,128)S(1)}, f32[1,4,128,128]{3,2,1,0:T(8,128)S(1)}, u32[]{:S(2)}, u32[]{:S(2)}) collective-permute-start(f32[1,4,128,128]{3,2,1,0:T(8,128)S(1)} %slice.64), channel_id=1, source_target_pairs={{16,0},{32,16},{48,32},{64,48},{80,64},{96,80},{112,96},{17,1},{33... | collective-permute-start | bytes 786440 | tf_op jit(solution)/shard_map/ppermute | solution.py:20
  17.4 0.7 copy-start.1
  18.1 0.8 copy-start
  36.2 18.8 %collective-permute-start.2 = (f32[8,1,128,128]{3,2,1,0:T(8,128)}, f32[8,1,128,128]{3,2,1,0:T(8,128)S(1)}, u32[]{:S(2)}, u32[]{:S(2)}) collective-permute-start(f32[8,1,128,128]{3,2,1,0:T(8,128)} %get-tuple-element.31), channel_id=1, source_target_pairs={{0,1},{1,2},{2,3},{3,4},{4,5},{5,6},{6,7},{7,8},{8,9},{9,10},{10,1... | collective-permute-start | bytes 1572872 | tf_op jit(solution)/shard_map/ppermute | solution.py:20
  42.3 12.0 %collective-permute-start.3 = (f32[1,4,128,128]{3,2,1,0:T(8,128)}, f32[1,4,128,128]{3,2,1,0:T(8,128)S(1)}, u32[]{:S(2)}, u32[]{:S(2)}) collective-permute-start(f32[1,4,128,128]{3,2,1,0:T(8,128)} %get-tuple-element.32), channel_id=1, source_target_pairs={{0,16},{16,32},{32,48},{48,64},{64,80},{80,96},{96,112},{1,17},{17... | collective-permute-start | bytes 786440 | tf_op jit(solution)/shard_map/ppermute | solution.py:20

commit v2 on v0

--- a/solution.py
+++ b/solution.py
@@ -69,13 +69,63 @@
     return jnp.concatenate([new_lead[None], new_side], axis=0)
 
 
-def cell_kernel(n_tm, n_sp, idx_ref, pc, pn, at, ax, m, sd, fd, nm_out, pay_out, ft_out, fx_out, ft_carry):
+def cell_kernel(n_tm, n_sp, idx_ref, pc, pn, p_any, m, sd, fd, nm_out, pay_out,
+                ft_carry, ahead_t, ahead_x, send_x, send_t, behind_t, behind_x,
+                at_sems, ax_sems, bt_sems, bx_sems):
     t = pl.program_id(0)
     steps_t = pl.num_programs(0)
     rows_x, width_y, width_z = pc.shape[1], pc.shape[2], pc.shape[3]
-    t_glob = idx_ref[0] * steps_t + t
+    tm = lax.axis_index("tm")
+    sp = lax.axis_index("space")
+    t_glob = tm * steps_t + t
     last_t = t_glob == n_tm * steps_t - 1
-    last_x_dev = idx_ref[1] == n_sp - 1
+    has_later_t = tm < n_tm - 1
+    has_earlier_t = tm > 0
+    has_later_x = sp < n_sp - 1
+    has_earlier_x = sp > 0
+    mesh_id = pl.DeviceIdType.MESH
+
+    def ahead_t_copy():
+        return pltpu.make_async_remote_copy(
+            p_any.at[0], ahead_t, at_sems.at[0], at_sems.at[1],
+            device_id=(tm - 1, sp), device_id_type=mesh_id)
+
+    def ahead_x_copy(row):
+        return pltpu.make_async_remote_copy(
+            p_any.at[row, 0], ahead_x.at[row], ax_sems.at[0, row], ax_sems.at[1, row],
+            device_id=(tm, sp - 1), device_id_type=mesh_id)
+
+    def behind_t_copy():
+        return pltpu.make_async_remote_copy(
+            send_t, behind_t, bt_sems.at[0], bt_sems.at[1],
+            device_id=(tm + 1, sp), device_id_type=mesh_id)
+
+    def behind_x_copy(row):
+        return pltpu.make_async_remote_copy(
+            send_x.at[row], behind_x.at[row], bx_sems.at[0, row], bx_sems.at[1, row],
+            device_id=(tm, sp + 1), device_id_type=mesh_id)
+
+    @pl.when(t == 0)
+    def _():
+        barrier = pltpu.get_barrier_semaphore()
+        for cond, dev in ((has_earlier_t, (tm - 1, sp)), (has_later_t, (tm + 1, sp)),
+                          (has_earlier_x, (tm, sp - 1)), (has_later_x, (tm, sp + 1))):
+            @pl.when(cond)
+            def _():
+                pl.semaphore_signal(barrier, 1, device_id=dev, device_id_type=mesh_id)
+        peers = (has_earlier_t.astype(jnp.int32) + has_later_t.astype(jnp.int32)
+                 + has_earlier_x.astype(jnp.int32) + has_later_x.astype(jnp.int32))
+        pl.semaphore_wait(barrier, peers)
+
+        @pl.when(has_earlier_t)
+        def _():
+            ahead_t_copy().start()
+
+        @pl.when(has_earlier_x)
+        def _():
+            for row in range(steps_t):
+                ahead_x_copy(row).start()
+
     row = lax.broadcasted_iota(jnp.int32, (width_y, width_z), 0)
     col = lax.broadcasted_iota(jnp.int32, (width_y, width_z), 1)
     first_row = row == 0
@@ -85,12 +135,19 @@
     fx_prev = None
     for x in range(rows_x):
         p = pc[0, x]
-        nxt = jnp.where(t == steps_t - 1, at[0, x], pn[0, x])
+        if x == 0:
+            @pl.when(jnp.logical_and(t == steps_t - 1, has_later_t))
+            def _():
+                ahead_t_copy().wait_recv()
+        nxt = lax.cond(t == steps_t - 1, lambda: ahead_t[x], lambda: pn[0, x])
         grad_t = jnp.where(last_t, 0.0, nxt - p)
         if x < rows_x - 1:
             grad_x = pc[0, x + 1] - p
         else:
-            grad_x = jnp.where(last_x_dev, 0.0, ax[0, 0] - p)
+            @pl.when(has_later_x)
+            def _():
+                ahead_x_copy(t).wait_recv()
+            grad_x = lax.cond(has_later_x, lambda: ahead_x[t] - p, lambda: jnp.zeros_like(p))
         grad_y = jnp.where(last_row, 0.0, pltpu.roll(p, width_y - 1, 0) - p)
         grad_z = jnp.where(last_col, 0.0, pltpu.roll(p, width_z - 1, 1) - p)
         grads = (grad_t, grad_x, grad_y, grad_z)
@@ -123,21 +180,55 @@
         ft_prev = jnp.where(t == 0, 0.0, ft_carry[x])
         div_t = ft_prev - jnp.where(last_t, 0.0, flux[0])
         ft_carry[x] = flux[0]
-        ft_out[0, x] = flux[0]
+        send_t[x] = flux[0]
         if x < rows_x - 1:
             fx_cur = flux[1]
         else:
-            fx_cur = jnp.where(last_x_dev, 0.0, flux[1])
-            fx_out[0, 0] = flux[1]
+            fx_cur = jnp.where(has_later_x, flux[1], 0.0)
+            send_x[t] = flux[1]
+
+            @pl.when(has_later_x)
+            def _():
+                behind_x_copy(t).start()
         div_x = -fx_cur if fx_prev is None else fx_prev - fx_cur
         fx_prev = flux[1]
-        pay_out[0, x] = rest - div_t - div_x
-
-
-def cells(potential, ahead_t, ahead_x, multiplier, start_density, final_density, n_tm, n_sp):
+        pay_out[t, x] = rest - div_t - div_x
+
+    @pl.when(t == steps_t - 1)
+    def _():
+        @pl.when(has_later_t)
+        def _():
+            behind_t_copy().start()
+
+        @pl.when(has_earlier_t)
+        def _():
+            ahead_t_copy().wait_send()
+            behind_t_copy().wait_recv()
+            for x in range(rows_x):
+                pay_out[0, x] = pay_out[0, x] - behind_t[x]
+
+        @pl.when(has_earlier_x)
+        def _():
+            for r in range(steps_t):
+                ahead_x_copy(r).wait_send()
+                behind_x_copy(r).wait_recv()
+                pay_out[r, 0] = pay_out[r, 0] - behind_x[r]
+
+        @pl.when(has_later_x)
+        def _():
+            for r in range(steps_t):
+                behind_x_copy(r).wait_send()
+
+        @pl.when(has_later_t)
+        def _():
+            behind_t_copy().wait_send()
+
+
+def cells(potential, multiplier, start_density, final_density, n_tm, n_sp):
     steps_t, rows_x, width_y, width_z = potential.shape
     idx = jnp.stack([lax.axis_index("tm"), lax.axis_index("space")]).astype(jnp.int32)
     slab = (1, rows_x, width_y, width_z)
+    plane = (rows_x, width_y, width_z)
     f32 = jnp.float32
     grid_spec = pltpu.PrefetchScalarGridSpec(
         num_scalar_prefetch=1,
@@ -145,19 +236,28 @@
         in_specs=[
             pl.BlockSpec(slab, lambda t, s: (t, 0, 0, 0)),
             pl.BlockSpec(slab, lambda t, s: (jnp.minimum(t + 1, steps_t - 1), 0, 0, 0)),
-            pl.BlockSpec(slab, lambda t, s: (0, 0, 0, 0)),
-            pl.BlockSpec((1, 1, width_y, width_z), lambda t, s: (t, 0, 0, 0)),
+            pl.BlockSpec(memory_space=pl.ANY),
             pl.BlockSpec((4, 1, rows_x, width_y, width_z), lambda t, s: (0, t, 0, 0, 0)),
-            pl.BlockSpec((rows_x, width_y, width_z), lambda t, s: (0, 0, 0)),
-            pl.BlockSpec((rows_x, width_y, width_z), lambda t, s: (0, 0, 0)),
+            pl.BlockSpec(plane, lambda t, s: (0, 0, 0)),
+            pl.BlockSpec(plane, lambda t, s: (0, 0, 0)),
         ],
         out_specs=[
             pl.BlockSpec((4, 1, rows_x, width_y, width_z), lambda t, s: (0, t, 0, 0, 0)),
-            pl.BlockSpec(slab, lambda t, s: (t, 0, 0, 0)),
-            pl.BlockSpec(slab, lambda t, s: (0, 0, 0, 0)),
-            pl.BlockSpec((1, 1, width_y, width_z), lambda t, s: (t, 0, 0, 0)),
+            pl.BlockSpec(potential.shape, lambda t, s: (0, 0, 0, 0)),
         ],
-        scratch_shapes=[pltpu.VMEM((rows_x, width_y, width_z), f32)],
+        scratch_shapes=[
+            pltpu.VMEM(plane, f32),
+            pltpu.VMEM(plane, f32),
+            pltpu.VMEM((steps_t, width_y, width_z), f32),
+            pltpu.VMEM((steps_t, width_y, width_z), f32),
+            pltpu.VMEM(plane, f32),
+            pltpu.VMEM(plane, f32),
+            pltpu.VMEM((steps_t, width_y, width_z), f32),
+            pltpu.SemaphoreType.DMA((2,)),
+            pltpu.SemaphoreType.DMA((2, steps_t)),
+            pltpu.SemaphoreType.DMA((2,)),
+            pltpu.SemaphoreType.DMA((2, steps_t)),
+        ],
     )
     cells_n = potential.size
     return pl.pallas_call(
@@ -166,15 +266,14 @@
         out_shape=[
             jax.ShapeDtypeStruct(multiplier.shape, f32),
             jax.ShapeDtypeStruct(potential.shape, f32),
-            jax.ShapeDtypeStruct(slab, f32),
-            jax.ShapeDtypeStruct((steps_t, 1, width_y, width_z), f32),
         ],
-        compiler_params=pltpu.CompilerParams(dimension_semantics=("arbitrary",)),
+        compiler_params=pltpu.CompilerParams(
+            dimension_semantics=("arbitrary",), collective_id=0, has_side_effects=True
+        ),
         cost_estimate=pl.CostEstimate(
             flops=cells_n * 200, transcendentals=cells_n * 11, bytes_accessed=cells_n * 4 * 12
         ),
-    )(idx, potential, potential, ahead_t, ahead_x, multiplier, start_density, final_density)
-
+    )(idx, potential, potential, potential, multiplier, start_density, final_density)
 
 def body(potential, multiplier, start_density, final_density):
     high = lax.Precision.HIGHEST
@@ -186,23 +285,13 @@
     block_y = width_y // (n_tm * n_sp)
     time_at = lax.axis_index("tm") * steps_t + jnp.arange(steps_t)
     row_at = lax.axis_index("space") * rows_x + jnp.arange(rows_x)
-    ahead_t = from_behind(potential[:1], "tm", -1)
-    ahead_x = from_behind(potential[:, :1], "space", -1)
-    next_multiplier, partial, flux_t_last, flux_x_last = cells(
-        potential, ahead_t, ahead_x, multiplier, start_density, final_density, n_tm, n_sp
+    next_multiplier, partial = cells(
+        potential, multiplier, start_density, final_density, n_tm, n_sp
     )
-    behind_t = from_behind(flux_t_last, "tm", 1)
-    behind_x = from_behind(flux_x_last, "space", 1)
     cos_y = cosine_table(width_y)
     cos_z = cosine_table(width_z)
     payload = jnp.einsum("txyi,ki->txyk", partial, cos_z, precision=high)
     payload = jnp.einsum("txiz,ki->txkz", payload, cos_y, precision=high)
-    edge_t = jnp.einsum("txyi,ki->txyk", behind_t, cos_z, precision=high)
-    edge_t = jnp.einsum("txiz,ki->txkz", edge_t, cos_y, precision=high)
-    edge_x = jnp.einsum("txyi,ki->txyk", behind_x, cos_z, precision=high)
-    edge_x = jnp.einsum("txiz,ki->txkz", edge_x, cos_y, precision=high)
-    payload = payload.at[:, :1].add(-edge_x)
-    payload = payload.at[:1].add(-edge_t)
     both = ("tm", "space")
     middle = lax.all_to_all(payload, both, split_axis=2, concat_axis=0, tiled=True)
     middle = middle.reshape(n_tm, n_sp, steps_t, rows_x, block_y, width_z)

time: 161 us -> 155 us (0.963)
  blocking collectives: 34.9 us -> 0 us
  waiting for transfers between devices: 41.5 us -> 59.7 us
  Pallas kernels: 17.3 us -> 33.8 us
  starting transfers between devices: 26.4 us -> 17 us
  local copies, waits for them, and re-layouts: 11.4 us -> 18.2 us
  matrix products: 27.4 us -> 24.3 us
    all_to_all x1 -> x0, blocking collectives: 34.9 us -> none  [body(): lax.all_to_all(solved, both, split_axis=0, concat_axis=2, tiled=True)]
    all_to_all x0 -> x1, waiting for transfers between devices: none -> 30.2 us  [body(): lax.all_to_all(solved, both, split_axis=0, concat_axis=2, tiled=True)]
    pallas_call x1, Pallas kernels: 17.3 us -> 33.8 us  [cells(): pl.pallas_call(functools.partial(cell_kernel, n_tm, n_sp), grid_spec=grid...]
    ppermute x4 -> x0, starting transfers between devices: 14 us -> none  [from_behind(): return lax.ppermute(block, axis, route)]
    ppermute x4 -> x0, waiting for transfers between devices: 12 us -> none  [from_behind(): return lax.ppermute(block, axis, route)]
    unnamed x5 -> x3, local copies, waits for them, and re-layouts: 1.73 us -> 9.2 us
    all_to_all x0 -> x1, starting transfers between devices: none -> 4.78 us  [body(): lax.all_to_all(solved, both, split_axis=0, concat_axis=2, tiled=True)]
    dot_general x4 -> x0, matrix products: 3.07 us -> none  [the longest x1 0.87 us: body(): edge_x = jnp.einsum('txyi,ki->txyk', behind_x, cos_z, precision=high)]
  transfers between devices with their start and end apart: 5 -> 2, of which waited for: 3 -> 2; matrix products, arithmetic and copies ran while one was open for 5% -> 0% of each run, Pallas kernels for 0% -> 0%
where the time goes in v2:
time: 155 us
  waiting for transfers between devices  59.7 us (39%)
  Pallas kernels  33.8 us (22%)
  matrix products  24.3 us (16%)
  local copies, waits for them, and re-layouts  18.2 us (12%)
  starting transfers between devices  17 us (11%)
    pallas_call x1, Pallas kernels, cells(): pl.pallas_call(functools.partial(cell_kernel, n_tm, n_sp), grid_spec=grid...  33.8 us
    all_to_all x1, waiting for transfers between devices, body(): lax.all_to_all(solved, both, split_axis=0, concat_axis=2, tiled=True)  30.2 us
    all_to_all x1, waiting for transfers between devices, body(): lax.all_to_all(payload, both, split_axis=2, concat_axis=0, tiled=True)  29.5 us
    all_to_all x1, starting transfers between devices, body(): lax.all_to_all(payload, both, split_axis=2, concat_axis=0, tiled=True)  12.2 us
    unnamed x3, local copies, waits for them, and re-layouts  9.2 us
    dot_general x1, matrix products, body(): next_potential = jnp.einsum('ik,txyk->txyi', cos_z, local, precision=high)  5.03 us
    all_to_all x1, starting transfers between devices, body(): lax.all_to_all(solved, both, split_axis=0, concat_axis=2, tiled=True)  4.78 us
    dot_general x1, matrix products, body(): payload = jnp.einsum('txyi,ki->txyk', partial, cos_z, precision=high)  3.73 us
  transfers between devices with their start and end apart: 2, of which 2 were waited for; matrix products, arithmetic and copies ran while one was open for 0% of the time, Pallas kernels for 0%

profile of v2, /device:TPU:1, one launch (start us, length us, event | category | flops | bytes accessed | tf_op | source)
XLA Modules:
  0.0 154.6 jit_solution(9062963147455358064)
XLA Ops:
  0.7 0.6 pad_add_fusion.idx_ref
  1.2 33.8 %shard_map.59 = (f32[4,8,4,128,128]{4,3,2,1,0:T(8,128)}, f32[8,4,128,128]{3,2,1,0:T(8,128)}) custom-call(s32[2]{0:T(128)} %pad_add_fusion.idx_ref, f32[8,4,128,128]{3,2,1,0:T(8,128)} %p_any.1, f32[8,4,128,128]{3,2,1,0:T(8,128)} %p_any.1, f32[8,4,128,128]{3,2,1,0:T(8,128)} %p_any.1, f32[4,8,4,128,128]{4,3,2,1,0:T(8,128)} %m.1, f32[4,128,128]{2,1,0:T(8,128)} %sd.1, ...), custom_call_target="tpu_custom_call" | custom-call | flops 104857600 | bytes 25165824 | tf_op jit(solution)/shard_map/pallas_call | solution.py:263
  35.0 3.7 %fusion.23 = f32[8,4,128,128]{3,2,1,0:T(8,128)S(1)} fusion(f32[8,4,128,128]{3,2,1,0:T(8,128)} %get-tuple-element.4, f32[128]{0:T(128)S(1)} %get-tuple-element.7, f32[128]{0:T(128)S(1)} %iota_multiply_fusion, f32[128]{0:T(128)S(1)} %get-tuple-element.6), kind=kOutput, calls=%fused_computation.20 | convolution fusion | flops 805355520 | bytes 4195840 | tf_op jit(solution)/shard_map/txyi,ki->txyk/dot_general | solution.py:293
  38.7 2.2 %convolution_bitcast_fusion.1 = f32[8,4,128,128]{3,2,1,0:T(8,128)S(1)} fusion(f32[8,4,128,128]{3,2,1,0:T(8,128)S(1)} %fusion.23, f32[128]{0:T(128)S(1)} %get-tuple-element.7, f32[128]{0:T(128)S(1)} %iota_multiply_fusion, f32[128]{0:T(128)S(1)} %get-tuple-element.6), kind=kOutput, calls=%fused_computation.16 | convolution fusion | flops 805355520 | bytes 4195840 | tf_op jit(solution)/shard_map/txiz,ki->txkz/dot_general | solution.py:294
  40.9 2.7 %copy.14 = f32[8,4,128,128]{3,1,0,2:T(4,128)} copy(f32[8,4,128,128]{3,2,1,0:T(8,128)S(1)} %convolution_bitcast_fusion.1) | data formatting | bytes 4194304 | tf_op jit(solution)/shard_map/txiz,ki->txkz/transpose | solution.py:294
  43.6 12.2 %all-to-all-start = ((f32[8,4,128,128]{3,1,0,2:T(4,128)}), f32[8,4,128,128]{3,1,0,2:T(4,128)S(1)}, u32[]{:S(2)}, u32[]{:S(2)}) async-start(f32[8,4,128,128]{3,1,0,2:T(4,128)} %copy.14), calls=%async_computation | async-start | bytes 4194304 | tf_op jit(solution)/shard_map/all_to_all | solution.py:296
  56.1 0.1 add_add_fusion
  56.2 29.5 %all-to-all-done = f32[8,4,128,128]{3,1,0,2:T(4,128)S(1)} async-done(((f32[8,4,128,128]{3,1,0,2:T(4,128)}), f32[8,4,128,128]{3,1,0,2:T(4,128)S(1)}, u32[]{:S(2)}, u32[]{:S(2)}) %all-to-all-start) | async-done | bytes 2097184 | tf_op jit(solution)/shard_map/all_to_all | solution.py:296
  85.7 0.2 copy.15
  85.8 2.1 %convolution_bitcast_fusion = f32[64,16,4,128]{3,0,2,1:T(8,128)S(1)} fusion(f32[8,16,8,4,128]{4,2,3,1,0:T(8,128)S(1)} %bitcast.80, f32[8,8]{1,0:T(8,128)S(1)} %fusion.77, f32[64]{0:T(128)S(1)} %get-tuple-element.9, f32[64]{0:T(128)S(1)} %get-tuple-element.8), kind=kOutput, calls=%fused_computation.15 | convolution fusion | flops 402665472 | bytes 4195072 | tf_op jit(solution)/shard_map/kat,abtxyz->kbxyz/dot_general | solution.py:300
  88.0 3.6 %fusion.2 = f32[64,64,128]{2,1,0:T(8,128)S(1)} fusion(f32[64,16,4,128]{3,0,2,1:T(8,128)S(1)} %convolution_bitcast_fusion, f32[128]{0:T(128)S(1)} %multiply_multiply_fusion, f32[64,64]{1,0:T(8,128)S(1)} %add_add_fusion, f32[16,4]{0,1:T(4,128)S(1)} %fusion.82, f32[64]{0:T(128)S(1)} %get-tuple-element.9, f32[64]{0:T(128)S(1)} %get-tuple-element.8), kind=kOutput, calls=%fused_computation.3 | convolution fusion | flops 404762624 | bytes 4211968 | tf_op jit(solution)/shard_map/jbx,kbxyz->kjyz/dot_general | solution.py:301
  91.6 3.2 %fusion.12 = f32[8,8,64,128,1]{3,1,2,0,4:T(8,128)S(1)} fusion(f32[64,64,128]{2,1,0:T(8,128)S(1)} %fusion.2, f32[64]{0:T(128)S(1)} %iota_add_fusion.1, f32[8,8]{1,0:T(8,128)S(1)} %get-tuple-element.11, f32[8,8]{1,0:T(8,128)S(1)} %get-tuple-element.10), kind=kOutput, calls=%fused_computation.13 | convolution fusion | flops 402665472 | bytes 4195072 | tf_op jit(solution)/shard_map/atk,kjyz->atjyz/dot_general | solution.py:312
  94.7 2.3 %fusion.15 = f32[8,16,8,4,1,128]{5,1,3,2,0,4:T(8,128)S(1)} fusion(f32[8,8,64,128,1]{3,1,2,0,4:T(8,128)S(1)} %fusion.12, f32[64]{0:T(128)S(1)} %iota_add_fusion.1, f32[16,4]{0,1:T(4,128)S(1)} %get-tuple-element.13, f32[16,4]{0,1:T(4,128)S(1)} %get-tuple-element.12), kind=kOutput, calls=%fused_computation.14 | convolution fusion | flops 402665472 | bytes 4195072 | tf_op jit(solution)/shard_map/bxj,atjyz->abtxyz/dot_general | solution.py:313
  97.1 1.4 copy.20
  98.5 2.7 %copy.21 = f32[1024,4,1,128]{3,1,2,0:T(4,128)} copy(f32[1024,4,1,128]{3,0,1,2:T(8,128)S(1)} %bitcast.81) | data formatting | bytes 4194304 | tf_op jit(solution)/shard_map/reshape | solution.py:314
  101.2 4.8 %all-to-all-start.1 = ((f32[1024,4,1,128]{3,1,2,0:T(4,128)}), f32[1024,4,1,128]{3,1,2,0:T(4,128)S(1)}, u32[]{:S(2)}, u32[]{:S(2)}) async-start(f32[1024,4,1,128]{3,1,2,0:T(4,128)} %copy.21), calls=%async_computation.1 | async-start | bytes 4194304 | tf_op jit(solution)/shard_map/all_to_all | solution.py:315
  106.0 30.2 %all-to-all-done.1 = f32[1024,4,1,128]{3,1,2,0:T(4,128)S(1)} async-done(((f32[1024,4,1,128]{3,1,2,0:T(4,128)}), f32[1024,4,1,128]{3,1,2,0:T(4,128)S(1)}, u32[]{:S(2)}, u32[]{:S(2)}) %all-to-all-start.1) | async-done | bytes 2097184 | tf_op jit(solution)/shard_map/all_to_all | solution.py:315
  136.2 0.0 copy-start
  136.2 1.3 copy-done
  137.5 2.0 %copy.23 = f32[128,8,4,1,128]{0,4,2,1,3:T(8,128)S(1)} copy(f32[128,8,4,1,128]{4,2,1,0,3:T(4,128)} %bitcast.79) | data formatting | bytes 4194304 | tf_op jit(solution)/shard_map/all_to_all | solution.py:315
  139.5 2.1 %fusion = f32[8,4,128,128]{3,2,1,0:T(8,128)S(1)} fusion(f32[128,8,4,1,128]{0,4,2,1,3:T(8,128)S(1)} %copy.23, f32[128]{0:T(128)S(1)} %get-tuple-element.7, f32[128]{0:T(128)S(1)} %iota_multiply_fusion, f32[128]{0:T(128)S(1)} %get-tuple-element.6), kind=kOutput, calls=%fused_computation | convolution fusion | flops 805355520 | bytes 4195840 | tf_op jit(solution)/shard_map/ik,txkz->txiz/dot_general | solution.py:316
  141.6 5.0 %fusion.3 = f32[8,4,128,128]{3,2,1,0:T(8,128)} fusion(f32[8,4,128,128]{3,2,1,0:T(8,128)S(1)} %fusion, f32[128]{0:T(128)S(1)} %get-tuple-element.7, f32[128]{0:T(128)S(1)} %iota_multiply_fusion, f32[128]{0:T(128)S(1)} %get-tuple-element.6), kind=kOutput, calls=%fused_computation.4 | convolution fusion | flops 805355520 | bytes 4195840 | tf_op jit(solution)/shard_map/ik,txyk->txyi/dot_general | solution.py:317
  146.7 7.9 %copy.52 = f32[4,8,4,128,128]{4,3,2,1,0:T(8,128)} copy(f32[4,8,4,128,128]{4,3,2,1,0:T(8,128)} %get-tuple-element.17) | data formatting | bytes 16777216
  (10 shorter events, 0.2 us)
Async XLA Ops:
  43.6 42.1 %all-to-all-start = ((f32[8,4,128,128]{3,1,0,2:T(4,128)}), f32[8,4,128,128]{3,1,0,2:T(4,128)S(1)}, u32[]{:S(2)}, u32[]{:S(2)}) async-start(f32[8,4,128,128]{3,1,0,2:T(4,128)} %copy.14), calls=%async_computation | async-start | bytes 4194304 | tf_op jit(solution)/shard_map/all_to_all | solution.py:296
  101.2 34.9 %all-to-all-start.1 = ((f32[1024,4,1,128]{3,1,2,0:T(4,128)}), f32[1024,4,1,128]{3,1,2,0:T(4,128)S(1)}, u32[]{:S(2)}, u32[]{:S(2)}) async-start(f32[1024,4,1,128]{3,1,2,0:T(4,128)} %copy.21), calls=%async_computation.1 | async-start | bytes 4194304 | tf_op jit(solution)/shard_map/all_to_all | solution.py:315
  136.2 1.3 copy-start

commit v3 on v2

--- a/solution.py
+++ b/solution.py
@@ -294,6 +294,8 @@
     payload = jnp.einsum("txiz,ki->txkz", payload, cos_y, precision=high)
     both = ("tm", "space")
     middle = lax.all_to_all(payload, both, split_axis=2, concat_axis=0, tiled=True)
+    next_multiplier = jnp.where(next_multiplier == next_multiplier, next_multiplier, 0.0)
+    middle, next_multiplier = lax.optimization_barrier((middle, next_multiplier))
     middle = middle.reshape(n_tm, n_sp, steps_t, rows_x, block_y, width_z)
     cos_t = cosine_table(total_t).reshape(total_t, n_tm, steps_t)
     cos_x = cosine_table(total_x).reshape(total_x, n_sp, rows_x)

time: 155 us -> 144 us (0.929)
  waiting for transfers between devices: 59.7 us -> 21 us
  blocking collectives: 0 us -> 35 us
  local copies, waits for them, and re-layouts: 18.2 us -> 7.38 us
  other arithmetic: 0.84 us -> 9.36 us
  starting transfers between devices: 17 us -> 12.2 us
    all_to_all x0 -> x1, blocking collectives: none -> 35 us  [body(): lax.all_to_all(solved, both, split_axis=0, concat_axis=2, tiled=True)]
    all_to_all x1 -> x0, waiting for transfers between devices: 30.2 us -> none  [body(): lax.all_to_all(solved, both, split_axis=0, concat_axis=2, tiled=True)]
    unnamed x3 -> x0, local copies, waits for them, and re-layouts: 9.2 us -> none
    all_to_all x1, waiting for transfers between devices: 29.5 us -> 21 us  [body(): lax.all_to_all(payload, both, split_axis=2, concat_axis=0, tiled=True)]
    select_n x0 -> x1, other arithmetic: none -> 8.53 us  [body(): jnp.where(next_multiplier == next_multiplier, next_multiplier, 0.0)]
    all_to_all x1 -> x0, starting transfers between devices: 4.78 us -> none  [body(): lax.all_to_all(solved, both, split_axis=0, concat_axis=2, tiled=True)]
  transfers between devices with their start and end apart: 2 -> 1, of which waited for: 2 -> 1; matrix products, arithmetic and copies ran while one was open for 0% -> 6% of each run, Pallas kernels for 0% -> 0%
where the time goes in v3:
time: 144 us
  blocking collectives  35 us (24%)
  Pallas kernels  33.7 us (23%)
  matrix products  24.5 us (17%)
  waiting for transfers between devices  21 us (15%)
  starting transfers between devices  12.2 us (8%)
  other arithmetic  9.36 us (6%)
  local copies, waits for them, and re-layouts  7.38 us (5%)
    all_to_all x1, blocking collectives, body(): lax.all_to_all(solved, both, split_axis=0, concat_axis=2, tiled=True)  35 us
    pallas_call x1, Pallas kernels, cells(): pl.pallas_call(functools.partial(cell_kernel, n_tm, n_sp), grid_spec=grid...  33.7 us
    all_to_all x1, waiting for transfers between devices, body(): lax.all_to_all(payload, both, split_axis=2, concat_axis=0, tiled=True)  21 us
    all_to_all x1, starting transfers between devices, body(): lax.all_to_all(payload, both, split_axis=2, concat_axis=0, tiled=True)  12.2 us
    select_n x1, other arithmetic, body(): jnp.where(next_multiplier == next_multiplier, next_multiplier, 0.0)  8.53 us
    dot_general x1, matrix products, body(): next_potential = jnp.einsum('ik,txyk->txyi', cos_z, local, precision=high)  5.03 us
    dot_general x1, matrix products, body(): payload = jnp.einsum('txyi,ki->txyk', partial, cos_z, precision=high)  3.74 us
    dot_general x1, matrix products, body(): hat = jnp.einsum('jbx,kbxyz->kjyz', cos_x, hat, precision=high)  3.62 us
  transfers between devices with their start and end apart: 1, of which 1 were waited for; matrix products, arithmetic and copies ran while one was open for 6% of the time, Pallas kernels for 0%

profile of v3, /device:TPU:1, one launch (start us, length us, event | category | flops | bytes accessed | tf_op | source)
XLA Modules:
  0.0 144.0 jit_solution(15127375373688822445)
XLA Ops:
  0.7 0.6 pad_add_fusion.idx_ref
  1.2 33.7 %shard_map.59 = (f32[4,8,4,128,128]{4,3,2,1,0:T(8,128)}, f32[8,4,128,128]{3,2,1,0:T(8,128)}) custom-call(s32[2]{0:T(128)} %pad_add_fusion.idx_ref, f32[8,4,128,128]{3,2,1,0:T(8,128)} %p_any.1, f32[8,4,128,128]{3,2,1,0:T(8,128)} %p_any.1, f32[8,4,128,128]{3,2,1,0:T(8,128)} %p_any.1, f32[4,8,4,128,128]{4,3,2,1,0:T(8,128)} %m.1, f32[4,128,128]{2,1,0:T(8,128)} %sd.1, ...), custom_call_target="tpu_custom_call" | custom-call | flops 104857600 | bytes 25165824 | tf_op jit(solution)/shard_map/pallas_call | solution.py:263
  35.0 3.7 %fusion.28 = f32[8,4,128,128]{3,2,1,0:T(8,128)S(1)} fusion(f32[8,4,128,128]{3,2,1,0:T(8,128)} %get-tuple-element.6, f32[128]{0:T(128)S(1)} %get-tuple-element.11, f32[128]{0:T(128)S(1)} %iota_multiply_fusion, f32[128]{0:T(128)S(1)} %get-tuple-element.10), kind=kOutput, calls=%fused_computation.24 | convolution fusion | flops 805355520 | bytes 4195840 | tf_op jit(solution)/shard_map/txyi,ki->txyk/dot_general | solution.py:293
  38.7 2.2 %convolution_bitcast_fusion = f32[8,4,128,128]{3,2,1,0:T(8,128)S(1)} fusion(f32[8,4,128,128]{3,2,1,0:T(8,128)S(1)} %fusion.28, f32[128]{0:T(128)S(1)} %get-tuple-element.11, f32[128]{0:T(128)S(1)} %iota_multiply_fusion, f32[128]{0:T(128)S(1)} %get-tuple-element.10), kind=kOutput, calls=%fused_computation.20 | convolution fusion | flops 805355520 | bytes 4195840 | tf_op jit(solution)/shard_map/txiz,ki->txkz/dot_general | solution.py:294
  40.9 2.7 %copy.17 = f32[8,4,128,128]{3,1,0,2:T(4,128)} copy(f32[8,4,128,128]{3,2,1,0:T(8,128)S(1)} %convolution_bitcast_fusion) | data formatting | bytes 4194304 | tf_op jit(solution)/shard_map/txiz,ki->txkz/transpose | solution.py:294
  43.6 12.2 %all-to-all-start = ((f32[8,4,128,128]{3,1,0,2:T(4,128)}), f32[8,4,128,128]{3,1,0,2:T(4,128)S(1)}, u32[]{:S(2)}, u32[]{:S(2)}) async-start(f32[8,4,128,128]{3,1,0,2:T(4,128)} %copy.17), calls=%async_computation | async-start | bytes 4194304 | tf_op jit(solution)/shard_map/all_to_all | solution.py:296
  56.1 0.1 add_add_fusion
  56.1 8.5 %compare_select_fusion = f32[4,8,4,128,128]{4,3,2,1,0:T(8,128)} fusion(f32[4,8,4,128,128]{4,3,2,1,0:T(8,128)} %get-tuple-element.7), kind=kLoop, calls=%fused_computation | loop fusion | flops 4194304 | bytes 16777216 | tf_op jit(solution)/shard_map/jit(_where)/select_n | solution.py:297
  64.7 21.0 %all-to-all-done = f32[8,4,128,128]{3,1,0,2:T(4,128)S(1)} async-done(((f32[8,4,128,128]{3,1,0,2:T(4,128)}), f32[8,4,128,128]{3,1,0,2:T(4,128)S(1)}, u32[]{:S(2)}, u32[]{:S(2)}) %all-to-all-start) | async-done | bytes 2097184 | tf_op jit(solution)/shard_map/all_to_all | solution.py:296
  85.6 0.1 copy.59
  85.8 2.1 %fusion.14 = f32[64,16,4,128]{3,0,2,1:T(8,128)S(1)} fusion(f32[8,16,8,4,128]{4,2,1,0,3:T(8,128)S(1)} %bitcast.77, f32[8,8]{1,0:T(8,128)S(1)} %fusion.82, f32[64]{0:T(128)S(1)} %get-tuple-element.13, f32[64]{0:T(128)S(1)} %get-tuple-element.12), kind=kOutput, calls=%fused_computation.17 | convolution fusion | flops 402665472 | bytes 4195072 | tf_op jit(solution)/shard_map/kat,abtxyz->kbxyz/dot_general | solution.py:302
  87.9 3.6 %fusion.2 = f32[64,64,128]{2,1,0:T(8,128)S(1)} fusion(f32[64,16,4,128]{3,0,2,1:T(8,128)S(1)} %fusion.14, f32[128]{0:T(128)S(1)} %multiply_multiply_fusion, f32[64,64]{1,0:T(8,128)S(1)} %add_add_fusion, f32[16,4]{0,1:T(4,128)S(1)} %fusion.87, f32[64]{0:T(128)S(1)} %get-tuple-element.13, f32[64]{0:T(128)S(1)} %get-tuple-element.12), kind=kOutput, calls=%fused_computation.4 | convolution fusion | flops 404762624 | bytes 4211968 | tf_op jit(solution)/shard_map/jbx,kbxyz->kjyz/dot_general | solution.py:303
  91.5 3.2 %fusion.17 = f32[8,8,64,128,1]{3,1,2,0,4:T(8,128)S(1)} fusion(f32[64,64,128]{2,1,0:T(8,128)S(1)} %fusion.2, f32[64]{0:T(128)S(1)} %iota_add_fusion.1, f32[8,8]{1,0:T(8,128)S(1)} %get-tuple-element.15, f32[8,8]{1,0:T(8,128)S(1)} %get-tuple-element.14), kind=kOutput, calls=%fused_computation.18 | convolution fusion | flops 402665472 | bytes 4195072 | tf_op jit(solution)/shard_map/atk,kjyz->atjyz/dot_general | solution.py:314
  94.7 2.6 %fusion.20 = f32[8,16,8,4,1,128]{5,1,3,2,0,4:T(8,128)S(1)} fusion(f32[8,8,64,128,1]{3,1,2,0,4:T(8,128)S(1)} %fusion.17, f32[64]{0:T(128)S(1)} %iota_add_fusion.1, f32[16,4]{0,1:T(4,128)S(1)} %get-tuple-element.17, f32[16,4]{0,1:T(4,128)S(1)} %get-tuple-element.16), kind=kOutput, calls=%fused_computation.19 | convolution fusion | flops 402665472 | bytes 4195072 | tf_op jit(solution)/shard_map/bxj,atjyz->abtxyz/dot_general | solution.py:315
  97.3 1.2 copy.23
  98.5 1.4 copy.24
  99.8 35.0 %all_to_all.36 = f32[1024,4,1,128]{3,1,2,0:T(4,128)} all-to-all(f32[1024,4,1,128]{3,1,2,0:T(4,128)S(1)} %copy.24), channel_id=1, replica_groups=mesh['tm'=8,'space'=16] {'tm','space'}, dimensions={0} | all-to-all | bytes 4194304 | tf_op jit(solution)/shard_map/all_to_all | solution.py:317
  134.8 2.0 %copy.26 = f32[128,8,4,1,128]{0,4,2,1,3:T(8,128)S(1)} copy(f32[128,8,4,1,128]{4,2,1,0,3:T(4,128)} %bitcast.79) | data formatting | bytes 4194304 | tf_op jit(solution)/shard_map/all_to_all | solution.py:317
  136.8 2.1 %fusion = f32[8,4,128,128]{3,2,1,0:T(8,128)S(1)} fusion(f32[128,8,4,1,128]{0,4,2,1,3:T(8,128)S(1)} %copy.26, f32[128]{0:T(128)S(1)} %get-tuple-element.11, f32[128]{0:T(128)S(1)} %iota_multiply_fusion, f32[128]{0:T(128)S(1)} %get-tuple-element.10), kind=kOutput, calls=%fused_computation.1 | convolution fusion | flops 805355520 | bytes 4195840 | tf_op jit(solution)/shard_map/ik,txkz->txiz/dot_general | solution.py:318
  139.0 5.0 %fusion.3 = f32[8,4,128,128]{3,2,1,0:T(8,128)} fusion(f32[8,4,128,128]{3,2,1,0:T(8,128)S(1)} %fusion, f32[128]{0:T(128)S(1)} %get-tuple-element.11, f32[128]{0:T(128)S(1)} %iota_multiply_fusion, f32[128]{0:T(128)S(1)} %get-tuple-element.10), kind=kOutput, calls=%fused_computation.5 | convolution fusion | flops 805355520 | bytes 4195840 | tf_op jit(solution)/shard_map/ik,txyk->txyi/dot_general | solution.py:319
  (10 shorter events, 0.2 us)
Async XLA Ops:
  43.6 42.1 %all-to-all-start = ((f32[8,4,128,128]{3,1,0,2:T(4,128)}), f32[8,4,128,128]{3,1,0,2:T(4,128)S(1)}, u32[]{:S(2)}, u32[]{:S(2)}) async-start(f32[8,4,128,128]{3,1,0,2:T(4,128)} %copy.17), calls=%async_computation | async-start | bytes 4194304 | tf_op jit(solution)/shard_map/all_to_all | solution.py:296

commit v4 on v3

--- a/solution.py
+++ b/solution.py
@@ -291,15 +291,15 @@
     cos_y = cosine_table(width_y)
     cos_z = cosine_table(width_z)
     payload = jnp.einsum("txyi,ki->txyk", partial, cos_z, precision=high)
-    payload = jnp.einsum("txiz,ki->txkz", payload, cos_y, precision=high)
+    payload = jnp.einsum("txiz,ki->ktxz", payload, cos_y, precision=high)
     both = ("tm", "space")
-    middle = lax.all_to_all(payload, both, split_axis=2, concat_axis=0, tiled=True)
+    middle = lax.all_to_all(payload, both, split_axis=0, concat_axis=0, tiled=True)
     next_multiplier = jnp.where(next_multiplier == next_multiplier, next_multiplier, 0.0)
     middle, next_multiplier = lax.optimization_barrier((middle, next_multiplier))
-    middle = middle.reshape(n_tm, n_sp, steps_t, rows_x, block_y, width_z)
+    middle = middle.reshape(n_tm, n_sp, block_y, steps_t, rows_x, width_z)
     cos_t = cosine_table(total_t).reshape(total_t, n_tm, steps_t)
     cos_x = cosine_table(total_x).reshape(total_x, n_sp, rows_x)
-    hat = jnp.einsum("kat,abtxyz->kbxyz", cos_t, middle, precision=high)
+    hat = jnp.einsum("kat,abytxz->kbxyz", cos_t, middle, precision=high)
     hat = jnp.einsum("jbx,kbxyz->kjyz", cos_x, hat, precision=high)
     freq_y = (
         (lax.axis_index("tm") * n_sp + lax.axis_index("space")) * block_y + jnp.arange(block_y)
@@ -312,10 +312,10 @@
     denom = denom + eig_y[None, None, :, None] + eig_z[None, None, None, :]
     hat = hat / (RATE * denom + PROX)
     hat = jnp.einsum("atk,kjyz->atjyz", cos_t.reshape(n_tm, steps_t, total_t), hat, precision=high)
-    solved = jnp.einsum("bxj,atjyz->abtxyz", cos_x.reshape(n_sp, rows_x, total_x), hat, precision=high)
-    solved = solved.reshape(n_tm * n_sp * steps_t, rows_x, block_y, width_z)
-    local = lax.all_to_all(solved, both, split_axis=0, concat_axis=2, tiled=True)
-    local = jnp.einsum("ik,txkz->txiz", cos_y, local, precision=high)
+    solved = jnp.einsum("bxj,atjyz->abytxz", cos_x.reshape(n_sp, rows_x, total_x), hat, precision=high)
+    solved = solved.reshape(n_tm * n_sp * block_y, steps_t, rows_x, width_z)
+    local = lax.all_to_all(solved, both, split_axis=0, concat_axis=0, tiled=True)
+    local = jnp.einsum("ik,ktxz->txiz", cos_y, local, precision=high)
     next_potential = jnp.einsum("ik,txyk->txyi", cos_z, local, precision=high)
     return (next_potential, next_multiplier)
 

time: 144 us -> 143 us (level)
  local copies, waits for them, and re-layouts: 7.38 us -> 4.41 us
  matrix products: 24.5 us -> 27 us
    transpose x2 -> x1, local copies, waits for them, and re-layouts: 3.89 us -> 1.2 us  [body(): jnp.einsum('bxj,atjyz->abytxz', cos_x.reshape(n_sp, rows_x, total_x), hat...]
    dot_general x0 -> x1, local copies, waits for them, and re-layouts: none -> 2.67 us  [body(): payload = jnp.einsum('txiz,ki->ktxz', payload, cos_y, precision=high)]
    dot_general x4, matrix products: 8.99 us -> 11.4 us  [the longest x1 4.53 us: body(): local = jnp.einsum('ik,ktxz->txiz', cos_y, local, precision=high)]
    all_to_all x2 -> x0, local copies, waits for them, and re-layouts: 2.14 us -> none  [the longest x1 2.01 us: body(): lax.all_to_all(solved, both, split_axis=0, concat_axis=2, tiled=True)]
where the time goes in v4:
time: 143 us
  blocking collectives  34.6 us (24%)
  Pallas kernels  33.7 us (24%)
  matrix products  27 us (19%)
  waiting for transfers between devices  21 us (15%)
  starting transfers between devices  12.2 us (9%)
  other arithmetic  9.36 us (7%)
  local copies, waits for them, and re-layouts  4.41 us (3%)
    all_to_all x1, blocking collectives, body(): lax.all_to_all(solved, both, split_axis=0, concat_axis=0, tiled=True)  34.6 us
    pallas_call x1, Pallas kernels, cells(): pl.pallas_call(functools.partial(cell_kernel, n_tm, n_sp), grid_spec=grid...  33.7 us
    all_to_all x1, waiting for transfers between devices, body(): lax.all_to_all(payload, both, split_axis=0, concat_axis=0, tiled=True)  21 us
    all_to_all x1, starting transfers between devices, body(): lax.all_to_all(payload, both, split_axis=0, concat_axis=0, tiled=True)  12.2 us
    select_n x1, other arithmetic, body(): jnp.where(next_multiplier == next_multiplier, next_multiplier, 0.0)  8.53 us
    dot_general x1, matrix products, body(): next_potential = jnp.einsum('ik,txyk->txyi', cos_z, local, precision=high)  5.03 us
    dot_general x1, matrix products, body(): local = jnp.einsum('ik,ktxz->txiz', cos_y, local, precision=high)  4.53 us
    dot_general x1, matrix products, body(): payload = jnp.einsum('txyi,ki->txyk', partial, cos_z, precision=high)  3.74 us
  transfers between devices with their start and end apart: 1, of which 1 were waited for; matrix products, arithmetic and copies ran while one was open for 6% of the time, Pallas kernels for 0%

profile of v4, /device:TPU:1, one launch (start us, length us, event | category | flops | bytes accessed | tf_op | source)
XLA Modules:
  0.0 143.1 jit_solution(15071082547230530899)
XLA Ops:
  0.7 0.6 pad_add_fusion.idx_ref
  1.2 33.7 %shard_map.59 = (f32[4,8,4,128,128]{4,3,2,1,0:T(8,128)}, f32[8,4,128,128]{3,2,1,0:T(8,128)}) custom-call(s32[2]{0:T(128)} %pad_add_fusion.idx_ref, f32[8,4,128,128]{3,2,1,0:T(8,128)} %p_any.1, f32[8,4,128,128]{3,2,1,0:T(8,128)} %p_any.1, f32[8,4,128,128]{3,2,1,0:T(8,128)} %p_any.1, f32[4,8,4,128,128]{4,3,2,1,0:T(8,128)} %m.1, f32[4,128,128]{2,1,0:T(8,128)} %sd.1, ...), custom_call_target="tpu_custom_call" | custom-call | flops 104857600 | bytes 25165824 | tf_op jit(solution)/shard_map/pallas_call | solution.py:263
  35.0 3.7 %fusion.29 = f32[8,4,128,128]{3,2,1,0:T(8,128)S(1)} fusion(f32[8,4,128,128]{3,2,1,0:T(8,128)} %get-tuple-element.6, f32[128]{0:T(128)S(1)} %get-tuple-element.11, f32[128]{0:T(128)S(1)} %iota_multiply_fusion.1, f32[128]{0:T(128)S(1)} %get-tuple-element.10), kind=kOutput, calls=%fused_computation.23 | convolution fusion | flops 805355520 | bytes 4195840 | tf_op jit(solution)/shard_map/txyi,ki->txyk/dot_general | solution.py:293
  38.7 2.2 %fusion.27 = f32[128,8,4,128]{3,0,2,1:T(8,128)S(1)} fusion(f32[8,4,128,128]{3,2,1,0:T(8,128)S(1)} %fusion.29, f32[128]{0:T(128)S(1)} %get-tuple-element.11, f32[128]{0:T(128)S(1)} %iota_multiply_fusion.1, f32[128]{0:T(128)S(1)} %get-tuple-element.10), kind=kOutput, calls=%fused_computation.21 | convolution fusion | flops 805355520 | bytes 4195840 | tf_op jit(solution)/shard_map/txiz,ki->ktxz/dot_general | solution.py:294
  40.9 2.7 %copy.19 = f32[128,8,4,128]{3,2,1,0:T(4,128)} copy(f32[128,8,4,128]{3,0,2,1:T(8,128)S(1)} %fusion.27) | data formatting | bytes 4194304 | tf_op jit(solution)/shard_map/txiz,ki->ktxz/dot_general | solution.py:294
  43.6 12.2 %all-to-all-start = ((f32[128,8,4,128]{3,2,1,0:T(4,128)}), f32[128,8,4,128]{3,2,1,0:T(4,128)S(1)}, u32[]{:S(2)}, u32[]{:S(2)}) async-start(f32[128,8,4,128]{3,2,1,0:T(4,128)} %copy.19), calls=%async_computation | async-start | bytes 4194304 | tf_op jit(solution)/shard_map/all_to_all | solution.py:296
  56.1 0.1 add_add_fusion
  56.1 8.5 %compare_select_fusion = f32[4,8,4,128,128]{4,3,2,1,0:T(8,128)} fusion(f32[4,8,4,128,128]{4,3,2,1,0:T(8,128)} %get-tuple-element.7), kind=kLoop, calls=%fused_computation | loop fusion | flops 4194304 | bytes 16777216 | tf_op jit(solution)/shard_map/jit(_where)/select_n | solution.py:297
  64.7 21.0 %all-to-all-done = f32[128,8,4,128]{3,2,1,0:T(4,128)S(1)} async-done(((f32[128,8,4,128]{3,2,1,0:T(4,128)}), f32[128,8,4,128]{3,2,1,0:T(4,128)S(1)}, u32[]{:S(2)}, u32[]{:S(2)}) %all-to-all-start) | async-done | bytes 2097184 | tf_op jit(solution)/shard_map/all_to_all | solution.py:296
  85.6 2.1 %fusion.14 = f32[64,16,4,128]{3,0,2,1:T(8,128)S(1)} fusion(f32[8,16,8,4,128]{4,3,2,1,0:T(4,128)S(1)} %bitcast.67, f32[8,8]{1,0:T(8,128)S(1)} %fusion.83, f32[64]{0:T(128)S(1)} %get-tuple-element.13, f32[64]{0:T(128)S(1)} %get-tuple-element.12), kind=kOutput, calls=%fused_computation.16 | convolution fusion | flops 402665472 | bytes 4195072 | tf_op jit(solution)/shard_map/kat,abytxz->kbxyz/dot_general | solution.py:302
  87.8 3.6 %fusion = f32[64,64,128]{2,1,0:T(8,128)S(1)} fusion(f32[64,16,4,128]{3,0,2,1:T(8,128)S(1)} %fusion.14, f32[128]{0:T(128)S(1)} %multiply_multiply_fusion, f32[64,64]{1,0:T(8,128)S(1)} %add_add_fusion, f32[16,4]{0,1:T(4,128)S(1)} %fusion.88, f32[64]{0:T(128)S(1)} %get-tuple-element.13, f32[64]{0:T(128)S(1)} %get-tuple-element.12), kind=kOutput, calls=%fused_computation.2 | convolution fusion | flops 404762624 | bytes 4211968 | tf_op jit(solution)/shard_map/jbx,kbxyz->kjyz/dot_general | solution.py:303
  91.4 3.2 %fusion.17 = f32[8,8,64,128,1]{3,1,2,0,4:T(8,128)S(1)} fusion(f32[64,64,128]{2,1,0:T(8,128)S(1)} %fusion, f32[64]{0:T(128)S(1)} %iota_add_fusion.1, f32[8,8]{1,0:T(8,128)S(1)} %get-tuple-element.15, f32[8,8]{1,0:T(8,128)S(1)} %get-tuple-element.14), kind=kOutput, calls=%fused_computation.17 | convolution fusion | flops 402665472 | bytes 4195072 | tf_op jit(solution)/shard_map/atk,kjyz->atjyz/dot_general | solution.py:314
  94.6 2.6 %fusion.20 = f32[8,16,1,8,4,128]{5,1,4,3,0,2:T(8,128)S(1)} fusion(f32[8,8,64,128,1]{3,1,2,0,4:T(8,128)S(1)} %fusion.17, f32[64]{0:T(128)S(1)} %iota_add_fusion.1, f32[16,4]{0,1:T(4,128)S(1)} %get-tuple-element.17, f32[16,4]{0,1:T(4,128)S(1)} %get-tuple-element.16), kind=kOutput, calls=%fused_computation.18 | convolution fusion | flops 402665472 | bytes 4195072 | tf_op jit(solution)/shard_map/bxj,atjyz->abytxz/dot_general | solution.py:315
  97.1 1.2 copy.24
  98.3 0.5 copy.25
  98.9 34.6 %all_to_all.10 = f32[128,8,4,128]{3,2,1,0:T(4,128)S(1)} all-to-all(f32[128,8,4,128]{3,2,1,0:T(4,128)S(1)} %copy.25), channel_id=1, replica_groups=mesh['tm'=8,'space'=16] {'tm','space'}, dimensions={0} | all-to-all | bytes 4194304 | tf_op jit(solution)/shard_map/all_to_all | solution.py:317
  133.5 4.5 %fusion.7 = f32[8,4,128,128]{3,2,1,0:T(8,128)S(1)} fusion(f32[128,8,4,128]{3,2,1,0:T(4,128)S(1)} %all_to_all.10, f32[128]{0:T(128)S(1)} %get-tuple-element.11, f32[128]{0:T(128)S(1)} %iota_multiply_fusion.1, f32[128]{0:T(128)S(1)} %get-tuple-element.10), kind=kOutput, calls=%fused_computation.9 | convolution fusion | flops 805355520 | bytes 4195840 | tf_op jit(solution)/shard_map/ik,ktxz->txiz/dot_general | solution.py:318
  138.0 5.0 %fusion.1 = f32[8,4,128,128]{3,2,1,0:T(8,128)} fusion(f32[8,4,128,128]{3,2,1,0:T(8,128)S(1)} %fusion.7, f32[128]{0:T(128)S(1)} %get-tuple-element.11, f32[128]{0:T(128)S(1)} %iota_multiply_fusion.1, f32[128]{0:T(128)S(1)} %get-tuple-element.10), kind=kOutput, calls=%fused_computation.3 | convolution fusion | flops 805355520 | bytes 4195840 | tf_op jit(solution)/shard_map/ik,txyk->txyi/dot_general | solution.py:319
  (10 shorter events, 0.2 us)
Async XLA Ops:
  43.6 42.1 %all-to-all-start = ((f32[128,8,4,128]{3,2,1,0:T(4,128)}), f32[128,8,4,128]{3,2,1,0:T(4,128)S(1)}, u32[]{:S(2)}, u32[]{:S(2)}) async-start(f32[128,8,4,128]{3,2,1,0:T(4,128)} %copy.19), calls=%async_computation | async-start | bytes 4194304 | tf_op jit(solution)/shard_map/all_to_all | solution.py:296

commit v5 on v4

--- a/solution.py
+++ b/solution.py
@@ -69,7 +69,7 @@
     return jnp.concatenate([new_lead[None], new_side], axis=0)
 
 
-def cell_kernel(n_tm, n_sp, idx_ref, pc, pn, p_any, m, sd, fd, nm_out, pay_out,
+def cell_kernel(n_tm, n_sp, idx_ref, pc, pn, p_any, m, sd, fd, cy, cz, nm_out, pay_out,
                 ft_carry, ahead_t, ahead_x, send_x, send_t, behind_t, behind_x,
                 at_sems, ax_sems, bt_sems, bx_sems):
     t = pl.program_id(0)
@@ -95,10 +95,17 @@
             p_any.at[row, 0], ahead_x.at[row], ax_sems.at[0, row], ax_sems.at[1, row],
             device_id=(tm, sp - 1), device_id_type=mesh_id)
 
-    def behind_t_copy():
+    def behind_t_copy(x):
         return pltpu.make_async_remote_copy(
-            send_t, behind_t, bt_sems.at[0], bt_sems.at[1],
+            send_t.at[x], behind_t.at[x], bt_sems.at[0, x], bt_sems.at[1, x],
             device_id=(tm + 1, sp), device_id_type=mesh_id)
+
+    def transform(v):
+        high = lax.Precision.HIGHEST
+        along_z = lax.dot_general(v, cz[...], (((1,), (1,)), ((), ())), precision=high,
+                                  preferred_element_type=jnp.float32)
+        return lax.dot_general(cy[...], along_z, (((1,), (0,)), ((), ())), precision=high,
+                               preferred_element_type=jnp.float32)
 
     def behind_x_copy(row):
         return pltpu.make_async_remote_copy(
@@ -180,7 +187,14 @@
         ft_prev = jnp.where(t == 0, 0.0, ft_carry[x])
         div_t = ft_prev - jnp.where(last_t, 0.0, flux[0])
         ft_carry[x] = flux[0]
-        send_t[x] = flux[0]
+
+        @pl.when(t == steps_t - 1)
+        def _():
+            send_t[x] = flux[0]
+
+            @pl.when(has_later_t)
+            def _():
+                behind_t_copy(x).start()
         if x < rows_x - 1:
             fx_cur = flux[1]
         else:
@@ -192,27 +206,23 @@
                 behind_x_copy(t).start()
         div_x = -fx_cur if fx_prev is None else fx_prev - fx_cur
         fx_prev = flux[1]
-        pay_out[t, x] = rest - div_t - div_x
+        pay_out[t, x] = transform(rest - div_t - div_x)
 
     @pl.when(t == steps_t - 1)
     def _():
-        @pl.when(has_later_t)
-        def _():
-            behind_t_copy().start()
-
         @pl.when(has_earlier_t)
         def _():
             ahead_t_copy().wait_send()
-            behind_t_copy().wait_recv()
             for x in range(rows_x):
-                pay_out[0, x] = pay_out[0, x] - behind_t[x]
+                behind_t_copy(x).wait_recv()
+                pay_out[0, x] = pay_out[0, x] - transform(behind_t[x])
 
         @pl.when(has_earlier_x)
         def _():
             for r in range(steps_t):
                 ahead_x_copy(r).wait_send()
                 behind_x_copy(r).wait_recv()
-                pay_out[r, 0] = pay_out[r, 0] - behind_x[r]
+                pay_out[r, 0] = pay_out[r, 0] - transform(behind_x[r])
 
         @pl.when(has_later_x)
         def _():
@@ -221,7 +231,8 @@
 
         @pl.when(has_later_t)
         def _():
-            behind_t_copy().wait_send()
+            for x in range(rows_x):
+                behind_t_copy(x).wait_send()
 
 
 def cells(potential, multiplier, start_density, final_density, n_tm, n_sp):
@@ -240,6 +251,8 @@
             pl.BlockSpec((4, 1, rows_x, width_y, width_z), lambda t, s: (0, t, 0, 0, 0)),
             pl.BlockSpec(plane, lambda t, s: (0, 0, 0)),
             pl.BlockSpec(plane, lambda t, s: (0, 0, 0)),
+            pl.BlockSpec((width_y, width_y), lambda t, s: (0, 0)),
+            pl.BlockSpec((width_z, width_z), lambda t, s: (0, 0)),
         ],
         out_specs=[
             pl.BlockSpec((4, 1, rows_x, width_y, width_z), lambda t, s: (0, t, 0, 0, 0)),
@@ -255,7 +268,7 @@
             pltpu.VMEM((steps_t, width_y, width_z), f32),
             pltpu.SemaphoreType.DMA((2,)),
             pltpu.SemaphoreType.DMA((2, steps_t)),
-            pltpu.SemaphoreType.DMA((2,)),
+            pltpu.SemaphoreType.DMA((2, rows_x)),
             pltpu.SemaphoreType.DMA((2, steps_t)),
         ],
     )
@@ -273,7 +286,8 @@
         cost_estimate=pl.CostEstimate(
             flops=cells_n * 200, transcendentals=cells_n * 11, bytes_accessed=cells_n * 4 * 12
         ),
-    )(idx, potential, potential, potential, multiplier, start_density, final_density)
+    )(idx, potential, potential, potential, multiplier, start_density, final_density,
+      cosine_table(width_y), cosine_table(width_z))
 
 def body(potential, multiplier, start_density, final_density):
     high = lax.Precision.HIGHEST
@@ -290,8 +304,7 @@
     )
     cos_y = cosine_table(width_y)
     cos_z = cosine_table(width_z)
-    payload = jnp.einsum("txyi,ki->txyk", partial, cos_z, precision=high)
-    payload = jnp.einsum("txiz,ki->ktxz", payload, cos_y, precision=high)
+    payload = partial.transpose(2, 0, 1, 3)
     both = ("tm", "space")
     middle = lax.all_to_all(payload, both, split_axis=0, concat_axis=0, tiled=True)
     next_multiplier = jnp.where(next_multiplier == next_multiplier, next_multiplier, 0.0)

time: 143 us -> 156 us (1.091)
  Pallas kernels: 33.7 us -> 48.1 us
  matrix products: 27 us -> 21 us
  local copies, waits for them, and re-layouts: 4.41 us -> 6 us
    pallas_call x1, Pallas kernels: 33.7 us -> 48.1 us  [cells(): pl.pallas_call(functools.partial(cell_kernel, n_tm, n_sp), grid_spec=grid...]
    dot_general x2 -> x0, matrix products: 5.92 us -> none  [the longest x1 3.74 us: body(): payload = jnp.einsum('txyi,ki->txyk', partial, cos_z, precision=high)]
    transpose x0 -> x1, local copies, waits for them, and re-layouts: none -> 4.26 us  [body(): payload = partial.transpose(2, 0, 1, 3)]
    dot_general x1 -> x0, local copies, waits for them, and re-layouts: 2.67 us -> none  [body(): payload = jnp.einsum('txiz,ki->ktxz', payload, cos_y, precision=high)]
where the time goes in v5:
time: 156 us; the launch traced here: 155 us
  Pallas kernels  48.1 us (31%)
  blocking collectives  34.6 us (22%)
  waiting for transfers between devices  21 us (13%)
  matrix products  21 us (13%)
  starting transfers between devices  13.3 us (9%)
  other arithmetic  10.4 us (7%)
  local copies, waits for them, and re-layouts  6 us (4%)
    pallas_call x1, Pallas kernels, cells(): pl.pallas_call(functools.partial(cell_kernel, n_tm, n_sp), grid_spec=grid...  48.1 us
    all_to_all x1, blocking collectives, body(): lax.all_to_all(solved, both, split_axis=0, concat_axis=0, tiled=True)  34.6 us
    all_to_all x1, waiting for transfers between devices, body(): lax.all_to_all(payload, both, split_axis=0, concat_axis=0, tiled=True)  21 us
    all_to_all x1, starting transfers between devices, body(): lax.all_to_all(payload, both, split_axis=0, concat_axis=0, tiled=True)  13.3 us
    select_n x1, other arithmetic, body(): jnp.where(next_multiplier == next_multiplier, next_multiplier, 0.0)  8.53 us
    dot_general x1, matrix products, body(): next_potential = jnp.einsum('ik,txyk->txyi', cos_z, local, precision=high)  5.03 us
    dot_general x1, matrix products, body(): local = jnp.einsum('ik,ktxz->txiz', cos_y, local, precision=high)  4.53 us
    transpose x1, local copies, waits for them, and re-layouts, body(): payload = partial.transpose(2, 0, 1, 3)  4.26 us
  transfers between devices with their start and end apart: 1, of which 1 were waited for; matrix products, arithmetic and copies ran while one was open for 6% of the time, Pallas kernels for 0%

profile of v5, /device:TPU:1, one launch (start us, length us, event | category | flops | bytes accessed | tf_op | source)
XLA Modules:
  0.0 155.2 jit_solution(12068394115410141137)
XLA Ops:
  0.7 0.7 pad_add_fusion.idx_ref
  1.3 0.9 cosine_multiply_fusion.cy.cz
  2.3 48.1 %shard_map.59 = (f32[4,8,4,128,128]{4,3,2,1,0:T(8,128)}, f32[8,4,128,128]{3,2,1,0:T(8,128)}) custom-call(s32[2]{0:T(128)} %pad_add_fusion.idx_ref, f32[8,4,128,128]{3,2,1,0:T(8,128)} %p_any.1, f32[8,4,128,128]{3,2,1,0:T(8,128)} %p_any.1, f32[8,4,128,128]{3,2,1,0:T(8,128)} %p_any.1, f32[4,8,4,128,128]{4,3,2,1,0:T(8,128)} %m.1, f32[4,128,128]{2,1,0:T(8,128)} %sd.1, ...), custom_call_target="tpu_custom_call" | custom-call | flops 104857600 | bytes 25165824 | tf_op jit(solution)/shard_map/pallas_call | solution.py:276
  50.4 4.3 %copy.19 = f32[128,8,4,128]{3,2,1,0:T(4,128)} copy(f32[128,8,4,128]{3,0,2,1:T(8,128)} %bitcast.64) | data formatting | bytes 4194304 | tf_op jit(solution)/shard_map/transpose | solution.py:307
  54.6 13.3 %all-to-all-start = ((f32[128,8,4,128]{3,2,1,0:T(4,128)}), f32[128,8,4,128]{3,2,1,0:T(4,128)S(1)}, u32[]{:S(2)}, u32[]{:S(2)}) async-start(f32[128,8,4,128]{3,2,1,0:T(4,128)} %copy.19), calls=%async_computation | async-start | bytes 4194304 | tf_op jit(solution)/shard_map/all_to_all | solution.py:309
  68.2 0.1 add_add_fusion
  68.3 8.5 %compare_select_fusion = f32[4,8,4,128,128]{4,3,2,1,0:T(8,128)} fusion(f32[4,8,4,128,128]{4,3,2,1,0:T(8,128)} %get-tuple-element.7), kind=kLoop, calls=%fused_computation | loop fusion | flops 4194304 | bytes 16777216 | tf_op jit(solution)/shard_map/jit(_where)/select_n | solution.py:310
  76.8 21.0 %all-to-all-done = f32[128,8,4,128]{3,2,1,0:T(4,128)S(1)} async-done(((f32[128,8,4,128]{3,2,1,0:T(4,128)}), f32[128,8,4,128]{3,2,1,0:T(4,128)S(1)}, u32[]{:S(2)}, u32[]{:S(2)}) %all-to-all-start) | async-done | bytes 2097184 | tf_op jit(solution)/shard_map/all_to_all | solution.py:309
  97.8 2.1 %fusion.14 = f32[64,16,4,128]{3,0,2,1:T(8,128)S(1)} fusion(f32[8,16,8,4,128]{4,3,2,1,0:T(4,128)S(1)} %bitcast.62, f32[8,8]{1,0:T(8,128)S(1)} %fusion.71, f32[64]{0:T(128)S(1)} %get-tuple-element.13, f32[64]{0:T(128)S(1)} %get-tuple-element.12), kind=kOutput, calls=%fused_computation.16 | convolution fusion | flops 402665472 | bytes 4195072 | tf_op jit(solution)/shard_map/kat,abytxz->kbxyz/dot_general | solution.py:315
  99.9 3.6 %fusion = f32[64,64,128]{2,1,0:T(8,128)S(1)} fusion(f32[64,16,4,128]{3,0,2,1:T(8,128)S(1)} %fusion.14, f32[128]{0:T(128)S(1)} %multiply_multiply_fusion, f32[64,64]{1,0:T(8,128)S(1)} %add_add_fusion, f32[16,4]{0,1:T(4,128)S(1)} %fusion.76, f32[64]{0:T(128)S(1)} %get-tuple-element.13, f32[64]{0:T(128)S(1)} %get-tuple-element.12), kind=kOutput, calls=%fused_computation.2 | convolution fusion | flops 404762624 | bytes 4211968 | tf_op jit(solution)/shard_map/jbx,kbxyz->kjyz/dot_general | solution.py:316
  103.5 3.2 %fusion.17 = f32[8,8,64,128,1]{3,1,2,0,4:T(8,128)S(1)} fusion(f32[64,64,128]{2,1,0:T(8,128)S(1)} %fusion, f32[64]{0:T(128)S(1)} %iota_add_fusion.1, f32[8,8]{1,0:T(8,128)S(1)} %get-tuple-element.15, f32[8,8]{1,0:T(8,128)S(1)} %get-tuple-element.14), kind=kOutput, calls=%fused_computation.17 | convolution fusion | flops 402665472 | bytes 4195072 | tf_op jit(solution)/shard_map/atk,kjyz->atjyz/dot_general | solution.py:327
  106.7 2.6 %fusion.20 = f32[8,16,1,8,4,128]{5,1,4,3,0,2:T(8,128)S(1)} fusion(f32[8,8,64,128,1]{3,1,2,0,4:T(8,128)S(1)} %fusion.17, f32[64]{0:T(128)S(1)} %iota_add_fusion.1, f32[16,4]{0,1:T(4,128)S(1)} %get-tuple-element.17, f32[16,4]{0,1:T(4,128)S(1)} %get-tuple-element.16), kind=kOutput, calls=%fused_computation.18 | convolution fusion | flops 402665472 | bytes 4195072 | tf_op jit(solution)/shard_map/bxj,atjyz->abytxz/dot_general | solution.py:328
  109.3 1.2 copy.24
  110.5 0.5 copy.25
  111.0 34.6 %all_to_all.10 = f32[128,8,4,128]{3,2,1,0:T(4,128)S(1)} all-to-all(f32[128,8,4,128]{3,2,1,0:T(4,128)S(1)} %copy.25), channel_id=1, replica_groups=mesh['tm'=8,'space'=16] {'tm','space'}, dimensions={0} | all-to-all | bytes 4194304 | tf_op jit(solution)/shard_map/all_to_all | solution.py:330
  145.6 4.5 %fusion.7 = f32[8,4,128,128]{3,2,1,0:T(8,128)S(1)} fusion(f32[128,8,4,128]{3,2,1,0:T(4,128)S(1)} %all_to_all.10, f32[128]{0:T(128)S(1)} %get-tuple-element.11, f32[128]{0:T(128)S(1)} %iota_multiply_fusion.1, f32[128]{0:T(128)S(1)} %get-tuple-element.10), kind=kOutput, calls=%fused_computation.9 | convolution fusion | flops 805355520 | bytes 4195840 | tf_op jit(solution)/shard_map/ik,ktxz->txiz/dot_general | solution.py:331
  150.2 5.0 %fusion.1 = f32[8,4,128,128]{3,2,1,0:T(8,128)} fusion(f32[8,4,128,128]{3,2,1,0:T(8,128)S(1)} %fusion.7, f32[128]{0:T(128)S(1)} %get-tuple-element.11, f32[128]{0:T(128)S(1)} %iota_multiply_fusion.1, f32[128]{0:T(128)S(1)} %get-tuple-element.10), kind=kOutput, calls=%fused_computation.3 | convolution fusion | flops 805355520 | bytes 4195840 | tf_op jit(solution)/shard_map/ik,txyk->txyi/dot_general | solution.py:332
  (10 shorter events, 0.2 us)
Async XLA Ops:
  54.6 43.1 %all-to-all-start = ((f32[128,8,4,128]{3,2,1,0:T(4,128)}), f32[128,8,4,128]{3,2,1,0:T(4,128)S(1)}, u32[]{:S(2)}, u32[]{:S(2)}) async-start(f32[128,8,4,128]{3,2,1,0:T(4,128)} %copy.19), calls=%async_computation | async-start | bytes 4194304 | tf_op jit(solution)/shard_map/all_to_all | solution.py:309

commit v6 on v4

--- a/solution.py
+++ b/solution.py
@@ -69,11 +69,16 @@
     return jnp.concatenate([new_lead[None], new_side], axis=0)
 
 
+def visit(step, steps_t):
+    return jnp.where(step < 2, step, jnp.where(step == 2, steps_t - 1, step - 1))
+
+
 def cell_kernel(n_tm, n_sp, idx_ref, pc, pn, p_any, m, sd, fd, nm_out, pay_out,
-                ft_carry, ahead_t, ahead_x, send_x, send_t, behind_t, behind_x,
+                ft_store, ahead_t, ahead_x, send_x, send_t, behind_t, behind_x,
                 at_sems, ax_sems, bt_sems, bx_sems):
-    t = pl.program_id(0)
+    s = pl.program_id(0)
     steps_t = pl.num_programs(0)
+    t = visit(s, steps_t)
     rows_x, width_y, width_z = pc.shape[1], pc.shape[2], pc.shape[3]
     tm = lax.axis_index("tm")
     sp = lax.axis_index("space")
@@ -95,9 +100,9 @@
             p_any.at[row, 0], ahead_x.at[row], ax_sems.at[0, row], ax_sems.at[1, row],
             device_id=(tm, sp - 1), device_id_type=mesh_id)
 
-    def behind_t_copy():
+    def behind_t_copy(x):
         return pltpu.make_async_remote_copy(
-            send_t, behind_t, bt_sems.at[0], bt_sems.at[1],
+            send_t.at[x], behind_t.at[x], bt_sems.at[0, x], bt_sems.at[1, x],
             device_id=(tm + 1, sp), device_id_type=mesh_id)
 
     def behind_x_copy(row):
@@ -105,7 +110,7 @@
             send_x.at[row], behind_x.at[row], bx_sems.at[0, row], bx_sems.at[1, row],
             device_id=(tm, sp + 1), device_id_type=mesh_id)
 
-    @pl.when(t == 0)
+    @pl.when(s == 0)
     def _():
         barrier = pltpu.get_barrier_semaphore()
         for cond, dev in ((has_earlier_t, (tm - 1, sp)), (has_later_t, (tm + 1, sp)),
@@ -123,7 +128,8 @@
 
         @pl.when(has_earlier_x)
         def _():
-            for row in range(steps_t):
+            rows = ahead_x.shape[0]
+            for row in [0, 1, rows - 1] + list(range(2, rows - 1)):
                 ahead_x_copy(row).start()
 
     row = lax.broadcasted_iota(jnp.int32, (width_y, width_z), 0)
@@ -177,10 +183,18 @@
         flow_z = jnp.where(first_col, 0.0, pltpu.roll(flux[3], 1, 1)) - jnp.where(last_col, 0.0, flux[3])
         rest = PROX * p - (flow_y + flow_z)
         rest = rest + jnp.where(t_glob == 0, sd[x], 0.0) - jnp.where(last_t, fd[x], 0.0)
-        ft_prev = jnp.where(t == 0, 0.0, ft_carry[x])
+        has_prev = jnp.logical_and(t > 0, t < steps_t - 1)
+        ft_prev = lax.cond(has_prev, lambda: ft_store[jnp.maximum(t - 1, 0), x], lambda: jnp.zeros_like(p))
         div_t = ft_prev - jnp.where(last_t, 0.0, flux[0])
-        ft_carry[x] = flux[0]
-        send_t[x] = flux[0]
+        ft_store[t, x] = flux[0]
+
+        @pl.when(t == steps_t - 1)
+        def _():
+            send_t[x] = flux[0]
+
+            @pl.when(has_later_t)
+            def _():
+                behind_t_copy(x).start()
         if x < rows_x - 1:
             fx_cur = flux[1]
         else:
@@ -194,17 +208,16 @@
         fx_prev = flux[1]
         pay_out[t, x] = rest - div_t - div_x
 
-    @pl.when(t == steps_t - 1)
+    @pl.when(s == steps_t - 1)
     def _():
-        @pl.when(has_later_t)
-        def _():
-            behind_t_copy().start()
+        for x in range(rows_x):
+            pay_out[steps_t - 1, x] = pay_out[steps_t - 1, x] - ft_store[steps_t - 2, x]
 
         @pl.when(has_earlier_t)
         def _():
             ahead_t_copy().wait_send()
-            behind_t_copy().wait_recv()
             for x in range(rows_x):
+                behind_t_copy(x).wait_recv()
                 pay_out[0, x] = pay_out[0, x] - behind_t[x]
 
         @pl.when(has_earlier_x)
@@ -221,7 +234,8 @@
 
         @pl.when(has_later_t)
         def _():
-            behind_t_copy().wait_send()
+            for x in range(rows_x):
+                behind_t_copy(x).wait_send()
 
 
 def cells(potential, multiplier, start_density, final_density, n_tm, n_sp):
@@ -234,19 +248,19 @@
         num_scalar_prefetch=1,
         grid=(steps_t,),
         in_specs=[
-            pl.BlockSpec(slab, lambda t, s: (t, 0, 0, 0)),
-            pl.BlockSpec(slab, lambda t, s: (jnp.minimum(t + 1, steps_t - 1), 0, 0, 0)),
+            pl.BlockSpec(slab, lambda i, s: (visit(i, steps_t), 0, 0, 0)),
+            pl.BlockSpec(slab, lambda i, s: (jnp.minimum(visit(i, steps_t) + 1, steps_t - 1), 0, 0, 0)),
             pl.BlockSpec(memory_space=pl.ANY),
-            pl.BlockSpec((4, 1, rows_x, width_y, width_z), lambda t, s: (0, t, 0, 0, 0)),
+            pl.BlockSpec((4, 1, rows_x, width_y, width_z), lambda i, s: (0, visit(i, steps_t), 0, 0, 0)),
             pl.BlockSpec(plane, lambda t, s: (0, 0, 0)),
             pl.BlockSpec(plane, lambda t, s: (0, 0, 0)),
         ],
         out_specs=[
-            pl.BlockSpec((4, 1, rows_x, width_y, width_z), lambda t, s: (0, t, 0, 0, 0)),
+            pl.BlockSpec((4, 1, rows_x, width_y, width_z), lambda i, s: (0, visit(i, steps_t), 0, 0, 0)),
             pl.BlockSpec(potential.shape, lambda t, s: (0, 0, 0, 0)),
         ],
         scratch_shapes=[
-            pltpu.VMEM(plane, f32),
+            pltpu.VMEM((steps_t,) + plane, f32),
             pltpu.VMEM(plane, f32),
             pltpu.VMEM((steps_t, width_y, width_z), f32),
             pltpu.VMEM((steps_t, width_y, width_z), f32),
@@ -255,7 +269,7 @@
             pltpu.VMEM((steps_t, width_y, width_z), f32),
             pltpu.SemaphoreType.DMA((2,)),
             pltpu.SemaphoreType.DMA((2, steps_t)),
-            pltpu.SemaphoreType.DMA((2,)),
+            pltpu.SemaphoreType.DMA((2, rows_x)),
             pltpu.SemaphoreType.DMA((2, steps_t)),
         ],
     )

time: 143 us -> 142 us (level)
  no operation moved by 1% of the time
where the time goes in v6:
time: 142 us
  blocking collectives  34.6 us (24%)
  Pallas kernels  33.6 us (24%)
  matrix products  26.9 us (19%)
  waiting for transfers between devices  21 us (15%)
  starting transfers between devices  11.1 us (8%)
  other arithmetic  9.36 us (7%)
  local copies, waits for them, and re-layouts  4.41 us (3%)
    all_to_all x1, blocking collectives, body(): lax.all_to_all(solved, both, split_axis=0, concat_axis=0, tiled=True)  34.6 us
    pallas_call x1, Pallas kernels, cells(): pl.pallas_call(functools.partial(cell_kernel, n_tm, n_sp), grid_spec=grid...  33.6 us
    all_to_all x1, waiting for transfers between devices, body(): lax.all_to_all(payload, both, split_axis=0, concat_axis=0, tiled=True)  21 us
    all_to_all x1, starting transfers between devices, body(): lax.all_to_all(payload, both, split_axis=0, concat_axis=0, tiled=True)  11.1 us
    select_n x1, other arithmetic, body(): jnp.where(next_multiplier == next_multiplier, next_multiplier, 0.0)  8.53 us
    dot_general x1, matrix products, body(): next_potential = jnp.einsum('ik,txyk->txyi', cos_z, local, precision=high)  5.03 us
    dot_general x1, matrix products, body(): local = jnp.einsum('ik,ktxz->txiz', cos_y, local, precision=high)  4.53 us
    dot_general x1, matrix products, body(): payload = jnp.einsum('txyi,ki->txyk', partial, cos_z, precision=high)  3.73 us
  transfers between devices with their start and end apart: 1, of which 1 were waited for; matrix products, arithmetic and copies ran while one was open for 6% of the time, Pallas kernels for 0%

profile of v6, /device:TPU:1, one launch (start us, length us, event | category | flops | bytes accessed | tf_op | source)
XLA Modules:
  0.0 141.9 jit_solution(7105413768702444198)
XLA Ops:
  0.7 0.6 pad_add_fusion.idx_ref
  1.2 33.6 %shard_map.59 = (f32[4,8,4,128,128]{4,3,2,1,0:T(8,128)}, f32[8,4,128,128]{3,2,1,0:T(8,128)}) custom-call(s32[2]{0:T(128)} %pad_add_fusion.idx_ref, f32[8,4,128,128]{3,2,1,0:T(8,128)} %p_any.1, f32[8,4,128,128]{3,2,1,0:T(8,128)} %p_any.1, f32[8,4,128,128]{3,2,1,0:T(8,128)} %p_any.1, f32[4,8,4,128,128]{4,3,2,1,0:T(8,128)} %m.1, f32[4,128,128]{2,1,0:T(8,128)} %sd.1, ...), custom_call_target="tpu_custom_call" | custom-call | flops 104857600 | bytes 25165824 | tf_op jit(solution)/shard_map/pallas_call | solution.py:277
  34.9 3.7 %fusion.29 = f32[8,4,128,128]{3,2,1,0:T(8,128)S(1)} fusion(f32[8,4,128,128]{3,2,1,0:T(8,128)} %get-tuple-element.6, f32[128]{0:T(128)S(1)} %get-tuple-element.11, f32[128]{0:T(128)S(1)} %iota_multiply_fusion.1, f32[128]{0:T(128)S(1)} %get-tuple-element.10), kind=kOutput, calls=%fused_computation.23 | convolution fusion | flops 805355520 | bytes 4195840 | tf_op jit(solution)/shard_map/txyi,ki->txyk/dot_general | solution.py:307
  38.6 2.2 %fusion.27 = f32[128,8,4,128]{3,0,2,1:T(8,128)S(1)} fusion(f32[8,4,128,128]{3,2,1,0:T(8,128)S(1)} %fusion.29, f32[128]{0:T(128)S(1)} %get-tuple-element.11, f32[128]{0:T(128)S(1)} %iota_multiply_fusion.1, f32[128]{0:T(128)S(1)} %get-tuple-element.10), kind=kOutput, calls=%fused_computation.21 | convolution fusion | flops 805355520 | bytes 4195840 | tf_op jit(solution)/shard_map/txiz,ki->ktxz/dot_general | solution.py:308
  40.8 2.7 %copy.19 = f32[128,8,4,128]{3,2,1,0:T(4,128)} copy(f32[128,8,4,128]{3,0,2,1:T(8,128)S(1)} %fusion.27) | data formatting | bytes 4194304 | tf_op jit(solution)/shard_map/txiz,ki->ktxz/dot_general | solution.py:308
  43.5 11.1 %all-to-all-start = ((f32[128,8,4,128]{3,2,1,0:T(4,128)}), f32[128,8,4,128]{3,2,1,0:T(4,128)S(1)}, u32[]{:S(2)}, u32[]{:S(2)}) async-start(f32[128,8,4,128]{3,2,1,0:T(4,128)} %copy.19), calls=%async_computation | async-start | bytes 4194304 | tf_op jit(solution)/shard_map/all_to_all | solution.py:310
  54.9 0.1 add_add_fusion
  55.0 8.5 %compare_select_fusion = f32[4,8,4,128,128]{4,3,2,1,0:T(8,128)} fusion(f32[4,8,4,128,128]{4,3,2,1,0:T(8,128)} %get-tuple-element.7), kind=kLoop, calls=%fused_computation | loop fusion | flops 4194304 | bytes 16777216 | tf_op jit(solution)/shard_map/jit(_where)/select_n | solution.py:311
  63.5 21.0 %all-to-all-done = f32[128,8,4,128]{3,2,1,0:T(4,128)S(1)} async-done(((f32[128,8,4,128]{3,2,1,0:T(4,128)}), f32[128,8,4,128]{3,2,1,0:T(4,128)S(1)}, u32[]{:S(2)}, u32[]{:S(2)}) %all-to-all-start) | async-done | bytes 2097184 | tf_op jit(solution)/shard_map/all_to_all | solution.py:310
  84.5 2.1 %fusion.14 = f32[64,16,4,128]{3,0,2,1:T(8,128)S(1)} fusion(f32[8,16,8,4,128]{4,3,2,1,0:T(4,128)S(1)} %bitcast.67, f32[8,8]{1,0:T(8,128)S(1)} %fusion.83, f32[64]{0:T(128)S(1)} %get-tuple-element.13, f32[64]{0:T(128)S(1)} %get-tuple-element.12), kind=kOutput, calls=%fused_computation.16 | convolution fusion | flops 402665472 | bytes 4195072 | tf_op jit(solution)/shard_map/kat,abytxz->kbxyz/dot_general | solution.py:316
  86.6 3.6 %fusion = f32[64,64,128]{2,1,0:T(8,128)S(1)} fusion(f32[64,16,4,128]{3,0,2,1:T(8,128)S(1)} %fusion.14, f32[128]{0:T(128)S(1)} %multiply_multiply_fusion, f32[64,64]{1,0:T(8,128)S(1)} %add_add_fusion, f32[16,4]{0,1:T(4,128)S(1)} %fusion.88, f32[64]{0:T(128)S(1)} %get-tuple-element.13, f32[64]{0:T(128)S(1)} %get-tuple-element.12), kind=kOutput, calls=%fused_computation.2 | convolution fusion | flops 404762624 | bytes 4211968 | tf_op jit(solution)/shard_map/jbx,kbxyz->kjyz/dot_general | solution.py:317
  90.2 3.2 %fusion.17 = f32[8,8,64,128,1]{3,1,2,0,4:T(8,128)S(1)} fusion(f32[64,64,128]{2,1,0:T(8,128)S(1)} %fusion, f32[64]{0:T(128)S(1)} %iota_add_fusion.1, f32[8,8]{1,0:T(8,128)S(1)} %get-tuple-element.15, f32[8,8]{1,0:T(8,128)S(1)} %get-tuple-element.14), kind=kOutput, calls=%fused_computation.17 | convolution fusion | flops 402665472 | bytes 4195072 | tf_op jit(solution)/shard_map/atk,kjyz->atjyz/dot_general | solution.py:328
  93.4 2.6 %fusion.20 = f32[8,16,1,8,4,128]{5,1,4,3,0,2:T(8,128)S(1)} fusion(f32[8,8,64,128,1]{3,1,2,0,4:T(8,128)S(1)} %fusion.17, f32[64]{0:T(128)S(1)} %iota_add_fusion.1, f32[16,4]{0,1:T(4,128)S(1)} %get-tuple-element.17, f32[16,4]{0,1:T(4,128)S(1)} %get-tuple-element.16), kind=kOutput, calls=%fused_computation.18 | convolution fusion | flops 402665472 | bytes 4195072 | tf_op jit(solution)/shard_map/bxj,atjyz->abytxz/dot_general | solution.py:329
  95.9 1.2 copy.24
  97.1 0.5 copy.25
  97.7 34.6 %all_to_all.10 = f32[128,8,4,128]{3,2,1,0:T(4,128)S(1)} all-to-all(f32[128,8,4,128]{3,2,1,0:T(4,128)S(1)} %copy.25), channel_id=1, replica_groups=mesh['tm'=8,'space'=16] {'tm','space'}, dimensions={0} | all-to-all | bytes 4194304 | tf_op jit(solution)/shard_map/all_to_all | solution.py:331
  132.3 4.5 %fusion.7 = f32[8,4,128,128]{3,2,1,0:T(8,128)S(1)} fusion(f32[128,8,4,128]{3,2,1,0:T(4,128)S(1)} %all_to_all.10, f32[128]{0:T(128)S(1)} %get-tuple-element.11, f32[128]{0:T(128)S(1)} %iota_multiply_fusion.1, f32[128]{0:T(128)S(1)} %get-tuple-element.10), kind=kOutput, calls=%fused_computation.9 | convolution fusion | flops 805355520 | bytes 4195840 | tf_op jit(solution)/shard_map/ik,ktxz->txiz/dot_general | solution.py:332
  136.8 5.0 %fusion.1 = f32[8,4,128,128]{3,2,1,0:T(8,128)} fusion(f32[8,4,128,128]{3,2,1,0:T(8,128)S(1)} %fusion.7, f32[128]{0:T(128)S(1)} %get-tuple-element.11, f32[128]{0:T(128)S(1)} %iota_multiply_fusion.1, f32[128]{0:T(128)S(1)} %get-tuple-element.10), kind=kOutput, calls=%fused_computation.3 | convolution fusion | flops 805355520 | bytes 4195840 | tf_op jit(solution)/shard_map/ik,txyk->txyi/dot_general | solution.py:333
  (10 shorter events, 0.2 us)
Async XLA Ops:
  43.5 41.0 %all-to-all-start = ((f32[128,8,4,128]{3,2,1,0:T(4,128)}), f32[128,8,4,128]{3,2,1,0:T(4,128)S(1)}, u32[]{:S(2)}, u32[]{:S(2)}) async-start(f32[128,8,4,128]{3,2,1,0:T(4,128)} %copy.19), calls=%async_computation | async-start | bytes 4194304 | tf_op jit(solution)/shard_map/all_to_all | solution.py:310

commit v7 on v6

--- a/solution.py
+++ b/solution.py
@@ -290,7 +290,7 @@
     )(idx, potential, potential, potential, multiplier, start_density, final_density)
 
 def body(potential, multiplier, start_density, final_density):
-    high = lax.Precision.HIGHEST
+    high = lax.Precision.HIGH
     steps_t, rows_x, width_y, width_z = potential.shape
     n_tm = lax.axis_size("tm")
     n_sp = lax.axis_size("space")

time: 142 us -> 133 us (0.937)
  matrix products: 26.9 us -> 17.6 us
    dot_general x1, matrix products: 4.53 us -> 2.73 us  [body(): local = jnp.einsum('ik,ktxz->txiz', cos_y, local, precision=high)]
    dot_general x1, matrix products: 5.03 us -> 3.32 us  [body(): next_potential = jnp.einsum('ik,txyk->txyi', cos_z, local, precision=high)]
  transfers between devices with their start and end apart: 1 -> 1, of which waited for: 1 -> 1; matrix products, arithmetic and copies ran while one was open for 6% -> 7% of each run, Pallas kernels for 0% -> 0%
where the time goes in v7:
time: 133 us
  blocking collectives  34.6 us (26%)
  Pallas kernels  33.6 us (25%)
  waiting for transfers between devices  21.1 us (16%)
  matrix products  17.6 us (13%)
  starting transfers between devices  10.9 us (8%)
  other arithmetic  9.36 us (7%)
  local copies, waits for them, and re-layouts  4.41 us (3%)
    all_to_all x1, blocking collectives, body(): lax.all_to_all(solved, both, split_axis=0, concat_axis=0, tiled=True)  34.6 us
    pallas_call x1, Pallas kernels, cells(): pl.pallas_call(functools.partial(cell_kernel, n_tm, n_sp), grid_spec=grid...  33.6 us
    all_to_all x1, waiting for transfers between devices, body(): lax.all_to_all(payload, both, split_axis=0, concat_axis=0, tiled=True)  21.1 us
    all_to_all x1, starting transfers between devices, body(): lax.all_to_all(payload, both, split_axis=0, concat_axis=0, tiled=True)  10.9 us
    select_n x1, other arithmetic, body(): jnp.where(next_multiplier == next_multiplier, next_multiplier, 0.0)  8.53 us
    dot_general x1, matrix products, body(): next_potential = jnp.einsum('ik,txyk->txyi', cos_z, local, precision=high)  3.32 us
    dot_general x1, matrix products, body(): payload = jnp.einsum('txyi,ki->txyk', partial, cos_z, precision=high)  2.87 us
    dot_general x1, matrix products, body(): local = jnp.einsum('ik,ktxz->txiz', cos_y, local, precision=high)  2.73 us
  transfers between devices with their start and end apart: 1, of which 1 were waited for; matrix products, arithmetic and copies ran while one was open for 7% of the time, Pallas kernels for 0%

profile of v7, /device:TPU:1, one launch (start us, length us, event | category | flops | bytes accessed | tf_op | source)
XLA Modules:
  0.0 132.5 jit_solution(2114404959469742609)
XLA Ops:
  0.7 0.6 pad_add_fusion.idx_ref
  1.2 33.6 %shard_map.59 = (f32[4,8,4,128,128]{4,3,2,1,0:T(8,128)}, f32[8,4,128,128]{3,2,1,0:T(8,128)}) custom-call(s32[2]{0:T(128)} %pad_add_fusion.idx_ref, f32[8,4,128,128]{3,2,1,0:T(8,128)} %p_any.1, f32[8,4,128,128]{3,2,1,0:T(8,128)} %p_any.1, f32[8,4,128,128]{3,2,1,0:T(8,128)} %p_any.1, f32[4,8,4,128,128]{4,3,2,1,0:T(8,128)} %m.1, f32[4,128,128]{2,1,0:T(8,128)} %sd.1, ...), custom_call_target="tpu_custom_call" | custom-call | flops 104857600 | bytes 25165824 | tf_op jit(solution)/shard_map/pallas_call | solution.py:277
  34.9 2.9 %fusion.29 = f32[8,4,128,128]{3,2,1,0:T(8,128)S(1)} fusion(f32[8,4,128,128]{3,2,1,0:T(8,128)} %get-tuple-element.6, f32[128]{0:T(128)S(1)} %get-tuple-element.11, f32[128]{0:T(128)S(1)} %iota_multiply_fusion.1, f32[128]{0:T(128)S(1)} %get-tuple-element.10), kind=kOutput, calls=%fused_computation.23 | convolution fusion | flops 402702336 | bytes 4195840 | tf_op jit(solution)/shard_map/txyi,ki->txyk/dot_general | solution.py:307
  37.8 1.3 fusion.27
  39.1 2.7 %copy.19 = f32[128,8,4,128]{3,2,1,0:T(4,128)} copy(f32[128,8,4,128]{3,0,2,1:T(8,128)S(1)} %fusion.27) | data formatting | bytes 4194304 | tf_op jit(solution)/shard_map/txiz,ki->ktxz/dot_general | solution.py:308
  41.7 10.9 %all-to-all-start = ((f32[128,8,4,128]{3,2,1,0:T(4,128)}), f32[128,8,4,128]{3,2,1,0:T(4,128)S(1)}, u32[]{:S(2)}, u32[]{:S(2)}) async-start(f32[128,8,4,128]{3,2,1,0:T(4,128)} %copy.19), calls=%async_computation | async-start | bytes 4194304 | tf_op jit(solution)/shard_map/all_to_all | solution.py:310
  53.0 0.1 add_add_fusion
  53.1 8.5 %compare_select_fusion = f32[4,8,4,128,128]{4,3,2,1,0:T(8,128)} fusion(f32[4,8,4,128,128]{4,3,2,1,0:T(8,128)} %get-tuple-element.7), kind=kLoop, calls=%fused_computation | loop fusion | flops 4194304 | bytes 16777216 | tf_op jit(solution)/shard_map/jit(_where)/select_n | solution.py:311
  61.6 21.1 %all-to-all-done = f32[128,8,4,128]{3,2,1,0:T(4,128)S(1)} async-done(((f32[128,8,4,128]{3,2,1,0:T(4,128)}), f32[128,8,4,128]{3,2,1,0:T(4,128)S(1)}, u32[]{:S(2)}, u32[]{:S(2)}) %all-to-all-start) | async-done | bytes 2097184 | tf_op jit(solution)/shard_map/all_to_all | solution.py:310
  82.7 1.2 fusion.14
  83.9 2.5 %fusion = f32[64,64,128]{2,1,0:T(8,128)S(1)} fusion(f32[64,16,4,128]{3,0,2,1:T(8,128)S(1)} %fusion.14, f32[128]{0:T(128)S(1)} %multiply_multiply_fusion, f32[64,64]{1,0:T(8,128)S(1)} %add_add_fusion, f32[16,4]{0,1:T(4,128)S(1)} %fusion.88, f32[64]{0:T(128)S(1)} %get-tuple-element.13, f32[64]{0:T(128)S(1)} %get-tuple-element.12), kind=kOutput, calls=%fused_computation.2 | convolution fusion | flops 203436032 | bytes 4211968 | tf_op jit(solution)/shard_map/jbx,kbxyz->kjyz/dot_general | solution.py:317
  86.5 2.3 %fusion.17 = f32[8,8,64,128,1]{3,1,2,0,4:T(8,128)S(1)} fusion(f32[64,64,128]{2,1,0:T(8,128)S(1)} %fusion, f32[64]{0:T(128)S(1)} %iota_add_fusion.1, f32[8,8]{1,0:T(8,128)S(1)} %get-tuple-element.15, f32[8,8]{1,0:T(8,128)S(1)} %get-tuple-element.14), kind=kOutput, calls=%fused_computation.17 | convolution fusion | flops 201338880 | bytes 4195072 | tf_op jit(solution)/shard_map/atk,kjyz->atjyz/dot_general | solution.py:328
  88.7 1.4 %fusion.20 = f32[8,16,1,8,4,128]{5,1,4,3,0,2:T(8,128)S(1)} fusion(f32[8,8,64,128,1]{3,1,2,0,4:T(8,128)S(1)} %fusion.17, f32[64]{0:T(128)S(1)} %iota_add_fusion.1, f32[16,4]{0,1:T(4,128)S(1)} %get-tuple-element.17, f32[16,4]{0,1:T(4,128)S(1)} %get-tuple-element.16), kind=kOutput, calls=%fused_computation.18 | convolution fusion | flops 201338880 | bytes 4195072 | tf_op jit(solution)/shard_map/bxj,atjyz->abytxz/dot_general | solution.py:329
  90.1 1.2 copy.24
  91.3 0.5 copy.25
  91.9 34.6 %all_to_all.10 = f32[128,8,4,128]{3,2,1,0:T(4,128)S(1)} all-to-all(f32[128,8,4,128]{3,2,1,0:T(4,128)S(1)} %copy.25), channel_id=1, replica_groups=mesh['tm'=8,'space'=16] {'tm','space'}, dimensions={0} | all-to-all | bytes 4194304 | tf_op jit(solution)/shard_map/all_to_all | solution.py:331
  126.5 2.7 %fusion.7 = f32[8,4,128,128]{3,2,1,0:T(8,128)S(1)} fusion(f32[128,8,4,128]{3,2,1,0:T(4,128)S(1)} %all_to_all.10, f32[128]{0:T(128)S(1)} %get-tuple-element.11, f32[128]{0:T(128)S(1)} %iota_multiply_fusion.1, f32[128]{0:T(128)S(1)} %get-tuple-element.10), kind=kOutput, calls=%fused_computation.9 | convolution fusion | flops 402702336 | bytes 4195840 | tf_op jit(solution)/shard_map/ik,ktxz->txiz/dot_general | solution.py:332
  129.2 3.3 %fusion.1 = f32[8,4,128,128]{3,2,1,0:T(8,128)} fusion(f32[8,4,128,128]{3,2,1,0:T(8,128)S(1)} %fusion.7, f32[128]{0:T(128)S(1)} %get-tuple-element.11, f32[128]{0:T(128)S(1)} %iota_multiply_fusion.1, f32[128]{0:T(128)S(1)} %get-tuple-element.10), kind=kOutput, calls=%fused_computation.3 | convolution fusion | flops 402702336 | bytes 4195840 | tf_op jit(solution)/shard_map/ik,txyk->txyi/dot_general | solution.py:333
  (10 shorter events, 0.2 us)
Async XLA Ops:
  41.7 41.0 %all-to-all-start = ((f32[128,8,4,128]{3,2,1,0:T(4,128)}), f32[128,8,4,128]{3,2,1,0:T(4,128)S(1)}, u32[]{:S(2)}, u32[]{:S(2)}) async-start(f32[128,8,4,128]{3,2,1,0:T(4,128)} %copy.19), calls=%async_computation | async-start | bytes 4194304 | tf_op jit(solution)/shard_map/all_to_all | solution.py:310

commit v8 on v7

--- a/solution.py
+++ b/solution.py
@@ -70,7 +70,7 @@
 
 
 def visit(step, steps_t):
-    return jnp.where(step < 2, step, jnp.where(step == 2, steps_t - 1, step - 1))
+    return jnp.where(step < 3, step, jnp.where(step == 3, steps_t - 1, step - 1))
 
 
 def cell_kernel(n_tm, n_sp, idx_ref, pc, pn, p_any, m, sd, fd, nm_out, pay_out,
@@ -90,9 +90,9 @@
     has_earlier_x = sp > 0
     mesh_id = pl.DeviceIdType.MESH
 
-    def ahead_t_copy():
+    def ahead_t_copy(x):
         return pltpu.make_async_remote_copy(
-            p_any.at[0], ahead_t, at_sems.at[0], at_sems.at[1],
+            p_any.at[0, x], ahead_t.at[x], at_sems.at[0, x], at_sems.at[1, x],
             device_id=(tm - 1, sp), device_id_type=mesh_id)
 
     def ahead_x_copy(row):
@@ -124,12 +124,13 @@
 
         @pl.when(has_earlier_t)
         def _():
-            ahead_t_copy().start()
+            for x in range(rows_x):
+                ahead_t_copy(x).start()
 
         @pl.when(has_earlier_x)
         def _():
             rows = ahead_x.shape[0]
-            for row in [0, 1, rows - 1] + list(range(2, rows - 1)):
+            for row in [0, 1, 2, rows - 1] + list(range(3, rows - 1)):
                 ahead_x_copy(row).start()
 
     row = lax.broadcasted_iota(jnp.int32, (width_y, width_z), 0)
@@ -141,10 +142,9 @@
     fx_prev = None
     for x in range(rows_x):
         p = pc[0, x]
-        if x == 0:
-            @pl.when(jnp.logical_and(t == steps_t - 1, has_later_t))
-            def _():
-                ahead_t_copy().wait_recv()
+        @pl.when(jnp.logical_and(t == steps_t - 1, has_later_t))
+        def _():
+            ahead_t_copy(x).wait_recv()
         nxt = lax.cond(t == steps_t - 1, lambda: ahead_t[x], lambda: pn[0, x])
         grad_t = jnp.where(last_t, 0.0, nxt - p)
         if x < rows_x - 1:
@@ -215,7 +215,8 @@
 
         @pl.when(has_earlier_t)
         def _():
-            ahead_t_copy().wait_send()
+            for x in range(rows_x):
+                ahead_t_copy(x).wait_send()
             for x in range(rows_x):
                 behind_t_copy(x).wait_recv()
                 pay_out[0, x] = pay_out[0, x] - behind_t[x]
@@ -267,7 +268,7 @@
             pltpu.VMEM(plane, f32),
             pltpu.VMEM(plane, f32),
             pltpu.VMEM((steps_t, width_y, width_z), f32),
-            pltpu.SemaphoreType.DMA((2,)),
+            pltpu.SemaphoreType.DMA((2, rows_x)),
             pltpu.SemaphoreType.DMA((2, steps_t)),
             pltpu.SemaphoreType.DMA((2, rows_x)),
             pltpu.SemaphoreType.DMA((2, steps_t)),

time: 133 us -> 135 us (1.015)
  starting transfers between devices: 10.9 us -> 12.8 us
    all_to_all x1, starting transfers between devices: 10.9 us -> 12.8 us  [body(): lax.all_to_all(payload, both, split_axis=0, concat_axis=0, tiled=True)]
where the time goes in v8:
time: 135 us
  blocking collectives  34.6 us (26%)
  Pallas kernels  33.8 us (25%)
  waiting for transfers between devices  21.1 us (16%)
  matrix products  17.6 us (13%)
  starting transfers between devices  12.8 us (9%)
  other arithmetic  9.36 us (7%)
  local copies, waits for them, and re-layouts  4.41 us (3%)
    all_to_all x1, blocking collectives, body(): lax.all_to_all(solved, both, split_axis=0, concat_axis=0, tiled=True)  34.6 us
    pallas_call x1, Pallas kernels, cells(): pl.pallas_call(functools.partial(cell_kernel, n_tm, n_sp), grid_spec=grid...  33.8 us
    all_to_all x1, waiting for transfers between devices, body(): lax.all_to_all(payload, both, split_axis=0, concat_axis=0, tiled=True)  21.1 us
    all_to_all x1, starting transfers between devices, body(): lax.all_to_all(payload, both, split_axis=0, concat_axis=0, tiled=True)  12.8 us
    select_n x1, other arithmetic, body(): jnp.where(next_multiplier == next_multiplier, next_multiplier, 0.0)  8.53 us
    dot_general x1, matrix products, body(): next_potential = jnp.einsum('ik,txyk->txyi', cos_z, local, precision=high)  3.32 us
    dot_general x1, matrix products, body(): payload = jnp.einsum('txyi,ki->txyk', partial, cos_z, precision=high)  2.87 us
    dot_general x1, matrix products, body(): local = jnp.einsum('ik,ktxz->txiz', cos_y, local, precision=high)  2.73 us
  transfers between devices with their start and end apart: 1, of which 1 were waited for; matrix products, arithmetic and copies ran while one was open for 7% of the time, Pallas kernels for 0%

profile of v8, /device:TPU:1, one launch (start us, length us, event | category | flops | bytes accessed | tf_op | source)
XLA Modules:
  0.0 134.6 jit_solution(17832825667534103541)
XLA Ops:
  0.7 0.6 pad_add_fusion.idx_ref
  1.2 33.8 %shard_map.59 = (f32[4,8,4,128,128]{4,3,2,1,0:T(8,128)}, f32[8,4,128,128]{3,2,1,0:T(8,128)}) custom-call(s32[2]{0:T(128)} %pad_add_fusion.idx_ref, f32[8,4,128,128]{3,2,1,0:T(8,128)} %p_any.1, f32[8,4,128,128]{3,2,1,0:T(8,128)} %p_any.1, f32[8,4,128,128]{3,2,1,0:T(8,128)} %p_any.1, f32[4,8,4,128,128]{4,3,2,1,0:T(8,128)} %m.1, f32[4,128,128]{2,1,0:T(8,128)} %sd.1, ...), custom_call_target="tpu_custom_call" | custom-call | flops 104857600 | bytes 25165824 | tf_op jit(solution)/shard_map/pallas_call | solution.py:278
  35.1 2.9 %fusion.29 = f32[8,4,128,128]{3,2,1,0:T(8,128)S(1)} fusion(f32[8,4,128,128]{3,2,1,0:T(8,128)} %get-tuple-element.6, f32[128]{0:T(128)S(1)} %get-tuple-element.11, f32[128]{0:T(128)S(1)} %iota_multiply_fusion.1, f32[128]{0:T(128)S(1)} %get-tuple-element.10), kind=kOutput, calls=%fused_computation.23 | convolution fusion | flops 402702336 | bytes 4195840 | tf_op jit(solution)/shard_map/txyi,ki->txyk/dot_general | solution.py:308
  38.0 1.3 fusion.27
  39.3 2.7 %copy.19 = f32[128,8,4,128]{3,2,1,0:T(4,128)} copy(f32[128,8,4,128]{3,0,2,1:T(8,128)S(1)} %fusion.27) | data formatting | bytes 4194304 | tf_op jit(solution)/shard_map/txiz,ki->ktxz/dot_general | solution.py:309
  42.0 12.8 %all-to-all-start = ((f32[128,8,4,128]{3,2,1,0:T(4,128)}), f32[128,8,4,128]{3,2,1,0:T(4,128)S(1)}, u32[]{:S(2)}, u32[]{:S(2)}) async-start(f32[128,8,4,128]{3,2,1,0:T(4,128)} %copy.19), calls=%async_computation | async-start | bytes 4194304 | tf_op jit(solution)/shard_map/all_to_all | solution.py:311
  55.1 0.1 add_add_fusion
  55.1 8.5 %compare_select_fusion = f32[4,8,4,128,128]{4,3,2,1,0:T(8,128)} fusion(f32[4,8,4,128,128]{4,3,2,1,0:T(8,128)} %get-tuple-element.7), kind=kLoop, calls=%fused_computation | loop fusion | flops 4194304 | bytes 16777216 | tf_op jit(solution)/shard_map/jit(_where)/select_n | solution.py:312
  63.7 21.1 %all-to-all-done = f32[128,8,4,128]{3,2,1,0:T(4,128)S(1)} async-done(((f32[128,8,4,128]{3,2,1,0:T(4,128)}), f32[128,8,4,128]{3,2,1,0:T(4,128)S(1)}, u32[]{:S(2)}, u32[]{:S(2)}) %all-to-all-start) | async-done | bytes 2097184 | tf_op jit(solution)/shard_map/all_to_all | solution.py:311
  84.8 1.2 fusion.14
  86.0 2.5 %fusion = f32[64,64,128]{2,1,0:T(8,128)S(1)} fusion(f32[64,16,4,128]{3,0,2,1:T(8,128)S(1)} %fusion.14, f32[128]{0:T(128)S(1)} %multiply_multiply_fusion, f32[64,64]{1,0:T(8,128)S(1)} %add_add_fusion, f32[16,4]{0,1:T(4,128)S(1)} %fusion.88, f32[64]{0:T(128)S(1)} %get-tuple-element.13, f32[64]{0:T(128)S(1)} %get-tuple-element.12), kind=kOutput, calls=%fused_computation.2 | convolution fusion | flops 203436032 | bytes 4211968 | tf_op jit(solution)/shard_map/jbx,kbxyz->kjyz/dot_general | solution.py:318
  88.5 2.3 %fusion.17 = f32[8,8,64,128,1]{3,1,2,0,4:T(8,128)S(1)} fusion(f32[64,64,128]{2,1,0:T(8,128)S(1)} %fusion, f32[64]{0:T(128)S(1)} %iota_add_fusion.1, f32[8,8]{1,0:T(8,128)S(1)} %get-tuple-element.15, f32[8,8]{1,0:T(8,128)S(1)} %get-tuple-element.14), kind=kOutput, calls=%fused_computation.17 | convolution fusion | flops 201338880 | bytes 4195072 | tf_op jit(solution)/shard_map/atk,kjyz->atjyz/dot_general | solution.py:329
  90.8 1.4 %fusion.20 = f32[8,16,1,8,4,128]{5,1,4,3,0,2:T(8,128)S(1)} fusion(f32[8,8,64,128,1]{3,1,2,0,4:T(8,128)S(1)} %fusion.17, f32[64]{0:T(128)S(1)} %iota_add_fusion.1, f32[16,4]{0,1:T(4,128)S(1)} %get-tuple-element.17, f32[16,4]{0,1:T(4,128)S(1)} %get-tuple-element.16), kind=kOutput, calls=%fused_computation.18 | convolution fusion | flops 201338880 | bytes 4195072 | tf_op jit(solution)/shard_map/bxj,atjyz->abytxz/dot_general | solution.py:330
  92.2 1.2 copy.24
  93.4 0.5 copy.25
  94.0 34.6 %all_to_all.10 = f32[128,8,4,128]{3,2,1,0:T(4,128)S(1)} all-to-all(f32[128,8,4,128]{3,2,1,0:T(4,128)S(1)} %copy.25), channel_id=1, replica_groups=mesh['tm'=8,'space'=16] {'tm','space'}, dimensions={0} | all-to-all | bytes 4194304 | tf_op jit(solution)/shard_map/all_to_all | solution.py:332
  128.6 2.7 %fusion.7 = f32[8,4,128,128]{3,2,1,0:T(8,128)S(1)} fusion(f32[128,8,4,128]{3,2,1,0:T(4,128)S(1)} %all_to_all.10, f32[128]{0:T(128)S(1)} %get-tuple-element.11, f32[128]{0:T(128)S(1)} %iota_multiply_fusion.1, f32[128]{0:T(128)S(1)} %get-tuple-element.10), kind=kOutput, calls=%fused_computation.9 | convolution fusion | flops 402702336 | bytes 4195840 | tf_op jit(solution)/shard_map/ik,ktxz->txiz/dot_general | solution.py:333
  131.3 3.3 %fusion.1 = f32[8,4,128,128]{3,2,1,0:T(8,128)} fusion(f32[8,4,128,128]{3,2,1,0:T(8,128)S(1)} %fusion.7, f32[128]{0:T(128)S(1)} %get-tuple-element.11, f32[128]{0:T(128)S(1)} %iota_multiply_fusion.1, f32[128]{0:T(128)S(1)} %get-tuple-element.10), kind=kOutput, calls=%fused_computation.3 | convolution fusion | flops 402702336 | bytes 4195840 | tf_op jit(solution)/shard_map/ik,txyk->txyi/dot_general | solution.py:334
  (10 shorter events, 0.2 us)
Async XLA Ops:
  42.0 42.8 %all-to-all-start = ((f32[128,8,4,128]{3,2,1,0:T(4,128)}), f32[128,8,4,128]{3,2,1,0:T(4,128)S(1)}, u32[]{:S(2)}, u32[]{:S(2)}) async-start(f32[128,8,4,128]{3,2,1,0:T(4,128)} %copy.19), calls=%async_computation | async-start | bytes 4194304 | tf_op jit(solution)/shard_map/all_to_all | solution.py:311

commit v9 on v7

--- a/solution.py
+++ b/solution.py
@@ -138,75 +138,88 @@
     last_row = row == width_y - 1
     last_col = col == width_z - 1
     first_col = col == 0
-    fx_prev = None
-    for x in range(rows_x):
-        p = pc[0, x]
-        if x == 0:
-            @pl.when(jnp.logical_and(t == steps_t - 1, has_later_t))
+    def rows_in(order):
+        fx_done = {}
+        for x in order:
+            p = pc[0, x]
+            if x == order[0]:
+                @pl.when(jnp.logical_and(t == steps_t - 1, has_later_t))
+                def _():
+                    ahead_t_copy().wait_recv()
+            nxt = lax.cond(t == steps_t - 1, lambda: ahead_t[x], lambda: pn[0, x])
+            grad_t = jnp.where(last_t, 0.0, nxt - p)
+            if x < rows_x - 1:
+                grad_x = pc[0, x + 1] - p
+            else:
+                @pl.when(has_later_x)
+                def _():
+                    ahead_x_copy(t).wait_recv()
+                grad_x = lax.cond(has_later_x, lambda: ahead_x[t] - p, lambda: jnp.zeros_like(p))
+            grad_y = jnp.where(last_row, 0.0, pltpu.roll(p, width_y - 1, 0) - p)
+            grad_z = jnp.where(last_col, 0.0, pltpu.roll(p, width_z - 1, 1) - p)
+            grads = (grad_t, grad_x, grad_y, grad_z)
+            mults = tuple(m[c, 0, x] for c in range(4))
+            target = tuple(g + mu * (1.0 / RATE) for g, mu in zip(grads, mults))
+            lead = target[0]
+            wsq = target[1] * target[1] + target[2] * target[2] + target[3] * target[3]
+            excess = lead + 0.5 * wsq
+            shifted = lead + 1.0
+            half_again = 1.5 * wsq
+            stretch = jnp.maximum(1.0, shifted)
+            for step in range(NEWTON):
+                square = stretch * stretch
+                cube = square * stretch
+                stretch = jnp.maximum(1.0, stretch * (shifted * square + half_again) / (cube + wsq))
+            inside = excess <= 0.0
+            shrink = 1.0 / stretch
+            proj = (jnp.where(inside, lead, lead - (stretch - 1.0)),) + tuple(
+                jnp.where(inside, target[c], target[c] * shrink) for c in (1, 2, 3)
+            )
+            flux = []
+            for c in range(4):
+                nm = mults[c] + RATE * (grads[c] - proj[c])
+                nm_out[c, 0, x] = nm
+                flux.append(nm - RATE * proj[c])
+            flow_y = jnp.where(first_row, 0.0, pltpu.roll(flux[2], 1, 0)) - jnp.where(last_row, 0.0, flux[2])
+            flow_z = jnp.where(first_col, 0.0, pltpu.roll(flux[3], 1, 1)) - jnp.where(last_col, 0.0, flux[3])
+            rest = PROX * p - (flow_y + flow_z)
+            rest = rest + jnp.where(t_glob == 0, sd[x], 0.0) - jnp.where(last_t, fd[x], 0.0)
+            has_prev = jnp.logical_and(t > 0, t < steps_t - 1)
+            ft_prev = lax.cond(has_prev, lambda: ft_store[jnp.maximum(t - 1, 0), x], lambda: jnp.zeros_like(p))
+            div_t = ft_prev - jnp.where(last_t, 0.0, flux[0])
+            ft_store[t, x] = flux[0]
+
+            @pl.when(t == steps_t - 1)
             def _():
-                ahead_t_copy().wait_recv()
-        nxt = lax.cond(t == steps_t - 1, lambda: ahead_t[x], lambda: pn[0, x])
-        grad_t = jnp.where(last_t, 0.0, nxt - p)
-        if x < rows_x - 1:
-            grad_x = pc[0, x + 1] - p
-        else:
-            @pl.when(has_later_x)
-            def _():
-                ahead_x_copy(t).wait_recv()
-            grad_x = lax.cond(has_later_x, lambda: ahead_x[t] - p, lambda: jnp.zeros_like(p))
-        grad_y = jnp.where(last_row, 0.0, pltpu.roll(p, width_y - 1, 0) - p)
-        grad_z = jnp.where(last_col, 0.0, pltpu.roll(p, width_z - 1, 1) - p)
-        grads = (grad_t, grad_x, grad_y, grad_z)
-        mults = tuple(m[c, 0, x] for c in range(4))
-        target = tuple(g + mu * (1.0 / RATE) for g, mu in zip(grads, mults))
-        lead = target[0]
-        wsq = target[1] * target[1] + target[2] * target[2] + target[3] * target[3]
-        excess = lead + 0.5 * wsq
-        shifted = lead + 1.0
-        half_again = 1.5 * wsq
-        stretch = jnp.maximum(1.0, shifted)
-        for step in range(NEWTON):
-            square = stretch * stretch
-            cube = square * stretch
-            stretch = jnp.maximum(1.0, stretch * (shifted * square + half_again) / (cube + wsq))
-        inside = excess <= 0.0
-        shrink = 1.0 / stretch
-        proj = (jnp.where(inside, lead, lead - (stretch - 1.0)),) + tuple(
-            jnp.where(inside, target[c], target[c] * shrink) for c in (1, 2, 3)
-        )
-        flux = []
-        for c in range(4):
-            nm = mults[c] + RATE * (grads[c] - proj[c])
-            nm_out[c, 0, x] = nm
-            flux.append(nm - RATE * proj[c])
-        flow_y = jnp.where(first_row, 0.0, pltpu.roll(flux[2], 1, 0)) - jnp.where(last_row, 0.0, flux[2])
-        flow_z = jnp.where(first_col, 0.0, pltpu.roll(flux[3], 1, 1)) - jnp.where(last_col, 0.0, flux[3])
-        rest = PROX * p - (flow_y + flow_z)
-        rest = rest + jnp.where(t_glob == 0, sd[x], 0.0) - jnp.where(last_t, fd[x], 0.0)
-        has_prev = jnp.logical_and(t > 0, t < steps_t - 1)
-        ft_prev = lax.cond(has_prev, lambda: ft_store[jnp.maximum(t - 1, 0), x], lambda: jnp.zeros_like(p))
-        div_t = ft_prev - jnp.where(last_t, 0.0, flux[0])
-        ft_store[t, x] = flux[0]
-
-        @pl.when(t == steps_t - 1)
-        def _():
-            send_t[x] = flux[0]
-
-            @pl.when(has_later_t)
-            def _():
-                behind_t_copy(x).start()
-        if x < rows_x - 1:
-            fx_cur = flux[1]
-        else:
-            fx_cur = jnp.where(has_later_x, flux[1], 0.0)
-            send_x[t] = flux[1]
-
-            @pl.when(has_later_x)
-            def _():
-                behind_x_copy(t).start()
-        div_x = -fx_cur if fx_prev is None else fx_prev - fx_cur
-        fx_prev = flux[1]
-        pay_out[t, x] = rest - div_t - div_x
+                send_t[x] = flux[0]
+
+                @pl.when(has_later_t)
+                def _():
+                    behind_t_copy(x).start()
+            if x < rows_x - 1:
+                fx_cur = flux[1]
+            else:
+                fx_cur = jnp.where(has_later_x, flux[1], 0.0)
+                send_x[t] = flux[1]
+
+                @pl.when(has_later_x)
+                def _():
+                    behind_x_copy(t).start()
+            value = rest - div_t + fx_cur
+            if x - 1 in fx_done:
+                value = value - fx_done[x - 1]
+            pay_out[t, x] = value
+            if x + 1 in fx_done:
+                pay_out[t, x + 1] = pay_out[t, x + 1] - flux[1]
+            fx_done[x] = flux[1]
+
+    @pl.when(s == steps_t - 1)
+    def _():
+        rows_in([rows_x - 1] + list(range(rows_x - 1)))
+
+    @pl.when(s < steps_t - 1)
+    def _():
+        rows_in(list(range(rows_x)))
 
     @pl.when(s == steps_t - 1)
     def _():

time: 133 us -> 131 us (0.985)
  no operation moved by 1% of the time
where the time goes in v9:
time: 131 us
  blocking collectives  34.6 us (26%)
  Pallas kernels  32.5 us (25%)
  waiting for transfers between devices  21.1 us (16%)
  matrix products  17.6 us (13%)
  starting transfers between devices  10.7 us (8%)
  other arithmetic  9.36 us (7%)
  local copies, waits for them, and re-layouts  4.41 us (3%)
    all_to_all x1, blocking collectives, body(): lax.all_to_all(solved, both, split_axis=0, concat_axis=0, tiled=True)  34.6 us
    pallas_call x1, Pallas kernels, cells(): pl.pallas_call(functools.partial(cell_kernel, n_tm, n_sp), grid_spec=grid...  32.5 us
    all_to_all x1, waiting for transfers between devices, body(): lax.all_to_all(payload, both, split_axis=0, concat_axis=0, tiled=True)  21.1 us
    all_to_all x1, starting transfers between devices, body(): lax.all_to_all(payload, both, split_axis=0, concat_axis=0, tiled=True)  10.7 us
    select_n x1, other arithmetic, body(): jnp.where(next_multiplier == next_multiplier, next_multiplier, 0.0)  8.53 us
    dot_general x1, matrix products, body(): next_potential = jnp.einsum('ik,txyk->txyi', cos_z, local, precision=high)  3.32 us
    dot_general x1, matrix products, body(): payload = jnp.einsum('txyi,ki->txyk', partial, cos_z, precision=high)  2.87 us
    dot_general x1, matrix products, body(): local = jnp.einsum('ik,ktxz->txiz', cos_y, local, precision=high)  2.73 us
  transfers between devices with their start and end apart: 1, of which 1 were waited for; matrix products, arithmetic and copies ran while one was open for 7% of the time, Pallas kernels for 0%

profile of v9, /device:TPU:1, one launch (start us, length us, event | category | flops | bytes accessed | tf_op | source)
XLA Modules:
  0.0 131.2 jit_solution(13812066655085206787)
XLA Ops:
  0.7 0.6 pad_add_fusion.idx_ref
  1.2 32.5 %shard_map.59 = (f32[4,8,4,128,128]{4,3,2,1,0:T(8,128)}, f32[8,4,128,128]{3,2,1,0:T(8,128)}) custom-call(s32[2]{0:T(128)} %pad_add_fusion.idx_ref, f32[8,4,128,128]{3,2,1,0:T(8,128)} %p_any.1, f32[8,4,128,128]{3,2,1,0:T(8,128)} %p_any.1, f32[8,4,128,128]{3,2,1,0:T(8,128)} %p_any.1, f32[4,8,4,128,128]{4,3,2,1,0:T(8,128)} %m.1, f32[4,128,128]{2,1,0:T(8,128)} %sd.1, ...), custom_call_target="tpu_custom_call" | custom-call | flops 104857600 | bytes 25165824 | tf_op jit(solution)/shard_map/pallas_call | solution.py:290
  33.7 2.9 %fusion.29 = f32[8,4,128,128]{3,2,1,0:T(8,128)S(1)} fusion(f32[8,4,128,128]{3,2,1,0:T(8,128)} %get-tuple-element.6, f32[128]{0:T(128)S(1)} %get-tuple-element.11, f32[128]{0:T(128)S(1)} %iota_multiply_fusion.1, f32[128]{0:T(128)S(1)} %get-tuple-element.10), kind=kOutput, calls=%fused_computation.23 | convolution fusion | flops 402702336 | bytes 4195840 | tf_op jit(solution)/shard_map/txyi,ki->txyk/dot_general | solution.py:320
  36.6 1.3 fusion.27
  37.9 2.7 %copy.19 = f32[128,8,4,128]{3,2,1,0:T(4,128)} copy(f32[128,8,4,128]{3,0,2,1:T(8,128)S(1)} %fusion.27) | data formatting | bytes 4194304 | tf_op jit(solution)/shard_map/txiz,ki->ktxz/dot_general | solution.py:321
  40.6 10.7 %all-to-all-start = ((f32[128,8,4,128]{3,2,1,0:T(4,128)}), f32[128,8,4,128]{3,2,1,0:T(4,128)S(1)}, u32[]{:S(2)}, u32[]{:S(2)}) async-start(f32[128,8,4,128]{3,2,1,0:T(4,128)} %copy.19), calls=%async_computation | async-start | bytes 4194304 | tf_op jit(solution)/shard_map/all_to_all | solution.py:323
  51.6 0.1 add_add_fusion
  51.7 8.5 %compare_select_fusion = f32[4,8,4,128,128]{4,3,2,1,0:T(8,128)} fusion(f32[4,8,4,128,128]{4,3,2,1,0:T(8,128)} %get-tuple-element.7), kind=kLoop, calls=%fused_computation | loop fusion | flops 4194304 | bytes 16777216 | tf_op jit(solution)/shard_map/jit(_where)/select_n | solution.py:324
  60.2 21.1 %all-to-all-done = f32[128,8,4,128]{3,2,1,0:T(4,128)S(1)} async-done(((f32[128,8,4,128]{3,2,1,0:T(4,128)}), f32[128,8,4,128]{3,2,1,0:T(4,128)S(1)}, u32[]{:S(2)}, u32[]{:S(2)}) %all-to-all-start) | async-done | bytes 2097184 | tf_op jit(solution)/shard_map/all_to_all | solution.py:323
  81.4 1.2 fusion.14
  82.6 2.5 %fusion = f32[64,64,128]{2,1,0:T(8,128)S(1)} fusion(f32[64,16,4,128]{3,0,2,1:T(8,128)S(1)} %fusion.14, f32[128]{0:T(128)S(1)} %multiply_multiply_fusion, f32[64,64]{1,0:T(8,128)S(1)} %add_add_fusion, f32[16,4]{0,1:T(4,128)S(1)} %fusion.88, f32[64]{0:T(128)S(1)} %get-tuple-element.13, f32[64]{0:T(128)S(1)} %get-tuple-element.12), kind=kOutput, calls=%fused_computation.2 | convolution fusion | flops 203436032 | bytes 4211968 | tf_op jit(solution)/shard_map/jbx,kbxyz->kjyz/dot_general | solution.py:330
  85.1 2.3 %fusion.17 = f32[8,8,64,128,1]{3,1,2,0,4:T(8,128)S(1)} fusion(f32[64,64,128]{2,1,0:T(8,128)S(1)} %fusion, f32[64]{0:T(128)S(1)} %iota_add_fusion.1, f32[8,8]{1,0:T(8,128)S(1)} %get-tuple-element.15, f32[8,8]{1,0:T(8,128)S(1)} %get-tuple-element.14), kind=kOutput, calls=%fused_computation.17 | convolution fusion | flops 201338880 | bytes 4195072 | tf_op jit(solution)/shard_map/atk,kjyz->atjyz/dot_general | solution.py:341
  87.4 1.4 %fusion.20 = f32[8,16,1,8,4,128]{5,1,4,3,0,2:T(8,128)S(1)} fusion(f32[8,8,64,128,1]{3,1,2,0,4:T(8,128)S(1)} %fusion.17, f32[64]{0:T(128)S(1)} %iota_add_fusion.1, f32[16,4]{0,1:T(4,128)S(1)} %get-tuple-element.17, f32[16,4]{0,1:T(4,128)S(1)} %get-tuple-element.16), kind=kOutput, calls=%fused_computation.18 | convolution fusion | flops 201338880 | bytes 4195072 | tf_op jit(solution)/shard_map/bxj,atjyz->abytxz/dot_general | solution.py:342
  88.7 1.2 copy.24
  89.9 0.5 copy.25
  90.5 34.6 %all_to_all.10 = f32[128,8,4,128]{3,2,1,0:T(4,128)S(1)} all-to-all(f32[128,8,4,128]{3,2,1,0:T(4,128)S(1)} %copy.25), channel_id=1, replica_groups=mesh['tm'=8,'space'=16] {'tm','space'}, dimensions={0} | all-to-all | bytes 4194304 | tf_op jit(solution)/shard_map/all_to_all | solution.py:344
  125.1 2.7 %fusion.7 = f32[8,4,128,128]{3,2,1,0:T(8,128)S(1)} fusion(f32[128,8,4,128]{3,2,1,0:T(4,128)S(1)} %all_to_all.10, f32[128]{0:T(128)S(1)} %get-tuple-element.11, f32[128]{0:T(128)S(1)} %iota_multiply_fusion.1, f32[128]{0:T(128)S(1)} %get-tuple-element.10), kind=kOutput, calls=%fused_computation.9 | convolution fusion | flops 402702336 | bytes 4195840 | tf_op jit(solution)/shard_map/ik,ktxz->txiz/dot_general | solution.py:345
  127.8 3.3 %fusion.1 = f32[8,4,128,128]{3,2,1,0:T(8,128)} fusion(f32[8,4,128,128]{3,2,1,0:T(8,128)S(1)} %fusion.7, f32[128]{0:T(128)S(1)} %get-tuple-element.11, f32[128]{0:T(128)S(1)} %iota_multiply_fusion.1, f32[128]{0:T(128)S(1)} %get-tuple-element.10), kind=kOutput, calls=%fused_computation.3 | convolution fusion | flops 402702336 | bytes 4195840 | tf_op jit(solution)/shard_map/ik,txyk->txyi/dot_general | solution.py:346
  (10 shorter events, 0.2 us)
Async XLA Ops:
  40.6 40.8 %all-to-all-start = ((f32[128,8,4,128]{3,2,1,0:T(4,128)}), f32[128,8,4,128]{3,2,1,0:T(4,128)S(1)}, u32[]{:S(2)}, u32[]{:S(2)}) async-start(f32[128,8,4,128]{3,2,1,0:T(4,128)} %copy.19), calls=%async_computation | async-start | bytes 4194304 | tf_op jit(solution)/shard_map/all_to_all | solution.py:323

commit v10 on v9

--- a/solution.py
+++ b/solution.py
@@ -70,7 +70,7 @@
 
 
 def visit(step, steps_t):
-    return jnp.where(step < 2, step, jnp.where(step == 2, steps_t - 1, step - 1))
+    return jnp.where(step < 1, step, jnp.where(step == 1, steps_t - 1, step - 1))
 
 
 def cell_kernel(n_tm, n_sp, idx_ref, pc, pn, p_any, m, sd, fd, nm_out, pay_out,
@@ -129,7 +129,7 @@
         @pl.when(has_earlier_x)
         def _():
             rows = ahead_x.shape[0]
-            for row in [0, 1, rows - 1] + list(range(2, rows - 1)):
+            for row in [0, rows - 1] + list(range(1, rows - 1)):
                 ahead_x_copy(row).start()
 
     row = lax.broadcasted_iota(jnp.int32, (width_y, width_z), 0)

time: 131 us -> 131 us (level)
  no operation moved by 1% of the time
where the time goes in v10:
time: 131 us
  blocking collectives  34.6 us (26%)
  Pallas kernels  32.5 us (25%)
  waiting for transfers between devices  21.1 us (16%)
  matrix products  17.6 us (13%)
  starting transfers between devices  10.7 us (8%)
  other arithmetic  9.36 us (7%)
  local copies, waits for them, and re-layouts  4.41 us (3%)
    all_to_all x1, blocking collectives, body(): lax.all_to_all(solved, both, split_axis=0, concat_axis=0, tiled=True)  34.6 us
    pallas_call x1, Pallas kernels, cells(): pl.pallas_call(functools.partial(cell_kernel, n_tm, n_sp), grid_spec=grid...  32.5 us
    all_to_all x1, waiting for transfers between devices, body(): lax.all_to_all(payload, both, split_axis=0, concat_axis=0, tiled=True)  21.1 us
    all_to_all x1, starting transfers between devices, body(): lax.all_to_all(payload, both, split_axis=0, concat_axis=0, tiled=True)  10.7 us
    select_n x1, other arithmetic, body(): jnp.where(next_multiplier == next_multiplier, next_multiplier, 0.0)  8.53 us
    dot_general x1, matrix products, body(): next_potential = jnp.einsum('ik,txyk->txyi', cos_z, local, precision=high)  3.32 us
    dot_general x1, matrix products, body(): payload = jnp.einsum('txyi,ki->txyk', partial, cos_z, precision=high)  2.87 us
    dot_general x1, matrix products, body(): local = jnp.einsum('ik,ktxz->txiz', cos_y, local, precision=high)  2.73 us
  transfers between devices with their start and end apart: 1, of which 1 were waited for; matrix products, arithmetic and copies ran while one was open for 7% of the time, Pallas kernels for 0%

profile of v10, /device:TPU:1, one launch (start us, length us, event | category | flops | bytes accessed | tf_op | source)
XLA Modules:
  0.0 131.2 jit_solution(11167136575066359223)
XLA Ops:
  0.7 0.6 pad_add_fusion.idx_ref
  1.2 32.5 %shard_map.59 = (f32[4,8,4,128,128]{4,3,2,1,0:T(8,128)}, f32[8,4,128,128]{3,2,1,0:T(8,128)}) custom-call(s32[2]{0:T(128)} %pad_add_fusion.idx_ref, f32[8,4,128,128]{3,2,1,0:T(8,128)} %p_any.1, f32[8,4,128,128]{3,2,1,0:T(8,128)} %p_any.1, f32[8,4,128,128]{3,2,1,0:T(8,128)} %p_any.1, f32[4,8,4,128,128]{4,3,2,1,0:T(8,128)} %m.1, f32[4,128,128]{2,1,0:T(8,128)} %sd.1, ...), custom_call_target="tpu_custom_call" | custom-call | flops 104857600 | bytes 25165824 | tf_op jit(solution)/shard_map/pallas_call | solution.py:290
  33.7 2.9 %fusion.29 = f32[8,4,128,128]{3,2,1,0:T(8,128)S(1)} fusion(f32[8,4,128,128]{3,2,1,0:T(8,128)} %get-tuple-element.6, f32[128]{0:T(128)S(1)} %get-tuple-element.11, f32[128]{0:T(128)S(1)} %iota_multiply_fusion.1, f32[128]{0:T(128)S(1)} %get-tuple-element.10), kind=kOutput, calls=%fused_computation.23 | convolution fusion | flops 402702336 | bytes 4195840 | tf_op jit(solution)/shard_map/txyi,ki->txyk/dot_general | solution.py:320
  36.6 1.3 fusion.27
  37.9 2.7 %copy.19 = f32[128,8,4,128]{3,2,1,0:T(4,128)} copy(f32[128,8,4,128]{3,0,2,1:T(8,128)S(1)} %fusion.27) | data formatting | bytes 4194304 | tf_op jit(solution)/shard_map/txiz,ki->ktxz/dot_general | solution.py:321
  40.6 10.7 %all-to-all-start = ((f32[128,8,4,128]{3,2,1,0:T(4,128)}), f32[128,8,4,128]{3,2,1,0:T(4,128)S(1)}, u32[]{:S(2)}, u32[]{:S(2)}) async-start(f32[128,8,4,128]{3,2,1,0:T(4,128)} %copy.19), calls=%async_computation | async-start | bytes 4194304 | tf_op jit(solution)/shard_map/all_to_all | solution.py:323
  51.6 0.1 add_add_fusion
  51.7 8.5 %compare_select_fusion = f32[4,8,4,128,128]{4,3,2,1,0:T(8,128)} fusion(f32[4,8,4,128,128]{4,3,2,1,0:T(8,128)} %get-tuple-element.7), kind=kLoop, calls=%fused_computation | loop fusion | flops 4194304 | bytes 16777216 | tf_op jit(solution)/shard_map/jit(_where)/select_n | solution.py:324
  60.2 21.1 %all-to-all-done = f32[128,8,4,128]{3,2,1,0:T(4,128)S(1)} async-done(((f32[128,8,4,128]{3,2,1,0:T(4,128)}), f32[128,8,4,128]{3,2,1,0:T(4,128)S(1)}, u32[]{:S(2)}, u32[]{:S(2)}) %all-to-all-start) | async-done | bytes 2097184 | tf_op jit(solution)/shard_map/all_to_all | solution.py:323
  81.4 1.2 fusion.14
  82.6 2.5 %fusion = f32[64,64,128]{2,1,0:T(8,128)S(1)} fusion(f32[64,16,4,128]{3,0,2,1:T(8,128)S(1)} %fusion.14, f32[128]{0:T(128)S(1)} %multiply_multiply_fusion, f32[64,64]{1,0:T(8,128)S(1)} %add_add_fusion, f32[16,4]{0,1:T(4,128)S(1)} %fusion.88, f32[64]{0:T(128)S(1)} %get-tuple-element.13, f32[64]{0:T(128)S(1)} %get-tuple-element.12), kind=kOutput, calls=%fused_computation.2 | convolution fusion | flops 203436032 | bytes 4211968 | tf_op jit(solution)/shard_map/jbx,kbxyz->kjyz/dot_general | solution.py:330
  85.1 2.3 %fusion.17 = f32[8,8,64,128,1]{3,1,2,0,4:T(8,128)S(1)} fusion(f32[64,64,128]{2,1,0:T(8,128)S(1)} %fusion, f32[64]{0:T(128)S(1)} %iota_add_fusion.1, f32[8,8]{1,0:T(8,128)S(1)} %get-tuple-element.15, f32[8,8]{1,0:T(8,128)S(1)} %get-tuple-element.14), kind=kOutput, calls=%fused_computation.17 | convolution fusion | flops 201338880 | bytes 4195072 | tf_op jit(solution)/shard_map/atk,kjyz->atjyz/dot_general | solution.py:341
  87.4 1.4 %fusion.20 = f32[8,16,1,8,4,128]{5,1,4,3,0,2:T(8,128)S(1)} fusion(f32[8,8,64,128,1]{3,1,2,0,4:T(8,128)S(1)} %fusion.17, f32[64]{0:T(128)S(1)} %iota_add_fusion.1, f32[16,4]{0,1:T(4,128)S(1)} %get-tuple-element.17, f32[16,4]{0,1:T(4,128)S(1)} %get-tuple-element.16), kind=kOutput, calls=%fused_computation.18 | convolution fusion | flops 201338880 | bytes 4195072 | tf_op jit(solution)/shard_map/bxj,atjyz->abytxz/dot_general | solution.py:342
  88.7 1.2 copy.24
  89.9 0.5 copy.25
  90.5 34.6 %all_to_all.10 = f32[128,8,4,128]{3,2,1,0:T(4,128)S(1)} all-to-all(f32[128,8,4,128]{3,2,1,0:T(4,128)S(1)} %copy.25), channel_id=1, replica_groups=mesh['tm'=8,'space'=16] {'tm','space'}, dimensions={0} | all-to-all | bytes 4194304 | tf_op jit(solution)/shard_map/all_to_all | solution.py:344
  125.1 2.7 %fusion.7 = f32[8,4,128,128]{3,2,1,0:T(8,128)S(1)} fusion(f32[128,8,4,128]{3,2,1,0:T(4,128)S(1)} %all_to_all.10, f32[128]{0:T(128)S(1)} %get-tuple-element.11, f32[128]{0:T(128)S(1)} %iota_multiply_fusion.1, f32[128]{0:T(128)S(1)} %get-tuple-element.10), kind=kOutput, calls=%fused_computation.9 | convolution fusion | flops 402702336 | bytes 4195840 | tf_op jit(solution)/shard_map/ik,ktxz->txiz/dot_general | solution.py:345
  127.8 3.3 %fusion.1 = f32[8,4,128,128]{3,2,1,0:T(8,128)} fusion(f32[8,4,128,128]{3,2,1,0:T(8,128)S(1)} %fusion.7, f32[128]{0:T(128)S(1)} %get-tuple-element.11, f32[128]{0:T(128)S(1)} %iota_multiply_fusion.1, f32[128]{0:T(128)S(1)} %get-tuple-element.10), kind=kOutput, calls=%fused_computation.3 | convolution fusion | flops 402702336 | bytes 4195840 | tf_op jit(solution)/shard_map/ik,txyk->txyi/dot_general | solution.py:346
  (10 shorter events, 0.2 us)
Async XLA Ops:
  40.6 40.8 %all-to-all-start = ((f32[128,8,4,128]{3,2,1,0:T(4,128)}), f32[128,8,4,128]{3,2,1,0:T(4,128)S(1)}, u32[]{:S(2)}, u32[]{:S(2)}) async-start(f32[128,8,4,128]{3,2,1,0:T(4,128)} %copy.19), calls=%async_computation | async-start | bytes 4194304 | tf_op jit(solution)/shard_map/all_to_all | solution.py:323

commit v11 on v10

--- a/solution.py
+++ b/solution.py
@@ -70,7 +70,7 @@
 
 
 def visit(step, steps_t):
-    return jnp.where(step < 1, step, jnp.where(step == 1, steps_t - 1, step - 1))
+    return jnp.where(step == 0, steps_t - 1, step - 1)
 
 
 def cell_kernel(n_tm, n_sp, idx_ref, pc, pn, p_any, m, sd, fd, nm_out, pay_out,
@@ -129,7 +129,7 @@
         @pl.when(has_earlier_x)
         def _():
             rows = ahead_x.shape[0]
-            for row in [0, rows - 1] + list(range(1, rows - 1)):
+            for row in [rows - 1] + list(range(rows - 1)):
                 ahead_x_copy(row).start()
 
     row = lax.broadcasted_iota(jnp.int32, (width_y, width_z), 0)

time: 131 us -> 132 us (level)
  no operation moved by 1% of the time
where the time goes in v11:
time: 132 us
  blocking collectives  34.6 us (26%)
  Pallas kernels  33.3 us (25%)
  waiting for transfers between devices  21.1 us (16%)
  matrix products  17.6 us (13%)
  starting transfers between devices  10.7 us (8%)
  other arithmetic  9.36 us (7%)
  local copies, waits for them, and re-layouts  4.41 us (3%)
    all_to_all x1, blocking collectives, body(): lax.all_to_all(solved, both, split_axis=0, concat_axis=0, tiled=True)  34.6 us
    pallas_call x1, Pallas kernels, cells(): pl.pallas_call(functools.partial(cell_kernel, n_tm, n_sp), grid_spec=grid...  33.3 us
    all_to_all x1, waiting for transfers between devices, body(): lax.all_to_all(payload, both, split_axis=0, concat_axis=0, tiled=True)  21.1 us
    all_to_all x1, starting transfers between devices, body(): lax.all_to_all(payload, both, split_axis=0, concat_axis=0, tiled=True)  10.7 us
    select_n x1, other arithmetic, body(): jnp.where(next_multiplier == next_multiplier, next_multiplier, 0.0)  8.53 us
    dot_general x1, matrix products, body(): next_potential = jnp.einsum('ik,txyk->txyi', cos_z, local, precision=high)  3.32 us
    dot_general x1, matrix products, body(): payload = jnp.einsum('txyi,ki->txyk', partial, cos_z, precision=high)  2.87 us
    dot_general x1, matrix products, body(): local = jnp.einsum('ik,ktxz->txiz', cos_y, local, precision=high)  2.73 us
  transfers between devices with their start and end apart: 1, of which 1 were waited for; matrix products, arithmetic and copies ran while one was open for 7% of the time, Pallas kernels for 0%

profile of v11, /device:TPU:1, one launch (start us, length us, event | category | flops | bytes accessed | tf_op | source)
XLA Modules:
  0.0 132.0 jit_solution(17965730790618399274)
XLA Ops:
  0.7 0.6 pad_add_fusion.idx_ref
  1.2 33.3 %shard_map.59 = (f32[4,8,4,128,128]{4,3,2,1,0:T(8,128)}, f32[8,4,128,128]{3,2,1,0:T(8,128)}) custom-call(s32[2]{0:T(128)} %pad_add_fusion.idx_ref, f32[8,4,128,128]{3,2,1,0:T(8,128)} %p_any.1, f32[8,4,128,128]{3,2,1,0:T(8,128)} %p_any.1, f32[8,4,128,128]{3,2,1,0:T(8,128)} %p_any.1, f32[4,8,4,128,128]{4,3,2,1,0:T(8,128)} %m.1, f32[4,128,128]{2,1,0:T(8,128)} %sd.1, ...), custom_call_target="tpu_custom_call" | custom-call | flops 104857600 | bytes 25165824 | tf_op jit(solution)/shard_map/pallas_call | solution.py:290
  34.6 2.9 %fusion.29 = f32[8,4,128,128]{3,2,1,0:T(8,128)S(1)} fusion(f32[8,4,128,128]{3,2,1,0:T(8,128)} %get-tuple-element.6, f32[128]{0:T(128)S(1)} %get-tuple-element.11, f32[128]{0:T(128)S(1)} %iota_multiply_fusion.1, f32[128]{0:T(128)S(1)} %get-tuple-element.10), kind=kOutput, calls=%fused_computation.23 | convolution fusion | flops 402702336 | bytes 4195840 | tf_op jit(solution)/shard_map/txyi,ki->txyk/dot_general | solution.py:320
  37.4 1.3 fusion.27
  38.8 2.7 %copy.19 = f32[128,8,4,128]{3,2,1,0:T(4,128)} copy(f32[128,8,4,128]{3,0,2,1:T(8,128)S(1)} %fusion.27) | data formatting | bytes 4194304 | tf_op jit(solution)/shard_map/txiz,ki->ktxz/dot_general | solution.py:321
  41.4 10.7 %all-to-all-start = ((f32[128,8,4,128]{3,2,1,0:T(4,128)}), f32[128,8,4,128]{3,2,1,0:T(4,128)S(1)}, u32[]{:S(2)}, u32[]{:S(2)}) async-start(f32[128,8,4,128]{3,2,1,0:T(4,128)} %copy.19), calls=%async_computation | async-start | bytes 4194304 | tf_op jit(solution)/shard_map/all_to_all | solution.py:323
  52.4 0.1 add_add_fusion
  52.5 8.5 %compare_select_fusion = f32[4,8,4,128,128]{4,3,2,1,0:T(8,128)} fusion(f32[4,8,4,128,128]{4,3,2,1,0:T(8,128)} %get-tuple-element.7), kind=kLoop, calls=%fused_computation | loop fusion | flops 4194304 | bytes 16777216 | tf_op jit(solution)/shard_map/jit(_where)/select_n | solution.py:324
  61.0 21.1 %all-to-all-done = f32[128,8,4,128]{3,2,1,0:T(4,128)S(1)} async-done(((f32[128,8,4,128]{3,2,1,0:T(4,128)}), f32[128,8,4,128]{3,2,1,0:T(4,128)S(1)}, u32[]{:S(2)}, u32[]{:S(2)}) %all-to-all-start) | async-done | bytes 2097184 | tf_op jit(solution)/shard_map/all_to_all | solution.py:323
  82.2 1.2 fusion.14
  83.4 2.5 %fusion = f32[64,64,128]{2,1,0:T(8,128)S(1)} fusion(f32[64,16,4,128]{3,0,2,1:T(8,128)S(1)} %fusion.14, f32[128]{0:T(128)S(1)} %multiply_multiply_fusion, f32[64,64]{1,0:T(8,128)S(1)} %add_add_fusion, f32[16,4]{0,1:T(4,128)S(1)} %fusion.88, f32[64]{0:T(128)S(1)} %get-tuple-element.13, f32[64]{0:T(128)S(1)} %get-tuple-element.12), kind=kOutput, calls=%fused_computation.2 | convolution fusion | flops 203436032 | bytes 4211968 | tf_op jit(solution)/shard_map/jbx,kbxyz->kjyz/dot_general | solution.py:330
  85.9 2.3 %fusion.17 = f32[8,8,64,128,1]{3,1,2,0,4:T(8,128)S(1)} fusion(f32[64,64,128]{2,1,0:T(8,128)S(1)} %fusion, f32[64]{0:T(128)S(1)} %iota_add_fusion.1, f32[8,8]{1,0:T(8,128)S(1)} %get-tuple-element.15, f32[8,8]{1,0:T(8,128)S(1)} %get-tuple-element.14), kind=kOutput, calls=%fused_computation.17 | convolution fusion | flops 201338880 | bytes 4195072 | tf_op jit(solution)/shard_map/atk,kjyz->atjyz/dot_general | solution.py:341
  88.2 1.4 %fusion.20 = f32[8,16,1,8,4,128]{5,1,4,3,0,2:T(8,128)S(1)} fusion(f32[8,8,64,128,1]{3,1,2,0,4:T(8,128)S(1)} %fusion.17, f32[64]{0:T(128)S(1)} %iota_add_fusion.1, f32[16,4]{0,1:T(4,128)S(1)} %get-tuple-element.17, f32[16,4]{0,1:T(4,128)S(1)} %get-tuple-element.16), kind=kOutput, calls=%fused_computation.18 | convolution fusion | flops 201338880 | bytes 4195072 | tf_op jit(solution)/shard_map/bxj,atjyz->abytxz/dot_general | solution.py:342
  89.6 1.2 copy.24
  90.8 0.5 copy.25
  91.3 34.6 %all_to_all.10 = f32[128,8,4,128]{3,2,1,0:T(4,128)S(1)} all-to-all(f32[128,8,4,128]{3,2,1,0:T(4,128)S(1)} %copy.25), channel_id=1, replica_groups=mesh['tm'=8,'space'=16] {'tm','space'}, dimensions={0} | all-to-all | bytes 4194304 | tf_op jit(solution)/shard_map/all_to_all | solution.py:344
  125.9 2.7 %fusion.7 = f32[8,4,128,128]{3,2,1,0:T(8,128)S(1)} fusion(f32[128,8,4,128]{3,2,1,0:T(4,128)S(1)} %all_to_all.10, f32[128]{0:T(128)S(1)} %get-tuple-element.11, f32[128]{0:T(128)S(1)} %iota_multiply_fusion.1, f32[128]{0:T(128)S(1)} %get-tuple-element.10), kind=kOutput, calls=%fused_computation.9 | convolution fusion | flops 402702336 | bytes 4195840 | tf_op jit(solution)/shard_map/ik,ktxz->txiz/dot_general | solution.py:345
  128.7 3.3 %fusion.1 = f32[8,4,128,128]{3,2,1,0:T(8,128)} fusion(f32[8,4,128,128]{3,2,1,0:T(8,128)S(1)} %fusion.7, f32[128]{0:T(128)S(1)} %get-tuple-element.11, f32[128]{0:T(128)S(1)} %iota_multiply_fusion.1, f32[128]{0:T(128)S(1)} %get-tuple-element.10), kind=kOutput, calls=%fused_computation.3 | convolution fusion | flops 402702336 | bytes 4195840 | tf_op jit(solution)/shard_map/ik,txyk->txyi/dot_general | solution.py:346
  (10 shorter events, 0.2 us)
Async XLA Ops:
  41.4 40.7 %all-to-all-start = ((f32[128,8,4,128]{3,2,1,0:T(4,128)}), f32[128,8,4,128]{3,2,1,0:T(4,128)S(1)}, u32[]{:S(2)}, u32[]{:S(2)}) async-start(f32[128,8,4,128]{3,2,1,0:T(4,128)} %copy.19), calls=%async_computation | async-start | bytes 4194304 | tf_op jit(solution)/shard_map/all_to_all | solution.py:323

commit v12 on v10

--- a/solution.py
+++ b/solution.py
@@ -185,7 +185,7 @@
             rest = PROX * p - (flow_y + flow_z)
             rest = rest + jnp.where(t_glob == 0, sd[x], 0.0) - jnp.where(last_t, fd[x], 0.0)
             has_prev = jnp.logical_and(t > 0, t < steps_t - 1)
-            ft_prev = lax.cond(has_prev, lambda: ft_store[jnp.maximum(t - 1, 0), x], lambda: jnp.zeros_like(p))
+            ft_prev = jnp.where(has_prev, ft_store[jnp.maximum(t - 1, 0), x], 0.0)
             div_t = ft_prev - jnp.where(last_t, 0.0, flux[0])
             ft_store[t, x] = flux[0]
 

time: 131 us -> 131 us (level)
  no operation moved by 1% of the time
where the time goes in v12:
time: 131 us
  blocking collectives  34.6 us (26%)
  Pallas kernels  32.4 us (25%)
  waiting for transfers between devices  21.1 us (16%)
  matrix products  17.6 us (13%)
  starting transfers between devices  10.7 us (8%)
  other arithmetic  9.36 us (7%)
  local copies, waits for them, and re-layouts  4.41 us (3%)
    all_to_all x1, blocking collectives, body(): lax.all_to_all(solved, both, split_axis=0, concat_axis=0, tiled=True)  34.6 us
    pallas_call x1, Pallas kernels, cells(): pl.pallas_call(functools.partial(cell_kernel, n_tm, n_sp), grid_spec=grid...  32.4 us
    all_to_all x1, waiting for transfers between devices, body(): lax.all_to_all(payload, both, split_axis=0, concat_axis=0, tiled=True)  21.1 us
    all_to_all x1, starting transfers between devices, body(): lax.all_to_all(payload, both, split_axis=0, concat_axis=0, tiled=True)  10.7 us
    select_n x1, other arithmetic, body(): jnp.where(next_multiplier == next_multiplier, next_multiplier, 0.0)  8.53 us
    dot_general x1, matrix products, body(): next_potential = jnp.einsum('ik,txyk->txyi', cos_z, local, precision=high)  3.32 us
    dot_general x1, matrix products, body(): payload = jnp.einsum('txyi,ki->txyk', partial, cos_z, precision=high)  2.87 us
    dot_general x1, matrix products, body(): local = jnp.einsum('ik,ktxz->txiz', cos_y, local, precision=high)  2.73 us
  transfers between devices with their start and end apart: 1, of which 1 were waited for; matrix products, arithmetic and copies ran while one was open for 7% of the time, Pallas kernels for 0%

profile of v12, /device:TPU:1, one launch (start us, length us, event | category | flops | bytes accessed | tf_op | source)
XLA Modules:
  0.0 131.1 jit_solution(7713891733488155452)
XLA Ops:
  0.7 0.6 pad_add_fusion.idx_ref
  1.2 32.4 %shard_map.59 = (f32[4,8,4,128,128]{4,3,2,1,0:T(8,128)}, f32[8,4,128,128]{3,2,1,0:T(8,128)}) custom-call(s32[2]{0:T(128)} %pad_add_fusion.idx_ref, f32[8,4,128,128]{3,2,1,0:T(8,128)} %p_any.1, f32[8,4,128,128]{3,2,1,0:T(8,128)} %p_any.1, f32[8,4,128,128]{3,2,1,0:T(8,128)} %p_any.1, f32[4,8,4,128,128]{4,3,2,1,0:T(8,128)} %m.1, f32[4,128,128]{2,1,0:T(8,128)} %sd.1, ...), custom_call_target="tpu_custom_call" | custom-call | flops 104857600 | bytes 25165824 | tf_op jit(solution)/shard_map/pallas_call | solution.py:290
  33.7 2.9 %fusion.29 = f32[8,4,128,128]{3,2,1,0:T(8,128)S(1)} fusion(f32[8,4,128,128]{3,2,1,0:T(8,128)} %get-tuple-element.6, f32[128]{0:T(128)S(1)} %get-tuple-element.11, f32[128]{0:T(128)S(1)} %iota_multiply_fusion.1, f32[128]{0:T(128)S(1)} %get-tuple-element.10), kind=kOutput, calls=%fused_computation.23 | convolution fusion | flops 402702336 | bytes 4195840 | tf_op jit(solution)/shard_map/txyi,ki->txyk/dot_general | solution.py:320
  36.5 1.3 %fusion.27 = f32[128,8,4,128]{3,0,2,1:T(8,128)S(1)} fusion(f32[8,4,128,128]{3,2,1,0:T(8,128)S(1)} %fusion.29, f32[128]{0:T(128)S(1)} %get-tuple-element.11, f32[128]{0:T(128)S(1)} %iota_multiply_fusion.1, f32[128]{0:T(128)S(1)} %get-tuple-element.10), kind=kOutput, calls=%fused_computation.21 | convolution fusion | flops 402702336 | bytes 4195840 | tf_op jit(solution)/shard_map/txiz,ki->ktxz/dot_general | solution.py:321
  37.8 2.7 %copy.19 = f32[128,8,4,128]{3,2,1,0:T(4,128)} copy(f32[128,8,4,128]{3,0,2,1:T(8,128)S(1)} %fusion.27) | data formatting | bytes 4194304 | tf_op jit(solution)/shard_map/txiz,ki->ktxz/dot_general | solution.py:321
  40.5 10.7 %all-to-all-start = ((f32[128,8,4,128]{3,2,1,0:T(4,128)}), f32[128,8,4,128]{3,2,1,0:T(4,128)S(1)}, u32[]{:S(2)}, u32[]{:S(2)}) async-start(f32[128,8,4,128]{3,2,1,0:T(4,128)} %copy.19), calls=%async_computation | async-start | bytes 4194304 | tf_op jit(solution)/shard_map/all_to_all | solution.py:323
  51.5 0.1 add_add_fusion
  51.6 8.5 %compare_select_fusion = f32[4,8,4,128,128]{4,3,2,1,0:T(8,128)} fusion(f32[4,8,4,128,128]{4,3,2,1,0:T(8,128)} %get-tuple-element.7), kind=kLoop, calls=%fused_computation | loop fusion | flops 4194304 | bytes 16777216 | tf_op jit(solution)/shard_map/jit(_where)/select_n | solution.py:324
  60.1 21.1 %all-to-all-done = f32[128,8,4,128]{3,2,1,0:T(4,128)S(1)} async-done(((f32[128,8,4,128]{3,2,1,0:T(4,128)}), f32[128,8,4,128]{3,2,1,0:T(4,128)S(1)}, u32[]{:S(2)}, u32[]{:S(2)}) %all-to-all-start) | async-done | bytes 2097184 | tf_op jit(solution)/shard_map/all_to_all | solution.py:323
  81.3 1.2 fusion.14
  82.5 2.5 %fusion = f32[64,64,128]{2,1,0:T(8,128)S(1)} fusion(f32[64,16,4,128]{3,0,2,1:T(8,128)S(1)} %fusion.14, f32[128]{0:T(128)S(1)} %multiply_multiply_fusion, f32[64,64]{1,0:T(8,128)S(1)} %add_add_fusion, f32[16,4]{0,1:T(4,128)S(1)} %fusion.88, f32[64]{0:T(128)S(1)} %get-tuple-element.13, f32[64]{0:T(128)S(1)} %get-tuple-element.12), kind=kOutput, calls=%fused_computation.2 | convolution fusion | flops 203436032 | bytes 4211968 | tf_op jit(solution)/shard_map/jbx,kbxyz->kjyz/dot_general | solution.py:330
  85.0 2.3 %fusion.17 = f32[8,8,64,128,1]{3,1,2,0,4:T(8,128)S(1)} fusion(f32[64,64,128]{2,1,0:T(8,128)S(1)} %fusion, f32[64]{0:T(128)S(1)} %iota_add_fusion.1, f32[8,8]{1,0:T(8,128)S(1)} %get-tuple-element.15, f32[8,8]{1,0:T(8,128)S(1)} %get-tuple-element.14), kind=kOutput, calls=%fused_computation.17 | convolution fusion | flops 201338880 | bytes 4195072 | tf_op jit(solution)/shard_map/atk,kjyz->atjyz/dot_general | solution.py:341
  87.3 1.4 %fusion.20 = f32[8,16,1,8,4,128]{5,1,4,3,0,2:T(8,128)S(1)} fusion(f32[8,8,64,128,1]{3,1,2,0,4:T(8,128)S(1)} %fusion.17, f32[64]{0:T(128)S(1)} %iota_add_fusion.1, f32[16,4]{0,1:T(4,128)S(1)} %get-tuple-element.17, f32[16,4]{0,1:T(4,128)S(1)} %get-tuple-element.16), kind=kOutput, calls=%fused_computation.18 | convolution fusion | flops 201338880 | bytes 4195072 | tf_op jit(solution)/shard_map/bxj,atjyz->abytxz/dot_general | solution.py:342
  88.7 1.2 copy.24
  89.9 0.5 copy.25
  90.4 34.6 %all_to_all.10 = f32[128,8,4,128]{3,2,1,0:T(4,128)S(1)} all-to-all(f32[128,8,4,128]{3,2,1,0:T(4,128)S(1)} %copy.25), channel_id=1, replica_groups=mesh['tm'=8,'space'=16] {'tm','space'}, dimensions={0} | all-to-all | bytes 4194304 | tf_op jit(solution)/shard_map/all_to_all | solution.py:344
  125.0 2.7 %fusion.7 = f32[8,4,128,128]{3,2,1,0:T(8,128)S(1)} fusion(f32[128,8,4,128]{3,2,1,0:T(4,128)S(1)} %all_to_all.10, f32[128]{0:T(128)S(1)} %get-tuple-element.11, f32[128]{0:T(128)S(1)} %iota_multiply_fusion.1, f32[128]{0:T(128)S(1)} %get-tuple-element.10), kind=kOutput, calls=%fused_computation.9 | convolution fusion | flops 402702336 | bytes 4195840 | tf_op jit(solution)/shard_map/ik,ktxz->txiz/dot_general | solution.py:345
  127.8 3.3 %fusion.1 = f32[8,4,128,128]{3,2,1,0:T(8,128)} fusion(f32[8,4,128,128]{3,2,1,0:T(8,128)S(1)} %fusion.7, f32[128]{0:T(128)S(1)} %get-tuple-element.11, f32[128]{0:T(128)S(1)} %iota_multiply_fusion.1, f32[128]{0:T(128)S(1)} %get-tuple-element.10), kind=kOutput, calls=%fused_computation.3 | convolution fusion | flops 402702336 | bytes 4195840 | tf_op jit(solution)/shard_map/ik,txyk->txyi/dot_general | solution.py:346
  (10 shorter events, 0.2 us)
Async XLA Ops:
  40.5 40.8 %all-to-all-start = ((f32[128,8,4,128]{3,2,1,0:T(4,128)}), f32[128,8,4,128]{3,2,1,0:T(4,128)S(1)}, u32[]{:S(2)}, u32[]{:S(2)}) async-start(f32[128,8,4,128]{3,2,1,0:T(4,128)} %copy.19), calls=%async_computation | async-start | bytes 4194304 | tf_op jit(solution)/shard_map/all_to_all | solution.py:323

commit v13 on v10

--- a/solution.py
+++ b/solution.py
@@ -180,6 +180,20 @@
                 nm = mults[c] + RATE * (grads[c] - proj[c])
                 nm_out[c, 0, x] = nm
                 flux.append(nm - RATE * proj[c])
+            if x == rows_x - 1:
+                send_x[t] = flux[1]
+
+                @pl.when(has_later_x)
+                def _():
+                    behind_x_copy(t).start()
+
+            @pl.when(t == steps_t - 1)
+            def _():
+                send_t[x] = flux[0]
+
+                @pl.when(has_later_t)
+                def _():
+                    behind_t_copy(x).start()
             flow_y = jnp.where(first_row, 0.0, pltpu.roll(flux[2], 1, 0)) - jnp.where(last_row, 0.0, flux[2])
             flow_z = jnp.where(first_col, 0.0, pltpu.roll(flux[3], 1, 1)) - jnp.where(last_col, 0.0, flux[3])
             rest = PROX * p - (flow_y + flow_z)
@@ -188,23 +202,10 @@
             ft_prev = lax.cond(has_prev, lambda: ft_store[jnp.maximum(t - 1, 0), x], lambda: jnp.zeros_like(p))
             div_t = ft_prev - jnp.where(last_t, 0.0, flux[0])
             ft_store[t, x] = flux[0]
-
-            @pl.when(t == steps_t - 1)
-            def _():
-                send_t[x] = flux[0]
-
-                @pl.when(has_later_t)
-                def _():
-                    behind_t_copy(x).start()
             if x < rows_x - 1:
                 fx_cur = flux[1]
             else:
                 fx_cur = jnp.where(has_later_x, flux[1], 0.0)
-                send_x[t] = flux[1]
-
-                @pl.when(has_later_x)
-                def _():
-                    behind_x_copy(t).start()
             value = rest - div_t + fx_cur
             if x - 1 in fx_done:
                 value = value - fx_done[x - 1]

time: 131 us -> 131 us (level)
  no operation moved by 1% of the time
where the time goes in v13:
time: 131 us; the launch traced here: 130 us
  blocking collectives  34.6 us (26%)
  Pallas kernels  31.4 us (24%)
  waiting for transfers between devices  21.1 us (16%)
  matrix products  17.6 us (13%)
  starting transfers between devices  11 us (8%)
  other arithmetic  9.36 us (7%)
  local copies, waits for them, and re-layouts  4.41 us (3%)
    all_to_all x1, blocking collectives, body(): lax.all_to_all(solved, both, split_axis=0, concat_axis=0, tiled=True)  34.6 us
    pallas_call x1, Pallas kernels, cells(): pl.pallas_call(functools.partial(cell_kernel, n_tm, n_sp), grid_spec=grid...  31.4 us
    all_to_all x1, waiting for transfers between devices, body(): lax.all_to_all(payload, both, split_axis=0, concat_axis=0, tiled=True)  21.1 us
    all_to_all x1, starting transfers between devices, body(): lax.all_to_all(payload, both, split_axis=0, concat_axis=0, tiled=True)  11 us
    select_n x1, other arithmetic, body(): jnp.where(next_multiplier == next_multiplier, next_multiplier, 0.0)  8.53 us
    dot_general x1, matrix products, body(): next_potential = jnp.einsum('ik,txyk->txyi', cos_z, local, precision=high)  3.32 us
    dot_general x1, matrix products, body(): payload = jnp.einsum('txyi,ki->txyk', partial, cos_z, precision=high)  2.87 us
    dot_general x1, matrix products, body(): local = jnp.einsum('ik,ktxz->txiz', cos_y, local, precision=high)  2.73 us
  transfers between devices with their start and end apart: 1, of which 1 were waited for; matrix products, arithmetic and copies ran while one was open for 7% of the time, Pallas kernels for 0%

profile of v13, /device:TPU:1, one launch (start us, length us, event | category | flops | bytes accessed | tf_op | source)
XLA Modules:
  0.0 130.3 jit_solution(14421018191634022127)
XLA Ops:
  0.7 0.6 pad_add_fusion.idx_ref
  1.2 31.4 %shard_map.59 = (f32[4,8,4,128,128]{4,3,2,1,0:T(8,128)}, f32[8,4,128,128]{3,2,1,0:T(8,128)}) custom-call(s32[2]{0:T(128)} %pad_add_fusion.idx_ref, f32[8,4,128,128]{3,2,1,0:T(8,128)} %p_any.1, f32[8,4,128,128]{3,2,1,0:T(8,128)} %p_any.1, f32[8,4,128,128]{3,2,1,0:T(8,128)} %p_any.1, f32[4,8,4,128,128]{4,3,2,1,0:T(8,128)} %m.1, f32[4,128,128]{2,1,0:T(8,128)} %sd.1, ...), custom_call_target="tpu_custom_call" | custom-call | flops 104857600 | bytes 25165824 | tf_op jit(solution)/shard_map/pallas_call | solution.py:291
  32.6 2.9 %fusion.29 = f32[8,4,128,128]{3,2,1,0:T(8,128)S(1)} fusion(f32[8,4,128,128]{3,2,1,0:T(8,128)} %get-tuple-element.6, f32[128]{0:T(128)S(1)} %get-tuple-element.11, f32[128]{0:T(128)S(1)} %iota_multiply_fusion.1, f32[128]{0:T(128)S(1)} %get-tuple-element.10), kind=kOutput, calls=%fused_computation.23 | convolution fusion | flops 402702336 | bytes 4195840 | tf_op jit(solution)/shard_map/txyi,ki->txyk/dot_general | solution.py:321
  35.5 1.3 fusion.27
  36.8 2.7 %copy.19 = f32[128,8,4,128]{3,2,1,0:T(4,128)} copy(f32[128,8,4,128]{3,0,2,1:T(8,128)S(1)} %fusion.27) | data formatting | bytes 4194304 | tf_op jit(solution)/shard_map/txiz,ki->ktxz/dot_general | solution.py:322
  39.5 11.0 %all-to-all-start = ((f32[128,8,4,128]{3,2,1,0:T(4,128)}), f32[128,8,4,128]{3,2,1,0:T(4,128)S(1)}, u32[]{:S(2)}, u32[]{:S(2)}) async-start(f32[128,8,4,128]{3,2,1,0:T(4,128)} %copy.19), calls=%async_computation | async-start | bytes 4194304 | tf_op jit(solution)/shard_map/all_to_all | solution.py:324
  50.8 0.1 add_add_fusion
  50.9 8.5 %compare_select_fusion = f32[4,8,4,128,128]{4,3,2,1,0:T(8,128)} fusion(f32[4,8,4,128,128]{4,3,2,1,0:T(8,128)} %get-tuple-element.7), kind=kLoop, calls=%fused_computation | loop fusion | flops 4194304 | bytes 16777216 | tf_op jit(solution)/shard_map/jit(_where)/select_n | solution.py:325
  59.4 21.1 %all-to-all-done = f32[128,8,4,128]{3,2,1,0:T(4,128)S(1)} async-done(((f32[128,8,4,128]{3,2,1,0:T(4,128)}), f32[128,8,4,128]{3,2,1,0:T(4,128)S(1)}, u32[]{:S(2)}, u32[]{:S(2)}) %all-to-all-start) | async-done | bytes 2097184 | tf_op jit(solution)/shard_map/all_to_all | solution.py:324
  80.5 1.2 fusion.14
  81.8 2.5 %fusion = f32[64,64,128]{2,1,0:T(8,128)S(1)} fusion(f32[64,16,4,128]{3,0,2,1:T(8,128)S(1)} %fusion.14, f32[128]{0:T(128)S(1)} %multiply_multiply_fusion, f32[64,64]{1,0:T(8,128)S(1)} %add_add_fusion, f32[16,4]{0,1:T(4,128)S(1)} %fusion.88, f32[64]{0:T(128)S(1)} %get-tuple-element.13, f32[64]{0:T(128)S(1)} %get-tuple-element.12), kind=kOutput, calls=%fused_computation.2 | convolution fusion | flops 203436032 | bytes 4211968 | tf_op jit(solution)/shard_map/jbx,kbxyz->kjyz/dot_general | solution.py:331
  84.3 2.3 %fusion.17 = f32[8,8,64,128,1]{3,1,2,0,4:T(8,128)S(1)} fusion(f32[64,64,128]{2,1,0:T(8,128)S(1)} %fusion, f32[64]{0:T(128)S(1)} %iota_add_fusion.1, f32[8,8]{1,0:T(8,128)S(1)} %get-tuple-element.15, f32[8,8]{1,0:T(8,128)S(1)} %get-tuple-element.14), kind=kOutput, calls=%fused_computation.17 | convolution fusion | flops 201338880 | bytes 4195072 | tf_op jit(solution)/shard_map/atk,kjyz->atjyz/dot_general | solution.py:342
  86.5 1.4 %fusion.20 = f32[8,16,1,8,4,128]{5,1,4,3,0,2:T(8,128)S(1)} fusion(f32[8,8,64,128,1]{3,1,2,0,4:T(8,128)S(1)} %fusion.17, f32[64]{0:T(128)S(1)} %iota_add_fusion.1, f32[16,4]{0,1:T(4,128)S(1)} %get-tuple-element.17, f32[16,4]{0,1:T(4,128)S(1)} %get-tuple-element.16), kind=kOutput, calls=%fused_computation.18 | convolution fusion | flops 201338880 | bytes 4195072 | tf_op jit(solution)/shard_map/bxj,atjyz->abytxz/dot_general | solution.py:343
  87.9 1.2 copy.24
  89.1 0.5 copy.25
  89.7 34.6 %all_to_all.10 = f32[128,8,4,128]{3,2,1,0:T(4,128)S(1)} all-to-all(f32[128,8,4,128]{3,2,1,0:T(4,128)S(1)} %copy.25), channel_id=1, replica_groups=mesh['tm'=8,'space'=16] {'tm','space'}, dimensions={0} | all-to-all | bytes 4194304 | tf_op jit(solution)/shard_map/all_to_all | solution.py:345
  124.3 2.7 %fusion.7 = f32[8,4,128,128]{3,2,1,0:T(8,128)S(1)} fusion(f32[128,8,4,128]{3,2,1,0:T(4,128)S(1)} %all_to_all.10, f32[128]{0:T(128)S(1)} %get-tuple-element.11, f32[128]{0:T(128)S(1)} %iota_multiply_fusion.1, f32[128]{0:T(128)S(1)} %get-tuple-element.10), kind=kOutput, calls=%fused_computation.9 | convolution fusion | flops 402702336 | bytes 4195840 | tf_op jit(solution)/shard_map/ik,ktxz->txiz/dot_general | solution.py:346
  127.0 3.3 %fusion.1 = f32[8,4,128,128]{3,2,1,0:T(8,128)} fusion(f32[8,4,128,128]{3,2,1,0:T(8,128)S(1)} %fusion.7, f32[128]{0:T(128)S(1)} %get-tuple-element.11, f32[128]{0:T(128)S(1)} %iota_multiply_fusion.1, f32[128]{0:T(128)S(1)} %get-tuple-element.10), kind=kOutput, calls=%fused_computation.3 | convolution fusion | flops 402702336 | bytes 4195840 | tf_op jit(solution)/shard_map/ik,txyk->txyi/dot_general | solution.py:347
  (10 shorter events, 0.2 us)
Async XLA Ops:
  39.5 41.0 %all-to-all-start = ((f32[128,8,4,128]{3,2,1,0:T(4,128)}), f32[128,8,4,128]{3,2,1,0:T(4,128)S(1)}, u32[]{:S(2)}, u32[]{:S(2)}) async-start(f32[128,8,4,128]{3,2,1,0:T(4,128)} %copy.19), calls=%async_computation | async-start | bytes 4194304 | tf_op jit(solution)/shard_map/all_to_all | solution.py:324

commit v14 on v13

--- a/solution.py
+++ b/solution.py
@@ -238,6 +238,7 @@
         def _():
             for r in range(steps_t):
                 ahead_x_copy(r).wait_send()
+            for r in [steps_t - 1] + list(range(steps_t - 2)) + [steps_t - 2]:
                 behind_x_copy(r).wait_recv()
                 pay_out[r, 0] = pay_out[r, 0] - behind_x[r]
 

time: 131 us -> 131 us (level)
  no operation moved by 1% of the time
where the time goes in v14:
time: 131 us; the launch traced here: 130 us
  blocking collectives  34.6 us (26%)
  Pallas kernels  31.4 us (24%)
  waiting for transfers between devices  21.1 us (16%)
  matrix products  17.6 us (13%)
  starting transfers between devices  11 us (8%)
  other arithmetic  9.36 us (7%)
  local copies, waits for them, and re-layouts  4.41 us (3%)
    all_to_all x1, blocking collectives, body(): lax.all_to_all(solved, both, split_axis=0, concat_axis=0, tiled=True)  34.6 us
    pallas_call x1, Pallas kernels, cells(): pl.pallas_call(functools.partial(cell_kernel, n_tm, n_sp), grid_spec=grid...  31.4 us
    all_to_all x1, waiting for transfers between devices, body(): lax.all_to_all(payload, both, split_axis=0, concat_axis=0, tiled=True)  21.1 us
    all_to_all x1, starting transfers between devices, body(): lax.all_to_all(payload, both, split_axis=0, concat_axis=0, tiled=True)  11 us
    select_n x1, other arithmetic, body(): jnp.where(next_multiplier == next_multiplier, next_multiplier, 0.0)  8.53 us
    dot_general x1, matrix products, body(): next_potential = jnp.einsum('ik,txyk->txyi', cos_z, local, precision=high)  3.32 us
    dot_general x1, matrix products, body(): payload = jnp.einsum('txyi,ki->txyk', partial, cos_z, precision=high)  2.87 us
    dot_general x1, matrix products, body(): local = jnp.einsum('ik,ktxz->txiz', cos_y, local, precision=high)  2.73 us
  transfers between devices with their start and end apart: 1, of which 1 were waited for; matrix products, arithmetic and copies ran while one was open for 7% of the time, Pallas kernels for 0%

profile of v14, /device:TPU:1, one launch (start us, length us, event | category | flops | bytes accessed | tf_op | source)
XLA Modules:
  0.0 130.3 jit_solution(9216829408398741942)
XLA Ops:
  0.7 0.6 pad_add_fusion.idx_ref
  1.2 31.4 %shard_map.59 = (f32[4,8,4,128,128]{4,3,2,1,0:T(8,128)}, f32[8,4,128,128]{3,2,1,0:T(8,128)}) custom-call(s32[2]{0:T(128)} %pad_add_fusion.idx_ref, f32[8,4,128,128]{3,2,1,0:T(8,128)} %p_any.1, f32[8,4,128,128]{3,2,1,0:T(8,128)} %p_any.1, f32[8,4,128,128]{3,2,1,0:T(8,128)} %p_any.1, f32[4,8,4,128,128]{4,3,2,1,0:T(8,128)} %m.1, f32[4,128,128]{2,1,0:T(8,128)} %sd.1, ...), custom_call_target="tpu_custom_call" | custom-call | flops 104857600 | bytes 25165824 | tf_op jit(solution)/shard_map/pallas_call | solution.py:292
  32.6 2.9 %fusion.29 = f32[8,4,128,128]{3,2,1,0:T(8,128)S(1)} fusion(f32[8,4,128,128]{3,2,1,0:T(8,128)} %get-tuple-element.6, f32[128]{0:T(128)S(1)} %get-tuple-element.11, f32[128]{0:T(128)S(1)} %iota_multiply_fusion.1, f32[128]{0:T(128)S(1)} %get-tuple-element.10), kind=kOutput, calls=%fused_computation.23 | convolution fusion | flops 402702336 | bytes 4195840 | tf_op jit(solution)/shard_map/txyi,ki->txyk/dot_general | solution.py:322
  35.5 1.3 fusion.27
  36.8 2.7 %copy.19 = f32[128,8,4,128]{3,2,1,0:T(4,128)} copy(f32[128,8,4,128]{3,0,2,1:T(8,128)S(1)} %fusion.27) | data formatting | bytes 4194304 | tf_op jit(solution)/shard_map/txiz,ki->ktxz/dot_general | solution.py:323
  39.5 11.0 %all-to-all-start = ((f32[128,8,4,128]{3,2,1,0:T(4,128)}), f32[128,8,4,128]{3,2,1,0:T(4,128)S(1)}, u32[]{:S(2)}, u32[]{:S(2)}) async-start(f32[128,8,4,128]{3,2,1,0:T(4,128)} %copy.19), calls=%async_computation | async-start | bytes 4194304 | tf_op jit(solution)/shard_map/all_to_all | solution.py:325
  50.8 0.1 add_add_fusion
  50.8 8.5 %compare_select_fusion = f32[4,8,4,128,128]{4,3,2,1,0:T(8,128)} fusion(f32[4,8,4,128,128]{4,3,2,1,0:T(8,128)} %get-tuple-element.7), kind=kLoop, calls=%fused_computation | loop fusion | flops 4194304 | bytes 16777216 | tf_op jit(solution)/shard_map/jit(_where)/select_n | solution.py:326
  59.4 21.1 %all-to-all-done = f32[128,8,4,128]{3,2,1,0:T(4,128)S(1)} async-done(((f32[128,8,4,128]{3,2,1,0:T(4,128)}), f32[128,8,4,128]{3,2,1,0:T(4,128)S(1)}, u32[]{:S(2)}, u32[]{:S(2)}) %all-to-all-start) | async-done | bytes 2097184 | tf_op jit(solution)/shard_map/all_to_all | solution.py:325
  80.5 1.2 fusion.14
  81.7 2.5 %fusion = f32[64,64,128]{2,1,0:T(8,128)S(1)} fusion(f32[64,16,4,128]{3,0,2,1:T(8,128)S(1)} %fusion.14, f32[128]{0:T(128)S(1)} %multiply_multiply_fusion, f32[64,64]{1,0:T(8,128)S(1)} %add_add_fusion, f32[16,4]{0,1:T(4,128)S(1)} %fusion.88, f32[64]{0:T(128)S(1)} %get-tuple-element.13, f32[64]{0:T(128)S(1)} %get-tuple-element.12), kind=kOutput, calls=%fused_computation.2 | convolution fusion | flops 203436032 | bytes 4211968 | tf_op jit(solution)/shard_map/jbx,kbxyz->kjyz/dot_general | solution.py:332
  84.2 2.3 %fusion.17 = f32[8,8,64,128,1]{3,1,2,0,4:T(8,128)S(1)} fusion(f32[64,64,128]{2,1,0:T(8,128)S(1)} %fusion, f32[64]{0:T(128)S(1)} %iota_add_fusion.1, f32[8,8]{1,0:T(8,128)S(1)} %get-tuple-element.15, f32[8,8]{1,0:T(8,128)S(1)} %get-tuple-element.14), kind=kOutput, calls=%fused_computation.17 | convolution fusion | flops 201338880 | bytes 4195072 | tf_op jit(solution)/shard_map/atk,kjyz->atjyz/dot_general | solution.py:343
  86.5 1.4 %fusion.20 = f32[8,16,1,8,4,128]{5,1,4,3,0,2:T(8,128)S(1)} fusion(f32[8,8,64,128,1]{3,1,2,0,4:T(8,128)S(1)} %fusion.17, f32[64]{0:T(128)S(1)} %iota_add_fusion.1, f32[16,4]{0,1:T(4,128)S(1)} %get-tuple-element.17, f32[16,4]{0,1:T(4,128)S(1)} %get-tuple-element.16), kind=kOutput, calls=%fused_computation.18 | convolution fusion | flops 201338880 | bytes 4195072 | tf_op jit(solution)/shard_map/bxj,atjyz->abytxz/dot_general | solution.py:344
  87.9 1.2 copy.24
  89.1 0.5 copy.25
  89.7 34.6 %all_to_all.10 = f32[128,8,4,128]{3,2,1,0:T(4,128)S(1)} all-to-all(f32[128,8,4,128]{3,2,1,0:T(4,128)S(1)} %copy.25), channel_id=1, replica_groups=mesh['tm'=8,'space'=16] {'tm','space'}, dimensions={0} | all-to-all | bytes 4194304 | tf_op jit(solution)/shard_map/all_to_all | solution.py:346
  124.3 2.7 %fusion.7 = f32[8,4,128,128]{3,2,1,0:T(8,128)S(1)} fusion(f32[128,8,4,128]{3,2,1,0:T(4,128)S(1)} %all_to_all.10, f32[128]{0:T(128)S(1)} %get-tuple-element.11, f32[128]{0:T(128)S(1)} %iota_multiply_fusion.1, f32[128]{0:T(128)S(1)} %get-tuple-element.10), kind=kOutput, calls=%fused_computation.9 | convolution fusion | flops 402702336 | bytes 4195840 | tf_op jit(solution)/shard_map/ik,ktxz->txiz/dot_general | solution.py:347
  127.0 3.3 %fusion.1 = f32[8,4,128,128]{3,2,1,0:T(8,128)} fusion(f32[8,4,128,128]{3,2,1,0:T(8,128)S(1)} %fusion.7, f32[128]{0:T(128)S(1)} %get-tuple-element.11, f32[128]{0:T(128)S(1)} %iota_multiply_fusion.1, f32[128]{0:T(128)S(1)} %get-tuple-element.10), kind=kOutput, calls=%fused_computation.3 | convolution fusion | flops 402702336 | bytes 4195840 | tf_op jit(solution)/shard_map/ik,txyk->txyi/dot_general | solution.py:348
  (10 shorter events, 0.2 us)
Async XLA Ops:
  39.5 41.0 %all-to-all-start = ((f32[128,8,4,128]{3,2,1,0:T(4,128)}), f32[128,8,4,128]{3,2,1,0:T(4,128)S(1)}, u32[]{:S(2)}, u32[]{:S(2)}) async-start(f32[128,8,4,128]{3,2,1,0:T(4,128)} %copy.19), calls=%async_computation | async-start | bytes 4194304 | tf_op jit(solution)/shard_map/all_to_all | solution.py:325

commit v15 on v14

--- a/solution.py
+++ b/solution.py
@@ -229,10 +229,10 @@
 
         @pl.when(has_earlier_t)
         def _():
-            ahead_t_copy().wait_send()
             for x in range(rows_x):
                 behind_t_copy(x).wait_recv()
                 pay_out[0, x] = pay_out[0, x] - behind_t[x]
+            ahead_t_copy().wait_send()
 
         @pl.when(has_earlier_x)
         def _():

time: 131 us -> 131 us (level)
  no operation moved by 1% of the time
where the time goes in v15:
time: 131 us; the launch traced here: 130 us
  blocking collectives  34.6 us (26%)
  Pallas kernels  31.4 us (24%)
  waiting for transfers between devices  21.1 us (16%)
  matrix products  17.6 us (13%)
  starting transfers between devices  11 us (8%)
  other arithmetic  9.36 us (7%)
  local copies, waits for them, and re-layouts  4.41 us (3%)
    all_to_all x1, blocking collectives, body(): lax.all_to_all(solved, both, split_axis=0, concat_axis=0, tiled=True)  34.6 us
    pallas_call x1, Pallas kernels, cells(): pl.pallas_call(functools.partial(cell_kernel, n_tm, n_sp), grid_spec=grid...  31.4 us
    all_to_all x1, waiting for transfers between devices, body(): lax.all_to_all(payload, both, split_axis=0, concat_axis=0, tiled=True)  21.1 us
    all_to_all x1, starting transfers between devices, body(): lax.all_to_all(payload, both, split_axis=0, concat_axis=0, tiled=True)  11 us
    select_n x1, other arithmetic, body(): jnp.where(next_multiplier == next_multiplier, next_multiplier, 0.0)  8.53 us
    dot_general x1, matrix products, body(): next_potential = jnp.einsum('ik,txyk->txyi', cos_z, local, precision=high)  3.32 us
    dot_general x1, matrix products, body(): payload = jnp.einsum('txyi,ki->txyk', partial, cos_z, precision=high)  2.87 us
    dot_general x1, matrix products, body(): local = jnp.einsum('ik,ktxz->txiz', cos_y, local, precision=high)  2.73 us
  transfers between devices with their start and end apart: 1, of which 1 were waited for; matrix products, arithmetic and copies ran while one was open for 7% of the time, Pallas kernels for 0%

profile of v15, /device:TPU:1, one launch (start us, length us, event | category | flops | bytes accessed | tf_op | source)
XLA Modules:
  0.0 130.3 jit_solution(13702668417027378548)
XLA Ops:
  0.7 0.6 pad_add_fusion.idx_ref
  1.2 31.4 %shard_map.59 = (f32[4,8,4,128,128]{4,3,2,1,0:T(8,128)}, f32[8,4,128,128]{3,2,1,0:T(8,128)}) custom-call(s32[2]{0:T(128)} %pad_add_fusion.idx_ref, f32[8,4,128,128]{3,2,1,0:T(8,128)} %p_any.1, f32[8,4,128,128]{3,2,1,0:T(8,128)} %p_any.1, f32[8,4,128,128]{3,2,1,0:T(8,128)} %p_any.1, f32[4,8,4,128,128]{4,3,2,1,0:T(8,128)} %m.1, f32[4,128,128]{2,1,0:T(8,128)} %sd.1, ...), custom_call_target="tpu_custom_call" | custom-call | flops 104857600 | bytes 25165824 | tf_op jit(solution)/shard_map/pallas_call | solution.py:292
  32.6 2.9 %fusion.29 = f32[8,4,128,128]{3,2,1,0:T(8,128)S(1)} fusion(f32[8,4,128,128]{3,2,1,0:T(8,128)} %get-tuple-element.6, f32[128]{0:T(128)S(1)} %get-tuple-element.11, f32[128]{0:T(128)S(1)} %iota_multiply_fusion.1, f32[128]{0:T(128)S(1)} %get-tuple-element.10), kind=kOutput, calls=%fused_computation.23 | convolution fusion | flops 402702336 | bytes 4195840 | tf_op jit(solution)/shard_map/txyi,ki->txyk/dot_general | solution.py:322
  35.5 1.3 fusion.27
  36.8 2.7 %copy.19 = f32[128,8,4,128]{3,2,1,0:T(4,128)} copy(f32[128,8,4,128]{3,0,2,1:T(8,128)S(1)} %fusion.27) | data formatting | bytes 4194304 | tf_op jit(solution)/shard_map/txiz,ki->ktxz/dot_general | solution.py:323
  39.5 11.0 %all-to-all-start = ((f32[128,8,4,128]{3,2,1,0:T(4,128)}), f32[128,8,4,128]{3,2,1,0:T(4,128)S(1)}, u32[]{:S(2)}, u32[]{:S(2)}) async-start(f32[128,8,4,128]{3,2,1,0:T(4,128)} %copy.19), calls=%async_computation | async-start | bytes 4194304 | tf_op jit(solution)/shard_map/all_to_all | solution.py:325
  50.8 0.1 add_add_fusion
  50.8 8.5 %compare_select_fusion = f32[4,8,4,128,128]{4,3,2,1,0:T(8,128)} fusion(f32[4,8,4,128,128]{4,3,2,1,0:T(8,128)} %get-tuple-element.7), kind=kLoop, calls=%fused_computation | loop fusion | flops 4194304 | bytes 16777216 | tf_op jit(solution)/shard_map/jit(_where)/select_n | solution.py:326
  59.4 21.1 %all-to-all-done = f32[128,8,4,128]{3,2,1,0:T(4,128)S(1)} async-done(((f32[128,8,4,128]{3,2,1,0:T(4,128)}), f32[128,8,4,128]{3,2,1,0:T(4,128)S(1)}, u32[]{:S(2)}, u32[]{:S(2)}) %all-to-all-start) | async-done | bytes 2097184 | tf_op jit(solution)/shard_map/all_to_all | solution.py:325
  80.5 1.2 fusion.14
  81.7 2.5 %fusion = f32[64,64,128]{2,1,0:T(8,128)S(1)} fusion(f32[64,16,4,128]{3,0,2,1:T(8,128)S(1)} %fusion.14, f32[128]{0:T(128)S(1)} %multiply_multiply_fusion, f32[64,64]{1,0:T(8,128)S(1)} %add_add_fusion, f32[16,4]{0,1:T(4,128)S(1)} %fusion.88, f32[64]{0:T(128)S(1)} %get-tuple-element.13, f32[64]{0:T(128)S(1)} %get-tuple-element.12), kind=kOutput, calls=%fused_computation.2 | convolution fusion | flops 203436032 | bytes 4211968 | tf_op jit(solution)/shard_map/jbx,kbxyz->kjyz/dot_general | solution.py:332
  84.2 2.3 %fusion.17 = f32[8,8,64,128,1]{3,1,2,0,4:T(8,128)S(1)} fusion(f32[64,64,128]{2,1,0:T(8,128)S(1)} %fusion, f32[64]{0:T(128)S(1)} %iota_add_fusion.1, f32[8,8]{1,0:T(8,128)S(1)} %get-tuple-element.15, f32[8,8]{1,0:T(8,128)S(1)} %get-tuple-element.14), kind=kOutput, calls=%fused_computation.17 | convolution fusion | flops 201338880 | bytes 4195072 | tf_op jit(solution)/shard_map/atk,kjyz->atjyz/dot_general | solution.py:343
  86.5 1.4 %fusion.20 = f32[8,16,1,8,4,128]{5,1,4,3,0,2:T(8,128)S(1)} fusion(f32[8,8,64,128,1]{3,1,2,0,4:T(8,128)S(1)} %fusion.17, f32[64]{0:T(128)S(1)} %iota_add_fusion.1, f32[16,4]{0,1:T(4,128)S(1)} %get-tuple-element.17, f32[16,4]{0,1:T(4,128)S(1)} %get-tuple-element.16), kind=kOutput, calls=%fused_computation.18 | convolution fusion | flops 201338880 | bytes 4195072 | tf_op jit(solution)/shard_map/bxj,atjyz->abytxz/dot_general | solution.py:344
  87.9 1.2 copy.24
  89.1 0.5 copy.25
  89.7 34.6 %all_to_all.10 = f32[128,8,4,128]{3,2,1,0:T(4,128)S(1)} all-to-all(f32[128,8,4,128]{3,2,1,0:T(4,128)S(1)} %copy.25), channel_id=1, replica_groups=mesh['tm'=8,'space'=16] {'tm','space'}, dimensions={0} | all-to-all | bytes 4194304 | tf_op jit(solution)/shard_map/all_to_all | solution.py:346
  124.3 2.7 %fusion.7 = f32[8,4,128,128]{3,2,1,0:T(8,128)S(1)} fusion(f32[128,8,4,128]{3,2,1,0:T(4,128)S(1)} %all_to_all.10, f32[128]{0:T(128)S(1)} %get-tuple-element.11, f32[128]{0:T(128)S(1)} %iota_multiply_fusion.1, f32[128]{0:T(128)S(1)} %get-tuple-element.10), kind=kOutput, calls=%fused_computation.9 | convolution fusion | flops 402702336 | bytes 4195840 | tf_op jit(solution)/shard_map/ik,ktxz->txiz/dot_general | solution.py:347
  127.0 3.3 %fusion.1 = f32[8,4,128,128]{3,2,1,0:T(8,128)} fusion(f32[8,4,128,128]{3,2,1,0:T(8,128)S(1)} %fusion.7, f32[128]{0:T(128)S(1)} %get-tuple-element.11, f32[128]{0:T(128)S(1)} %iota_multiply_fusion.1, f32[128]{0:T(128)S(1)} %get-tuple-element.10), kind=kOutput, calls=%fused_computation.3 | convolution fusion | flops 402702336 | bytes 4195840 | tf_op jit(solution)/shard_map/ik,txyk->txyi/dot_general | solution.py:348
  (10 shorter events, 0.2 us)
Async XLA Ops:
  39.5 41.0 %all-to-all-start = ((f32[128,8,4,128]{3,2,1,0:T(4,128)}), f32[128,8,4,128]{3,2,1,0:T(4,128)S(1)}, u32[]{:S(2)}, u32[]{:S(2)}) async-start(f32[128,8,4,128]{3,2,1,0:T(4,128)} %copy.19), calls=%async_computation | async-start | bytes 4194304 | tf_op jit(solution)/shard_map/all_to_all | solution.py:325
